TPU v7x, 32 devices: a whole 2x2x4 slice. The times are simulated.
32 devices in a mesh: groups: 2 (over x), replica: 4 (over z), tensor: 4 (over y, core).
Axes of the slice: x: 2, y: 2, z: 4, core: 2. Of those that a mesh axis runs over, the one named last changes fastest.
Arguments:
- queries: bfloat16 [4096, 4096], P(('groups', 'replica'), 'tensor'), parts along dimension 0, may hold values from -8 to 8
- new_kv: bfloat16 [4096, 2, 512], P(('groups', 'replica'), None, 'tensor'), parts along dimension 0, may hold values from -6 to 6, as said below
- cache_kv: bfloat16 [16, 4096, 2, 512], P(('groups', 'replica'), None, None, 'tensor'), parts along dimension 0, may hold values from -6 to 6, as said below
- stored: int32 [8, 2], P('groups'), parts along dimension 0, may hold values from 0 to 3, as said below
- haystack_ids: int32 [64, 1], P(('groups', 'replica')), parts along dimension 0, may hold values from 0 to 3; in each aligned block of 8 rows (0 to 7, 8 to 15, ...) at most 2 rows name the same one
- token_counts: int32 [8, 8], P(('groups', 'replica')), parts along dimension 0, may hold values from 1 to 64, 384 in all within a row
- out_weight: bfloat16 [4096, 8192], P('tensor'), may hold values from -0.75 to 0.75
Outputs:
- answer: bfloat16 [4096, 8192], P(('groups', 'replica'), 'tensor'), parts along dimension 0
There are 2 independent parts, one for each index of `groups`. A program takes and returns all parts, laid end to end along the dimension named above; an argument that names none is the same for every part. Nothing has to cross between parts.
Inputs may be any that keep to these rules, and one draw needn't show every extreme that they name: `stored`: every haystack lies in slot 0 of exactly one replica index and in slot 1 of exactly one other. `haystack_ids`: among the 8 questions of one replica index no haystack is named more than 2 times; some haystack is named exactly 2 times. `token_counts`: the counts of one replica index sum to 384 and the largest is 64. `cache_kv`: slots holding the same haystack hold equal values; the cache heads serving one kv head are equal. `new_kv`: the cache heads serving one kv head are equal.
All inputs are finite; a program needn't handle non-finite values.
Results may differ from a plain program's by a relative error of at most 0.0053.
Values may be sent and summed in bfloat16 or wider, within the bound.
No kernel may reach another device: no remote copies, remote signals or barrier semaphores. Data moves between devices by JAX's collectives and lax.ppermute only.
A program may use at most 128 MiB of HBM per device.

v0:
```python
import functools
import math

import jax
import jax.numpy as jnp
from jax import lax
from jax.experimental import pallas as pl
from jax.experimental.pallas import tpu as pltpu
from jax.sharding import PartitionSpec as P


CAP = 2
BF16 = jnp.bfloat16
F32 = jnp.float32
LOG2E = 1.4426950408889634
TOTAL_MAX = 1e30
VMEM = pl.BlockSpec(memory_space=pltpu.VMEM)
SMEM = pl.BlockSpec(memory_space=pltpu.SMEM)


def pack_kernel(stored_hbm, ids_hbm, q_hbm, own_hbm, table_ref, *refs, route, heads, qlength):
    number = len(refs) - 5
    out_refs = refs[:number]
    stored_ref, ids_ref, q_ref, own_ref, sems = refs[number:]
    head_size = own_ref.shape[1]
    questions = ids_ref.shape[1]
    pairs = ((stored_hbm, stored_ref), (ids_hbm, ids_ref), (q_hbm, q_ref), (own_hbm, own_ref))
    copies = [pltpu.make_async_copy(source, target, sems.at[i]) for i, (source, target) in enumerate(pairs)]
    for copy in copies:
        copy.start()
    for copy in copies[:2]:
        copy.wait()
    places = []
    for s, haystack in enumerate(route(stored_ref, table_ref)):
        count = jnp.int32(0)
        found = [jnp.int32(-1)] * CAP
        for i in range(questions):
            hit = ids_ref[0, i] == haystack
            for j in range(CAP):
                found[j] = jnp.where(hit & (count == j), jnp.int32(i), found[j])
            count = count + hit.astype(jnp.int32)
        for j in range(CAP):
            table_ref[s * CAP + j] = found[j]
        places.append([jnp.maximum(place, 0) for place in found])
    for copy in copies[2:]:
        copy.wait()
    for s, out_ref in enumerate(out_refs):
        for j, place in enumerate(places[s]):
            rows = q_ref[pl.ds(pl.multiple_of(place * qlength, qlength), qlength), :]
            for h in range(heads):
                out_ref[j, h * qlength : (h + 1) * qlength, :] = rows[:, h * head_size : (h + 1) * head_size]
            own = own_ref[pl.ds(pl.multiple_of(place * 2 * qlength, 2 * qlength), 2 * qlength), :]
            out_ref[j, heads * qlength :, :] = own


def route_first(replicas, stored_ref, table_ref):
    me = lax.axis_index("replica")
    for s in range(replicas):
        table_ref[replicas * CAP + s] = jnp.int32(0)
    return [stored_ref[0, lax.rem(me + s, replicas)] for s in range(replicas)]


def route_near(stored_ref, table_ref):
    me = lax.axis_index("replica")

    def held(replica):
        return [stored_ref[slot, replica] for slot in range(2)]

    def plan(replica):
        here, after, before = [held(lax.rem(replica + d, 4)) for d in (0, 1, 3)]
        done = jnp.bool_(False)
        slots = [jnp.int32(0), jnp.int32(0)]
        chosen = [after[0], before[0]]
        for i in range(2):
            for k in range(2):
                one, two = after[i], before[k]
                fits = (one != here[0]) & (one != here[1]) & (two != here[0]) & (two != here[1]) & (one != two)
                take = fits & jnp.logical_not(done)
                slots = [jnp.where(take, i, slots[0]), jnp.where(take, k, slots[1])]
                chosen = [jnp.where(take, one, chosen[0]), jnp.where(take, two, chosen[1])]
                done = done | fits
        return slots, chosen, done

    plans = [plan(lax.rem(me + d, 4)) for d in range(4)]
    failed = jnp.int32(0)
    for _, _, done in plans:
        failed = jnp.where(done, failed, 1)
    table_ref[8] = jnp.int32(0)
    table_ref[9] = jnp.int32(1)
    table_ref[10] = plans[3][0][0]
    table_ref[11] = plans[1][0][1]
    table_ref[12] = failed
    return held(me) + plans[0][1]


def pack(stored, ids, queries, own, phases, route):
    questions = ids.shape[1]
    head_size = own.shape[1]
    qlength = queries.shape[0] // questions
    heads = queries.shape[1] // head_size
    rows = heads * qlength + 2 * qlength
    arguments = [pltpu.with_memory_space_constraint(x, pltpu.HBM) for x in (stored, ids, queries, own)]
    out = pl.pallas_call(
        functools.partial(pack_kernel, route=route, heads=heads, qlength=qlength),
        in_specs=[pl.BlockSpec(memory_space=pltpu.HBM)] * 4,
        out_specs=[SMEM] + [VMEM] * phases,
        out_shape=[jax.ShapeDtypeStruct((phases * (CAP + 1) + 1,), jnp.int32)]
        + [jax.ShapeDtypeStruct((CAP, rows, head_size), BF16)] * phases,
        scratch_shapes=[
            pltpu.SMEM(stored.shape, jnp.int32),
            pltpu.SMEM(ids.shape, jnp.int32),
            pltpu.VMEM(queries.shape, BF16),
            pltpu.VMEM(own.shape, BF16),
            pltpu.SemaphoreType.DMA((4,)),
        ],
        compiler_params=pltpu.CompilerParams(vmem_limit_bytes=16 << 20),
        cost_estimate=pl.CostEstimate(flops=0, bytes_accessed=4 << 20, transcendentals=0),
        name="pack",
    )(*arguments)
    return out[0], out[1:]


def split_kernel(x_ref, k_ref, vt_ref, pairs_ref, wide_ref, sems):
    parts, block, head_size = pairs_ref.shape
    half = block // 2
    slots, depth, context = vt_ref.shape
    per_slot = context // half
    copies = [
        pltpu.make_async_copy(x_ref.at[pl.ds(i * block, block), :], pairs_ref.at[i], sems.at[i]) for i in range(parts)
    ]
    for copy in copies:
        copy.start()
    vt_ref[:, head_size:, :] = jnp.ones((slots, depth - head_size, context), BF16)
    for i, copy in enumerate(copies):
        slot, place = i // per_slot, i % per_slot
        copy.wait()
        wide = wide_ref.at[i % 2]
        wide[...] = pairs_ref[i].astype(F32)
        k_ref[slot, place * half : (place + 1) * half, :] = wide[pl.ds(0, half, stride=2), :].astype(BF16)
        values = wide[pl.ds(1, half, stride=2), :]
        vt_ref[slot, :head_size, place * half : (place + 1) * half] = values.T.astype(BF16)


def split(pairs, context, slots):
    head_size = pairs.shape[1]
    per_slot = 8
    block = 2 * context // per_slot
    parts = slots * per_slot
    return pl.pallas_call(
        split_kernel,
        in_specs=[pl.BlockSpec(memory_space=pltpu.HBM)],
        out_specs=[VMEM, VMEM],
        out_shape=[
            jax.ShapeDtypeStruct((slots, context, head_size), BF16),
            jax.ShapeDtypeStruct((slots, head_size + 16, context), BF16),
        ],
        scratch_shapes=[
            pltpu.VMEM((parts, block, head_size), BF16),
            pltpu.VMEM((2, block, head_size), F32),
            pltpu.SemaphoreType.DMA((parts,)),
        ],
        compiler_params=pltpu.CompilerParams(vmem_limit_bytes=16 << 20),
        cost_estimate=pl.CostEstimate(flops=0, bytes_accessed=8 * slots * context * head_size, transcendentals=0),
        name="split",
    )(pltpu.with_memory_space_constraint(pairs, pltpu.HBM))


def attend_kernel(table_ref, x_ref, keys_ref, values_ref, o_ref, *, entry, heads, qlength, chunk):
    slot = table_ref[entry]
    k_ref, vt_ref = keys_ref.at[slot], values_ref.at[slot]
    context, head_size = k_ref.shape
    scale = LOG2E / math.sqrt(head_size)
    rows = heads * qlength

    def one(i, carry):
        qt = x_ref[i, :rows, :].T
        own = x_ref[i, rows:, :]
        near = jnp.dot(own, qt, preferred_element_type=F32) * scale
        u2 = lax.broadcasted_iota(jnp.int32, near.shape, 0)
        t = lax.broadcasted_iota(jnp.int32, near.shape, 1) % qlength
        near = jnp.where((u2 % 2 == 0) & (u2 <= 2 * t), near, -jnp.inf)
        near_top = jnp.max(near, axis=0, keepdims=True)
        own_t = own.astype(F32).T.astype(BF16)
        own_vt = jnp.concatenate([own_t, jnp.ones((16, own.shape[0]), BF16)], axis=0)

        def mix_near(top):
            weights = pltpu.roll(jnp.exp2(near - top), 1, 0).astype(BF16)
            return jnp.dot(own_vt, weights, preferred_element_type=F32)

        def store(mixed):
            result = (mixed[:head_size] / mixed[head_size : head_size + 1]).T.astype(BF16)
            for h in range(heads):
                o_ref[pl.ds(pl.multiple_of(i * qlength, qlength), qlength), h * head_size : (h + 1) * head_size] = (
                    result[h * qlength : (h + 1) * qlength, :]
                )

        scores = jnp.dot(k_ref[...], qt, preferred_element_type=F32) * scale
        weights = jnp.exp2(scores - near_top).astype(BF16)
        mixed = jnp.dot(vt_ref[...], weights, preferred_element_type=F32) + mix_near(near_top)
        store(mixed)
        total = jnp.max(mixed[head_size : head_size + 1])

        @pl.when(jnp.logical_not(total < TOTAL_MAX))
        def _():
            def part(j):
                keys = k_ref[pl.ds(pl.multiple_of(j * chunk, chunk), chunk), :]
                return jnp.dot(keys, qt, preferred_element_type=F32) * scale

            def raise_top(j, top):
                return jnp.maximum(top, jnp.max(part(j), axis=0, keepdims=True))

            top = lax.fori_loop(0, context // chunk, raise_top, near_top)

            def add(j, mixed):
                weights = jnp.exp2(part(j) - top).astype(BF16)
                values = vt_ref[:, pl.ds(pl.multiple_of(j * chunk, chunk), chunk)]
                return mixed + jnp.dot(values, weights, preferred_element_type=F32)

            store(lax.fori_loop(0, context // chunk, add, mix_near(top)))

        return carry

    lax.fori_loop(0, x_ref.shape[0], one, 0)


def attend(table, entry, x, keys, values_t, heads, qlength):
    number, _, head_size = x.shape
    context = keys.shape[1]
    return pl.pallas_call(
        functools.partial(attend_kernel, entry=entry, heads=heads, qlength=qlength, chunk=512),
        in_specs=[SMEM, VMEM, VMEM, VMEM],
        out_specs=VMEM,
        out_shape=jax.ShapeDtypeStruct((number * qlength, heads * head_size), BF16),
        compiler_params=pltpu.CompilerParams(vmem_limit_bytes=24 << 20),
        cost_estimate=pl.CostEstimate(
            flops=8 * number * qlength * heads * context * head_size,
            bytes_accessed=4 << 20,
            transcendentals=number * qlength * heads * context,
        ),
        name="attend",
    )(table, x, keys, values_t)


def project_kernel(a_ref, w_ref, give_ref, keep_ref, *, flip, tile):
    columns = keep_ref.shape[1]
    me = lax.axis_index("tensor")

    def one(i, carry):
        out = pl.ds(pl.multiple_of(i * tile, tile), tile)
        for ref, block in ((give_ref, me ^ flip ^ 1), (keep_ref, me ^ flip)):
            source = pl.ds(pl.multiple_of(block * columns + i * tile, tile), tile)
            product = jnp.dot(a_ref[...], w_ref[:, source], preferred_element_type=F32)
            ref[:, out] = product.astype(ref.dtype)
        return carry

    lax.fori_loop(0, columns // tile, one, 0)


def project(rows, weight, flip, shares, tile):
    number, depth = rows.shape
    columns = weight.shape[1] // shares
    return pl.pallas_call(
        functools.partial(project_kernel, flip=flip, tile=tile),
        in_specs=[VMEM, VMEM],
        out_specs=[VMEM, VMEM],
        out_shape=[
            jax.ShapeDtypeStruct((number, columns), BF16),
            jax.ShapeDtypeStruct((number, columns), F32),
        ],
        compiler_params=pltpu.CompilerParams(vmem_limit_bytes=12 << 20),
        cost_estimate=pl.CostEstimate(
            flops=4 * number * depth * columns, bytes_accessed=4 * depth * columns, transcendentals=0
        ),
        name="project",
    )(rows, weight)


def finish_kernel(table_ref, counts_ref, kept_ref, core_ref, far_ref, *refs, first, qlength):
    o_ref, block_ref, sems = refs[-3:]
    copies = []
    for i in range(block_ref.shape[0]):
        place = jnp.maximum(table_ref[first + i], 0)
        rows = slice(i * qlength, (i + 1) * qlength)
        total = kept_ref[rows, :] + core_ref[rows, :].astype(F32) + far_ref[rows, :].astype(F32)
        t = lax.broadcasted_iota(jnp.int32, total.shape, 0)
        block_ref[i] = jnp.where(t < counts_ref[0, place], total, 0.0).astype(BF16)
        target = o_ref.at[pl.ds(pl.multiple_of(place * qlength, qlength), qlength), :]
        copies.append(pltpu.make_async_copy(block_ref.at[i], target, sems.at[i]))
        copies[-1].start()
    for copy in copies:
        copy.wait()


def finish(table, counts, kept, from_core, from_far, first, previous, rows, qlength):
    number, columns = kept.shape[0] // qlength, kept.shape[1]
    extra = [] if previous is None else [previous]
    hbm = pl.BlockSpec(memory_space=pl.ANY)
    return pl.pallas_call(
        functools.partial(finish_kernel, first=first, qlength=qlength),
        in_specs=[SMEM, SMEM, VMEM, VMEM, VMEM] + [hbm] * len(extra),
        out_specs=hbm,
        out_shape=jax.ShapeDtypeStruct((rows, columns), BF16),
        scratch_shapes=[pltpu.VMEM((number, qlength, columns), BF16), pltpu.SemaphoreType.DMA((number,))],
        input_output_aliases={5: 0} if extra else {},
        compiler_params=pltpu.CompilerParams(vmem_limit_bytes=16 << 20),
        cost_estimate=pl.CostEstimate(flops=0, bytes_accessed=20 * number * qlength * columns, transcendentals=0),
        name="finish",
    )(table, counts, kept, from_core, from_far, *extra)


def by_shift(shift, replicas):
    return [(i, (i + shift) % replicas) for i in range(replicas)]


def small_slice(groups, replicas, shares):
    return groups <= 2 and replicas == 4 and shares == 4


def project_out(table, counts, results, weight, shares, first, out, rows, qlength):
    other_core = [(i, i ^ 1) for i in range(shares)]
    other_chip = [(i, i ^ 2) for i in range(shares)]
    tile = 512
    far_give, far_keep = project(results, weight, 2, shares, tile)
    far_core = lax.ppermute(far_give, "tensor", other_core)
    near_give, near_keep = project(results, weight, 0, shares, tile)
    near_core = lax.ppermute(near_give, "tensor", other_core)
    chip_sum = (far_keep + far_core.astype(F32)).astype(BF16)
    far = lax.ppermute(chip_sum, "tensor", other_chip)
    return finish(table, counts, near_keep, near_core, far, first, out, rows, qlength)


def answer_by_first_slots(queries, own, keys, values_t, stored, ids, heads, qlength):
    replicas = stored.shape[1]
    route = functools.partial(route_first, replicas)
    table, packed = pack(stored, ids, queries, own, replicas, route)
    arrived = [packed[0]] + [lax.ppermute(packed[s], "replica", by_shift(s, replicas)) for s in range(1, replicas)]
    result = attend(table, replicas * CAP, jnp.concatenate(arrived), keys, values_t, heads, qlength)
    parts = result.reshape(replicas, CAP * qlength, -1)
    returned = [parts[0]] + [lax.ppermute(parts[s], "replica", by_shift(-s, replicas)) for s in range(1, replicas)]
    return table, jnp.concatenate(returned)


def on_device(queries, new_kv, cache_kv, stored, haystack_ids, token_counts, out_weight):
    groups = lax.axis_size("groups")
    replicas = lax.axis_size("replica")
    shares = lax.axis_size("tensor")
    slots, context = cache_kv.shape[:2]
    head_size = cache_kv.shape[-1]
    questions = haystack_ids.shape[0]
    rows = queries.shape[0]
    qlength = rows // questions
    heads = queries.shape[1] // head_size
    own = new_kv.reshape(2 * rows, head_size)
    pairs = cache_kv.reshape(-1, head_size)
    ids = haystack_ids.T
    stored = stored.T

    if small_slice(groups, replicas, shares) and replicas * CAP == questions and slots == 2:
        table, packed = pack(stored, ids, queries, own, 4, route_near)
        arrived, returned = dict(enumerate(packed)), {}
        shifts = {2: 1, 3: -1}
        for s, shift in shifts.items():
            arrived[s] = lax.ppermute(packed[s], "replica", by_shift(shift, replicas))
        keys, values_t = split(pairs, context, slots)
        for s in range(4):
            returned[s] = attend(table, 8 + s, arrived[s], keys, values_t, heads, qlength)
            if s in shifts:
                returned[s] = lax.ppermute(returned[s], "replica", by_shift(-shifts[s], replicas))
        out = None
        for s in range(4):
            out = project_out(table, token_counts, returned[s], out_weight, shares, s * CAP, out, rows, qlength)
        failed = table[12]
        if groups == 2:
            failed = failed + lax.ppermute(failed, "groups", [(0, 1), (1, 0)])

        def again():
            keys, values_t = split(pairs, context, 1)
            table, results = answer_by_first_slots(queries, own, keys, values_t, stored, ids, heads, qlength)
            return project_out(table, token_counts, results, out_weight, shares, 0, None, rows, qlength)

        return lax.cond(failed > 0, again, lambda: out)

    keys, values_t = split(pairs, context, 1)
    table, results = answer_by_first_slots(queries, own, keys, values_t, stored, ids, heads, qlength)
    blocks = results.reshape(replicas * CAP, qlength, -1)
    match = table[None, : replicas * CAP] == jnp.arange(questions, dtype=jnp.int32)[:, None]
    position = jnp.argmax(match.astype(jnp.int32), axis=1)
    used = jnp.arange(qlength, dtype=jnp.int32)[None, :] < token_counts[0][:, None]
    attended = jnp.where(used[..., None], blocks[position], jnp.zeros((), BF16)).reshape(rows, -1)
    summed = lax.psum_scatter(
        lax.dot_general(out_weight, attended, (((0,), (1,)), ((), ())), preferred_element_type=F32),
        "tensor",
        scatter_dimension=0,
        tiled=True,
    )
    return summed.T.astype(BF16)


def solution(mesh):
    in_specs = (
        P(("groups", "replica"), "tensor"),
        P(("groups", "replica"), None, "tensor"),
        P(("groups", "replica"), None, None, "tensor"),
        P("groups", None),
        P(("groups", "replica"), None),
        P(("groups", "replica"), None),
        P("tensor", None),
    )
    out_specs = P(("groups", "replica"), "tensor")
    return jax.shard_map(
        on_device, mesh=mesh, in_specs=in_specs, out_specs=out_specs, check_vma=False
    )
```

profile of v0, /device:TPU:0, one launch (start us, length us, event | category | flops | bytes accessed | tf_op | source)
XLA Modules:
  0.0 173.6 jit_solution(5223812837112665264)
XLA Ops:
  0.0 2.0 %pack.3 = (s32[13]{0:T(128)S(1)}, bf16[2,640,128]{2,1,0:T(8,128)(2,1)S(1)}, bf16[2,640,128]{2,1,0:T(8,128)(2,1)S(1)}, bf16[2,640,128]{2,1,0:T(8,128)(2,1)S(1)}, bf16[2,640,128]{2,1,0:T(8,128)(2,1)S(1)}) custom-call(s32[2,4]{1,0:T(2,128)} %bitcast.11, s32[1,8]{1,0:T(1,128)} %bitcast.13, bf16[512,1024]{1,0:T(8,128)(2,1)} %q_hbm.1, bf16[1024,128]{1,0:T(8,128)(2,1)} %bitcast.9), custom_call_target="tpu_custom_call" | custom-call | bytes 4194304 | tf_op jit(solution)/shard_map/pack/pallas_call | solution.py:103
  2.7 3.0 %collective-permute-start.9 = (s32[]{:T(128)}, s32[]{:T(128)}, u32[]{:S(2)}, u32[]{:S(2)}) collective-permute-start(s32[]{:T(128)} %bitcast.3), channel_id=1, source_target_pairs={{0,16},{16,0},{1,17},{17,1},{2,18},{18,2},{3,19},{19,3},{4,20},{20... | collective-permute-start | bytes 20 | tf_op jit(solution)/shard_map/ppermute | solution.py:374
  5.6 3.6 %collective-permute-start.10 = (bf16[2,640,128]{2,1,0:T(8,128)(2,1)S(1)}, bf16[2,640,128]{2,1,0:T(8,128)(2,1)S(1)}, u32[]{:S(2)}, u32[]{:S(2)}) collective-permute-start(bf16[2,640,128]{2,1,0:T(8,128)(2,1)S(1)} %get-tuple-element.65), channel_id=1, source_target_pairs={{0,12},{4,0},{8,4},{12,8},{1,13},{5,1},{9,5},{13,9},{2,14},{6,2},{... | collective-permute-start | bytes 983048 | tf_op jit(solution)/shard_map/ppermute | solution.py:363
  9.2 3.4 %split.3 = (bf16[2,4096,128]{2,1,0:T(8,128)(2,1)S(1)}, bf16[2,144,4096]{2,1,0:T(8,128)(2,1)S(1)}) custom-call(bf16[16384,128]{1,0:T(8,128)(2,1)} %bitcast.7), custom_call_target="tpu_custom_call" | custom-call | bytes 8388608 | tf_op jit(solution)/shard_map/split/pallas_call | solution.py:149
  12.6 18.6 %attend.8.a_ref = bf16[128,1024]{1,0:T(8,128)(2,1)S(1)} custom-call(s32[13]{0:T(128)S(1)} %get-tuple-element.64.table_ref, bf16[2,640,128]{2,1,0:T(8,128)(2,1)S(1)} %get-tuple-element.77.x_ref, bf16[2,4096,128]{2,1,0:T(8,128)(2,1)S(1)} %get-tuple-element.66.keys_ref, bf16[2,144,4096]{2,1,0:T(8,128)(2,1)S(1)} %get-tuple-element.67.values_ref), custom_call_target="tpu_custom_call" | custom-call | flops 4294967296 | bytes 4194304 | tf_op jit(solution)/shard_map/attend/pallas_call | solution.py:229
  31.3 1.9 %project.17 = (bf16[128,2048]{1,0:T(8,128)(2,1)S(1)}, f32[128,2048]{1,0:T(8,128)S(1)}) custom-call(bf16[128,1024]{1,0:T(8,128)(2,1)S(1)} %attend.8.a_ref, bf16[1024,8192]{1,0:T(8,128)(2,1)S(1)} %copy-done.8), custom_call_target="tpu_custom_call" | custom-call | flops 1073741824 | bytes 8388608 | tf_op jit(solution)/shard_map/project/pallas_call | solution.py:262
  33.2 1.9 %project.16 = (bf16[128,2048]{1,0:T(8,128)(2,1)S(1)}, f32[128,2048]{1,0:T(8,128)S(1)}) custom-call(bf16[128,1024]{1,0:T(8,128)(2,1)S(1)} %attend.8.a_ref, bf16[1024,8192]{1,0:T(8,128)(2,1)S(1)} %copy-done.8), custom_call_target="tpu_custom_call" | custom-call | flops 1073741824 | bytes 8388608 | tf_op jit(solution)/shard_map/project/pallas_call | solution.py:262
  35.6 18.6 %attend.9.a_ref = bf16[128,1024]{1,0:T(8,128)(2,1)S(1)} custom-call(s32[13]{0:T(128)S(1)} %get-tuple-element.64.table_ref, bf16[2,640,128]{2,1,0:T(8,128)(2,1)S(1)} %get-tuple-element.82.x_ref, bf16[2,4096,128]{2,1,0:T(8,128)(2,1)S(1)} %get-tuple-element.66.keys_ref, bf16[2,144,4096]{2,1,0:T(8,128)(2,1)S(1)} %get-tuple-element.67.values_ref), custom_call_target="tpu_custom_call" | custom-call | flops 4294967296 | bytes 4194304 | tf_op jit(solution)/shard_map/attend/pallas_call | solution.py:229
  54.3 1.8 %project.19 = (bf16[128,2048]{1,0:T(8,128)(2,1)S(1)}, f32[128,2048]{1,0:T(8,128)S(1)}) custom-call(bf16[128,1024]{1,0:T(8,128)(2,1)S(1)} %attend.9.a_ref, bf16[1024,8192]{1,0:T(8,128)(2,1)S(1)} %copy-done.8), custom_call_target="tpu_custom_call" | custom-call | flops 1073741824 | bytes 8388608 | tf_op jit(solution)/shard_map/project/pallas_call | solution.py:262
  56.1 1.8 %project.18 = (bf16[128,2048]{1,0:T(8,128)(2,1)S(1)}, f32[128,2048]{1,0:T(8,128)S(1)}) custom-call(bf16[128,1024]{1,0:T(8,128)(2,1)S(1)} %attend.9.a_ref, bf16[1024,8192]{1,0:T(8,128)(2,1)S(1)} %copy-done.8), custom_call_target="tpu_custom_call" | custom-call | flops 1073741824 | bytes 8388608 | tf_op jit(solution)/shard_map/project/pallas_call | solution.py:262
  58.1 18.6 %attend.7 = bf16[128,1024]{1,0:T(8,128)(2,1)S(1)} custom-call(s32[13]{0:T(128)S(1)} %get-tuple-element.64.table_ref, bf16[2,640,128]{2,1,0:T(8,128)(2,1)S(1)} %collective-permute-done.15.x_ref, bf16[2,4096,128]{2,1,0:T(8,128)(2,1)S(1)} %get-tuple-element.66.keys_ref, bf16[2,144,4096]{2,1,0:T(8,128)(2,1)S(1)} %get-tuple-element.67.values_ref), custom_call_target="tpu_custom_call" | custom-call | flops 4294967296 | bytes 4194304 | tf_op jit(solution)/shard_map/attend/pallas_call | solution.py:229
  77.3 18.8 %attend.6 = bf16[128,1024]{1,0:T(8,128)(2,1)S(1)} custom-call(s32[13]{0:T(128)S(1)} %get-tuple-element.64.table_ref, bf16[2,640,128]{2,1,0:T(8,128)(2,1)S(1)} %collective-permute-done.10.x_ref, bf16[2,4096,128]{2,1,0:T(8,128)(2,1)S(1)} %get-tuple-element.66.keys_ref, bf16[2,144,4096]{2,1,0:T(8,128)(2,1)S(1)} %get-tuple-element.67.values_ref), custom_call_target="tpu_custom_call" | custom-call | flops 4294967296 | bytes 4194304 | tf_op jit(solution)/shard_map/attend/pallas_call | solution.py:229
  96.1 3.9 %collective-permute-start.16 = (bf16[128,1024]{1,0:T(8,128)(2,1)S(1)}, bf16[128,1024]{1,0:T(8,128)(2,1)S(1)}, u32[]{:S(2)}, u32[]{:S(2)}) collective-permute-start(bf16[128,1024]{1,0:T(8,128)(2,1)S(1)} %attend.7), channel_id=1, source_target_pairs={{0,12},{4,0},{8,4},{12,8},{1,13},{5,1},{9,5},{13,9},{2,14},{6,2},{... | collective-permute-start | bytes 786440 | tf_op jit(solution)/shard_map/ppermute | solution.py:368
  100.9 5.3 %collective-permute-done.16.a_ref = bf16[128,1024]{1,0:T(8,128)(2,1)S(1)} collective-permute-done((bf16[128,1024]{1,0:T(8,128)(2,1)S(1)}, bf16[128,1024]{1,0:T(8,128)(2,1)S(1)}, u32[]{:S(2)}, u32[]{:S(2)}) %collective-permute-start.16) | collective-permute-done | bytes 262176 | tf_op jit(solution)/shard_map/ppermute | solution.py:368
  106.2 1.8 %project.15 = (bf16[128,2048]{1,0:T(8,128)(2,1)S(1)}, f32[128,2048]{1,0:T(8,128)S(1)}) custom-call(bf16[128,1024]{1,0:T(8,128)(2,1)S(1)} %collective-permute-done.16.a_ref, bf16[1024,8192]{1,0:T(8,128)(2,1)S(1)} %copy-done.8), custom_call_target="tpu_custom_call" | custom-call | flops 1073741824 | bytes 8388608 | tf_op jit(solution)/shard_map/project/pallas_call | solution.py:262
  108.2 7.4 %collective-permute-done.11.a_ref = bf16[128,1024]{1,0:T(8,128)(2,1)S(1)} collective-permute-done((bf16[128,1024]{1,0:T(8,128)(2,1)S(1)}, bf16[128,1024]{1,0:T(8,128)(2,1)S(1)}, u32[]{:S(2)}, u32[]{:S(2)}) %collective-permute-start.11) | collective-permute-done | bytes 262176 | tf_op jit(solution)/shard_map/ppermute | solution.py:368
  115.6 1.8 %project.13 = (bf16[128,2048]{1,0:T(8,128)(2,1)S(1)}, f32[128,2048]{1,0:T(8,128)S(1)}) custom-call(bf16[128,1024]{1,0:T(8,128)(2,1)S(1)} %collective-permute-done.11.a_ref, bf16[1024,8192]{1,0:T(8,128)(2,1)S(1)} %copy-done.8), custom_call_target="tpu_custom_call" | custom-call | flops 1073741824 | bytes 8388608 | tf_op jit(solution)/shard_map/project/pallas_call | solution.py:262
  117.6 2.5 %project.14 = (bf16[128,2048]{1,0:T(8,128)(2,1)}, f32[128,2048]{1,0:T(8,128)S(1)}) custom-call(bf16[128,1024]{1,0:T(8,128)(2,1)S(1)} %collective-permute-done.16.a_ref, bf16[1024,8192]{1,0:T(8,128)(2,1)S(1)} %copy-done.8), custom_call_target="tpu_custom_call" | custom-call | flops 1073741824 | bytes 8388608 | tf_op jit(solution)/shard_map/project/pallas_call | solution.py:262
  120.1 2.5 %project.12 = (bf16[128,2048]{1,0:T(8,128)(2,1)}, f32[128,2048]{1,0:T(8,128)S(1)}) custom-call(bf16[128,1024]{1,0:T(8,128)(2,1)S(1)} %collective-permute-done.11.a_ref, bf16[1024,8192]{1,0:T(8,128)(2,1)S(1)} %copy-done.8), custom_call_target="tpu_custom_call" | custom-call | flops 1073741824 | bytes 8388608 | tf_op jit(solution)/shard_map/project/pallas_call | solution.py:262
  122.6 1.5 collective-permute-start.25
  129.9 7.5 %collective-permute-done.25.far_ref = bf16[128,2048]{1,0:T(8,128)(2,1)S(1)} collective-permute-done((bf16[128,2048]{1,0:T(8,128)(2,1)S(1)}, bf16[128,2048]{1,0:T(8,128)(2,1)S(1)}, u32[]{:S(2)}, u32[]{:S(2)}) %collective-permute-start.25) | collective-permute-done | bytes 524320 | tf_op jit(solution)/shard_map/ppermute | solution.py:328
  143.9 4.8 %collective-permute-done.22.far_ref = bf16[128,2048]{1,0:T(8,128)(2,1)} collective-permute-done((bf16[128,2048]{1,0:T(8,128)(2,1)}, bf16[128,2048]{1,0:T(8,128)(2,1)}, u32[]{:S(2)}, u32[]{:S(2)}) %collective-permute-start.22) | collective-permute-done | bytes 524320 | tf_op jit(solution)/shard_map/ppermute | solution.py:328
  150.2 9.8 %collective-permute-done.19.far_ref = bf16[128,2048]{1,0:T(8,128)(2,1)} collective-permute-done((bf16[128,2048]{1,0:T(8,128)(2,1)}, bf16[128,2048]{1,0:T(8,128)(2,1)}, u32[]{:S(2)}, u32[]{:S(2)}) %collective-permute-start.19) | collective-permute-done | bytes 524320 | tf_op jit(solution)/shard_map/ppermute | solution.py:328
  161.5 9.2 %collective-permute-done.14.far_ref = bf16[128,2048]{1,0:T(8,128)(2,1)} collective-permute-done((bf16[128,2048]{1,0:T(8,128)(2,1)}, bf16[128,2048]{1,0:T(8,128)(2,1)}, u32[]{:S(2)}, u32[]{:S(2)}) %collective-permute-start.14) | collective-permute-done | bytes 524320 | tf_op jit(solution)/shard_map/ppermute | solution.py:328
  (56 shorter events, 19.7 us)
Async XLA Ops:
  2.7 123.8 %collective-permute-start.9 = (s32[]{:T(128)}, s32[]{:T(128)}, u32[]{:S(2)}, u32[]{:S(2)}) collective-permute-start(s32[]{:T(128)} %bitcast.3), channel_id=1, source_target_pairs={{0,16},{16,0},{1,17},{17,1},{2,18},{18,2},{3,19},{19,3},{4,20},{20... | collective-permute-start | bytes 20 | tf_op jit(solution)/shard_map/ppermute | solution.py:374
  5.6 71.1 %collective-permute-start.10 = (bf16[2,640,128]{2,1,0:T(8,128)(2,1)S(1)}, bf16[2,640,128]{2,1,0:T(8,128)(2,1)S(1)}, u32[]{:S(2)}, u32[]{:S(2)}) collective-permute-start(bf16[2,640,128]{2,1,0:T(8,128)(2,1)S(1)} %get-tuple-element.65), channel_id=1, source_target_pairs={{0,12},{4,0},{8,4},{12,8},{1,13},{5,1},{9,5},{13,9},{2,14},{6,2},{... | collective-permute-start | bytes 983048 | tf_op jit(solution)/shard_map/ppermute | solution.py:363
  9.2 48.8 %collective-permute-start.15 = (bf16[2,640,128]{2,1,0:T(8,128)(2,1)S(1)}, bf16[2,640,128]{2,1,0:T(8,128)(2,1)S(1)}, u32[]{:S(2)}, u32[]{:S(2)}) collective-permute-start(bf16[2,640,128]{2,1,0:T(8,128)(2,1)S(1)} %get-tuple-element.72), channel_id=1, source_target_pairs={{0,4},{4,8},{8,12},{12,0},{1,5},{5,9},{9,13},{13,1},{2,6},{6,10},{... | collective-permute-start | bytes 983048 | tf_op jit(solution)/shard_map/ppermute | solution.py:363
  9.2 22.1 %copy-start.8 = (bf16[1024,8192]{1,0:T(8,128)(2,1)S(1)}, bf16[1024,8192]{1,0:T(8,128)(2,1)}, u32[]{:S(2)}) copy-start(bf16[1024,8192]{1,0:T(8,128)(2,1)} %w_ref.15) | copy-start | bytes 50331652
  33.2 63.0 %collective-permute-start.21 = (bf16[128,2048]{1,0:T(8,128)(2,1)S(1)}, bf16[128,2048]{1,0:T(8,128)(2,1)S(1)}, u32[]{:S(2)}, u32[]{:S(2)}) collective-permute-start(bf16[128,2048]{1,0:T(8,128)(2,1)S(1)} %get-tuple-element.81), channel_id=1, source_target_pairs={{0,1},{1,0},{2,3},{3,2},{4,5},{5,4},{6,7},{7,6},{8,9},{9,8},{10,11... | collective-permute-start | bytes 1572872 | tf_op jit(solution)/shard_map/ppermute | solution.py:324
  35.1 91.4 %collective-permute-start.20 = (bf16[128,2048]{1,0:T(8,128)(2,1)S(1)}, bf16[128,2048]{1,0:T(8,128)(2,1)S(1)}, u32[]{:S(2)}, u32[]{:S(2)}) collective-permute-start(bf16[128,2048]{1,0:T(8,128)(2,1)S(1)} %get-tuple-element.79), channel_id=1, source_target_pairs={{0,1},{1,0},{2,3},{3,2},{4,5},{5,4},{6,7},{7,6},{8,9},{9,8},{10,11... | collective-permute-start | bytes 1572872 | tf_op jit(solution)/shard_map/ppermute | solution.py:326
  58.0 50.0 %collective-permute-start.24 = (bf16[128,2048]{1,0:T(8,128)(2,1)S(1)}, bf16[128,2048]{1,0:T(8,128)(2,1)S(1)}, u32[]{:S(2)}, u32[]{:S(2)}) collective-permute-start(bf16[128,2048]{1,0:T(8,128)(2,1)S(1)} %get-tuple-element.86), channel_id=1, source_target_pairs={{0,1},{1,0},{2,3},{3,2},{4,5},{5,4},{6,7},{7,6},{8,9},{9,8},{10,11... | collective-permute-start | bytes 1572872 | tf_op jit(solution)/shard_map/ppermute | solution.py:324
  76.7 52.1 %collective-permute-start.23 = (bf16[128,2048]{1,0:T(8,128)(2,1)S(1)}, bf16[128,2048]{1,0:T(8,128)(2,1)S(1)}, u32[]{:S(2)}, u32[]{:S(2)}) collective-permute-start(bf16[128,2048]{1,0:T(8,128)(2,1)S(1)} %get-tuple-element.84), channel_id=1, source_target_pairs={{0,1},{1,0},{2,3},{3,2},{4,5},{5,4},{6,7},{7,6},{8,9},{9,8},{10,11... | collective-permute-start | bytes 1572872 | tf_op jit(solution)/shard_map/ppermute | solution.py:326
  96.1 10.0 %collective-permute-start.16 = (bf16[128,1024]{1,0:T(8,128)(2,1)S(1)}, bf16[128,1024]{1,0:T(8,128)(2,1)S(1)}, u32[]{:S(2)}, u32[]{:S(2)}) collective-permute-start(bf16[128,1024]{1,0:T(8,128)(2,1)S(1)} %attend.7), channel_id=1, source_target_pairs={{0,12},{4,0},{8,4},{12,8},{1,13},{5,1},{9,5},{13,9},{2,14},{6,2},{... | collective-permute-start | bytes 786440 | tf_op jit(solution)/shard_map/ppermute | solution.py:368
  106.2 9.5 %collective-permute-start.11 = (bf16[128,1024]{1,0:T(8,128)(2,1)S(1)}, bf16[128,1024]{1,0:T(8,128)(2,1)S(1)}, u32[]{:S(2)}, u32[]{:S(2)}) collective-permute-start(bf16[128,1024]{1,0:T(8,128)(2,1)S(1)} %attend.6), channel_id=1, source_target_pairs={{0,4},{4,8},{8,12},{12,0},{1,5},{5,9},{9,13},{13,1},{2,6},{6,10},{... | collective-permute-start | bytes 786440 | tf_op jit(solution)/shard_map/ppermute | solution.py:368
  108.0 14.6 %collective-permute-start.18 = (bf16[128,2048]{1,0:T(8,128)(2,1)S(1)}, bf16[128,2048]{1,0:T(8,128)(2,1)S(1)}, u32[]{:S(2)}, u32[]{:S(2)}) collective-permute-start(bf16[128,2048]{1,0:T(8,128)(2,1)S(1)} %get-tuple-element.76), channel_id=1, source_target_pairs={{0,1},{1,0},{2,3},{3,2},{4,5},{5,4},{6,7},{7,6},{8,9},{9,8},{10,11... | collective-permute-start | bytes 1572872 | tf_op jit(solution)/shard_map/ppermute | solution.py:324
  117.5 7.6 %collective-permute-start.13 = (bf16[128,2048]{1,0:T(8,128)(2,1)S(1)}, bf16[128,2048]{1,0:T(8,128)(2,1)S(1)}, u32[]{:S(2)}, u32[]{:S(2)}) collective-permute-start(bf16[128,2048]{1,0:T(8,128)(2,1)S(1)} %get-tuple-element.71), channel_id=1, source_target_pairs={{0,1},{1,0},{2,3},{3,2},{4,5},{5,4},{6,7},{7,6},{8,9},{9,8},{10,11... | collective-permute-start | bytes 1572872 | tf_op jit(solution)/shard_map/ppermute | solution.py:324
  120.1 2.5 %copy-start = (f32[128,2048]{1,0:T(8,128)}, f32[128,2048]{1,0:T(8,128)S(1)}, u32[]{:S(2)}) copy-start(f32[128,2048]{1,0:T(8,128)S(1)} %get-tuple-element.73.kept_ref) | copy-start | bytes 3145732
  122.6 14.8 %collective-permute-start.25 = (bf16[128,2048]{1,0:T(8,128)(2,1)S(1)}, bf16[128,2048]{1,0:T(8,128)(2,1)S(1)}, u32[]{:S(2)}, u32[]{:S(2)}) collective-permute-start(bf16[128,2048]{1,0:T(8,128)(2,1)S(1)} %add_convert_fusion.1), channel_id=1, source_target_pairs={{0,2},{1,3},{2,0},{3,1},{4,6},{5,7},{6,4},{7,5},{8,10},{9,11},{10,... | collective-permute-start | bytes 1572872 | tf_op jit(solution)/shard_map/ppermute | solution.py:328
  124.2 16.8 %copy-start.10 = (s32[1,8]{1,0:T(1,128)S(1)}, s32[1,8]{1,0:T(1,128)}, u32[]{:S(2)}) copy-start(s32[1,8]{1,0:T(1,128)} %counts_ref.7) | copy-start | bytes 100
  125.1 23.7 %collective-permute-start.22 = (bf16[128,2048]{1,0:T(8,128)(2,1)}, bf16[128,2048]{1,0:T(8,128)(2,1)}, u32[]{:S(2)}, u32[]{:S(2)}) collective-permute-start(bf16[128,2048]{1,0:T(8,128)(2,1)} %add_convert_fusion.2), channel_id=1, source_target_pairs={{0,2},{1,3},{2,0},{3,1},{4,6},{5,7},{6,4},{7,5},{8,10},{9,11},{10,... | collective-permute-start | bytes 1572872 | tf_op jit(solution)/shard_map/ppermute | solution.py:328
  126.5 23.7 %collective-permute-start.17 = (bf16[128,2048]{1,0:T(8,128)(2,1)}, bf16[128,2048]{1,0:T(8,128)(2,1)}, u32[]{:S(2)}, u32[]{:S(2)}) collective-permute-start(bf16[128,2048]{1,0:T(8,128)(2,1)} %get-tuple-element.74), channel_id=1, source_target_pairs={{0,1},{1,0},{2,3},{3,2},{4,5},{5,4},{6,7},{7,6},{8,9},{9,8},{10,11... | collective-permute-start | bytes 1572872 | tf_op jit(solution)/shard_map/ppermute | solution.py:326
  127.3 32.7 %collective-permute-start.19 = (bf16[128,2048]{1,0:T(8,128)(2,1)}, bf16[128,2048]{1,0:T(8,128)(2,1)}, u32[]{:S(2)}, u32[]{:S(2)}) collective-permute-start(bf16[128,2048]{1,0:T(8,128)(2,1)} %add_convert_fusion.3), channel_id=1, source_target_pairs={{0,2},{1,3},{2,0},{3,1},{4,6},{5,7},{6,4},{7,5},{8,10},{9,11},{10,... | collective-permute-start | bytes 1572872 | tf_op jit(solution)/shard_map/ppermute | solution.py:328
  129.7 31.9 %collective-permute-start.12 = (bf16[128,2048]{1,0:T(8,128)(2,1)}, bf16[128,2048]{1,0:T(8,128)(2,1)}, u32[]{:S(2)}, u32[]{:S(2)}) collective-permute-start(bf16[128,2048]{1,0:T(8,128)(2,1)} %get-tuple-element.69), channel_id=1, source_target_pairs={{0,1},{1,0},{2,3},{3,2},{4,5},{5,4},{6,7},{7,6},{8,9},{9,8},{10,11... | collective-permute-start | bytes 1572872 | tf_op jit(solution)/shard_map/ppermute | solution.py:326
  138.2 32.5 %collective-permute-start.14 = (bf16[128,2048]{1,0:T(8,128)(2,1)}, bf16[128,2048]{1,0:T(8,128)(2,1)}, u32[]{:S(2)}, u32[]{:S(2)}) collective-permute-start(bf16[128,2048]{1,0:T(8,128)(2,1)} %add_convert_fusion.4), channel_id=1, source_target_pairs={{0,2},{1,3},{2,0},{3,1},{4,6},{5,7},{6,4},{7,5},{8,10},{9,11},{10,... | collective-permute-start | bytes 1572872 | tf_op jit(solution)/shard_map/ppermute | solution.py:328
  141.0 1.0 copy-start.3
  143.1 5.7 %copy-start.7 = (bf16[128,2048]{1,0:T(8,128)(2,1)S(1)}, bf16[128,2048]{1,0:T(8,128)(2,1)}, u32[]{:S(2)}) copy-start(bf16[128,2048]{1,0:T(8,128)(2,1)} %copy-done.6) | copy-start | bytes 1572868
  148.8 11.2 %copy-start.1 = (f32[128,2048]{1,0:T(8,128)S(1)}, f32[128,2048]{1,0:T(8,128)}, u32[]{:S(2)}) copy-start(f32[128,2048]{1,0:T(8,128)} %copy-done) | copy-start | bytes 3145732
  172.3 1.3 copy-start.9
  (4 other events, 3.5 us)
where the time goes:
time: 174 us
  Pallas kernels  102 us (59%)
  waiting for transfers between devices  44.1 us (25%)
  starting transfers between devices  17.2 us (10%)
  local copies, waits for them, and re-layouts  6.42 us (4%)
  other arithmetic  2.83 us (2%)
    pallas_call x4, Pallas kernels, attend(): pl.pallas_call(functools.partial(attend_kernel, entry=entry, heads=heads,...  74.7 us
    ppermute x4, waiting for transfers between devices, project_out(): far = lax.ppermute(chip_sum, 'tensor', other_chip)  31.4 us
    pallas_call x8, Pallas kernels, project(): pl.pallas_call(functools.partial(project_kernel, flip=flip, tile=tile), i...  16.1 us
    ppermute x2, waiting for transfers between devices, on_device(): lax.ppermute(returned[s], 'replica', by_shift(-shifts[s], replicas))  12.7 us
    unnamed x22, local copies, waits for them, and re-layouts  5.82 us
    pallas_call x4, Pallas kernels, finish(): pl.pallas_call(functools.partial(finish_kernel, first=first, qlength=qlen...  5.25 us
    ppermute x4, starting transfers between devices, project_out(): far = lax.ppermute(chip_sum, 'tensor', other_chip)  5.1 us
    ppermute x2, starting transfers between devices, on_device(): lax.ppermute(returned[s], 'replica', by_shift(-shifts[s], replicas))  3.85 us
  transfers between devices with their start and end apart: 17, of which 6 were waited for; matrix products, arithmetic and copies ran while one was open for 2% of the time, Pallas kernels for 56%

commit v1 on v0

--- a/solution.py
+++ b/solution.py
@@ -120,35 +120,36 @@
     return out[0], out[1:]
 
 
-def split_kernel(x_ref, k_ref, vt_ref, pairs_ref, wide_ref, sems):
+def split_kernel(x_ref, *refs, slot):
+    k_ref, vt_ref, pairs_ref, wide_ref, sems = refs[-5:]
     parts, block, head_size = pairs_ref.shape
     half = block // 2
-    slots, depth, context = vt_ref.shape
-    per_slot = context // half
+    depth, context = vt_ref.shape[1:]
     copies = [
-        pltpu.make_async_copy(x_ref.at[pl.ds(i * block, block), :], pairs_ref.at[i], sems.at[i]) for i in range(parts)
+        pltpu.make_async_copy(x_ref.at[pl.ds((slot * parts + i) * block, block), :], pairs_ref.at[i], sems.at[i])
+        for i in range(parts)
     ]
     for copy in copies:
         copy.start()
-    vt_ref[:, head_size:, :] = jnp.ones((slots, depth - head_size, context), BF16)
+    vt_ref[slot, head_size:, :] = jnp.ones((depth - head_size, context), BF16)
     for i, copy in enumerate(copies):
-        slot, place = i // per_slot, i % per_slot
         copy.wait()
         wide = wide_ref.at[i % 2]
         wide[...] = pairs_ref[i].astype(F32)
-        k_ref[slot, place * half : (place + 1) * half, :] = wide[pl.ds(0, half, stride=2), :].astype(BF16)
+        k_ref[slot, i * half : (i + 1) * half, :] = wide[pl.ds(0, half, stride=2), :].astype(BF16)
         values = wide[pl.ds(1, half, stride=2), :]
-        vt_ref[slot, :head_size, place * half : (place + 1) * half] = values.T.astype(BF16)
-
-
-def split(pairs, context, slots):
+        vt_ref[slot, :head_size, i * half : (i + 1) * half] = values.T.astype(BF16)
+
+
+def split(pairs, context, slots, slot=0, previous=None, after=None):
     head_size = pairs.shape[1]
-    per_slot = 8
-    block = 2 * context // per_slot
-    parts = slots * per_slot
+    parts = 8
+    block = 2 * context // parts
+    hbm = pl.BlockSpec(memory_space=pltpu.HBM)
+    extra = [] if previous is None else [*previous, after]
     return pl.pallas_call(
-        split_kernel,
-        in_specs=[pl.BlockSpec(memory_space=pltpu.HBM)],
+        functools.partial(split_kernel, slot=slot),
+        in_specs=[hbm] + ([VMEM, VMEM, pl.BlockSpec(memory_space=pl.ANY)] if extra else []),
         out_specs=[VMEM, VMEM],
         out_shape=[
             jax.ShapeDtypeStruct((slots, context, head_size), BF16),
@@ -159,10 +160,11 @@
             pltpu.VMEM((2, block, head_size), F32),
             pltpu.SemaphoreType.DMA((parts,)),
         ],
+        input_output_aliases={1: 0, 2: 1} if extra else {},
         compiler_params=pltpu.CompilerParams(vmem_limit_bytes=16 << 20),
-        cost_estimate=pl.CostEstimate(flops=0, bytes_accessed=8 * slots * context * head_size, transcendentals=0),
+        cost_estimate=pl.CostEstimate(flops=0, bytes_accessed=8 * context * head_size, transcendentals=0),
         name="split",
-    )(pltpu.with_memory_space_constraint(pairs, pltpu.HBM))
+    )(pltpu.with_memory_space_constraint(pairs, pltpu.HBM), *extra)
 
 
 def attend_kernel(table_ref, x_ref, keys_ref, values_ref, o_ref, *, entry, heads, qlength, chunk):
@@ -231,7 +233,7 @@
         in_specs=[SMEM, VMEM, VMEM, VMEM],
         out_specs=VMEM,
         out_shape=jax.ShapeDtypeStruct((number * qlength, heads * head_size), BF16),
-        compiler_params=pltpu.CompilerParams(vmem_limit_bytes=24 << 20),
+        compiler_params=pltpu.CompilerParams(vmem_limit_bytes=20 << 20),
         cost_estimate=pl.CostEstimate(
             flops=8 * number * qlength * heads * context * head_size,
             bytes_accessed=4 << 20,
@@ -293,13 +295,13 @@
 
 def finish(table, counts, kept, from_core, from_far, first, previous, rows, qlength):
     number, columns = kept.shape[0] // qlength, kept.shape[1]
-    extra = [] if previous is None else [previous]
-    hbm = pl.BlockSpec(memory_space=pl.ANY)
+    extra = [] if previous is None else [pltpu.with_memory_space_constraint(previous, pltpu.HBM)]
+    hbm = pl.BlockSpec(memory_space=pltpu.HBM)
     return pl.pallas_call(
         functools.partial(finish_kernel, first=first, qlength=qlength),
         in_specs=[SMEM, SMEM, VMEM, VMEM, VMEM] + [hbm] * len(extra),
         out_specs=hbm,
-        out_shape=jax.ShapeDtypeStruct((rows, columns), BF16),
+        out_shape=pltpu.HBM((rows, columns), BF16),
         scratch_shapes=[pltpu.VMEM((number, qlength, columns), BF16), pltpu.SemaphoreType.DMA((number,))],
         input_output_aliases={5: 0} if extra else {},
         compiler_params=pltpu.CompilerParams(vmem_limit_bytes=16 << 20),
@@ -361,8 +363,10 @@
         shifts = {2: 1, 3: -1}
         for s, shift in shifts.items():
             arrived[s] = lax.ppermute(packed[s], "replica", by_shift(shift, replicas))
-        keys, values_t = split(pairs, context, slots)
         for s in range(4):
+            if s < 2:
+                previous, after = ((keys, values_t), returned[0]) if s else (None, None)
+                keys, values_t = split(pairs, context, slots, s, previous, after)
             returned[s] = attend(table, 8 + s, arrived[s], keys, values_t, heads, qlength)
             if s in shifts:
                 returned[s] = lax.ppermute(returned[s], "replica", by_shift(-shifts[s], replicas))

time: 174 us -> 175 us (level)
  Pallas kernels: 102 us -> 105 us
  waiting for transfers between devices: 44.1 us -> 42.3 us
    pallas_call x4, Pallas kernels: 5.25 us -> 7.83 us  [finish(): pl.pallas_call(functools.partial(finish_kernel, first=first, qlength=qlen...]
    ppermute x4, waiting for transfers between devices: 31.4 us -> 29.4 us  [project_out(): far = lax.ppermute(chip_sum, 'tensor', other_chip)]
    unnamed x22 -> x26, local copies, waits for them, and re-layouts: 5.82 us -> 4.51 us
    pallas_call x1 -> x2, Pallas kernels: 3.4 us -> 4.35 us  [split(): pl.pallas_call(functools.partial(split_kernel, slot=slot), in_specs=[hbm]...]
  transfers between devices with their start and end apart: 17 -> 17, of which waited for: 6 -> 6; matrix products, arithmetic and copies ran while one was open for 2% -> 2% of each run, Pallas kernels for 56% -> 58%
where the time goes in v1:
time: 175 us
  Pallas kernels  105 us (60%)
  waiting for transfers between devices  42.3 us (24%)
  starting transfers between devices  17.1 us (10%)
  local copies, waits for them, and re-layouts  5.16 us (3%)
  other arithmetic  2.86 us (2%)
  between operations  1.8 us (1%)
    pallas_call x4, Pallas kernels, attend(): pl.pallas_call(functools.partial(attend_kernel, entry=entry, heads=heads,...  75.1 us
    ppermute x4, waiting for transfers between devices, project_out(): far = lax.ppermute(chip_sum, 'tensor', other_chip)  29.4 us
    pallas_call x8, Pallas kernels, project(): pl.pallas_call(functools.partial(project_kernel, flip=flip, tile=tile), i...  16.1 us
    ppermute x2, waiting for transfers between devices, on_device(): lax.ppermute(returned[s], 'replica', by_shift(-shifts[s], replicas))  12.8 us
    pallas_call x4, Pallas kernels, finish(): pl.pallas_call(functools.partial(finish_kernel, first=first, qlength=qlen...  7.83 us
    ppermute x4, starting transfers between devices, project_out(): far = lax.ppermute(chip_sum, 'tensor', other_chip)  5.06 us
    unnamed x26, local copies, waits for them, and re-layouts  4.51 us
    pallas_call x2, Pallas kernels, split(): pl.pallas_call(functools.partial(split_kernel, slot=slot), in_specs=[hbm]...  4.35 us
  transfers between devices with their start and end apart: 17, of which 6 were waited for; matrix products, arithmetic and copies ran while one was open for 2% of the time, Pallas kernels for 58%

profile of v1, /device:TPU:0, one launch (start us, length us, event | category | flops | bytes accessed | tf_op | source)
XLA Modules:
  0.0 174.6 jit_solution(677151593284164180)
XLA Ops:
  0.0 2.0 %pack.3 = (s32[13]{0:T(128)S(1)}, bf16[2,640,128]{2,1,0:T(8,128)(2,1)S(1)}, bf16[2,640,128]{2,1,0:T(8,128)(2,1)S(1)}, bf16[2,640,128]{2,1,0:T(8,128)(2,1)S(1)}, bf16[2,640,128]{2,1,0:T(8,128)(2,1)S(1)}) custom-call(s32[2,4]{1,0:T(2,128)} %bitcast.14, s32[1,8]{1,0:T(1,128)} %bitcast.16, bf16[512,1024]{1,0:T(8,128)(2,1)} %q_hbm.1, bf16[1024,128]{1,0:T(8,128)(2,1)} %bitcast.12), custom_call_target="tpu_custom_call" | custom-call | bytes 4194304 | tf_op jit(solution)/shard_map/pack/pallas_call | solution.py:103
  2.7 3.0 %collective-permute-start.9 = (s32[]{:T(128)}, s32[]{:T(128)}, u32[]{:S(2)}, u32[]{:S(2)}) collective-permute-start(s32[]{:T(128)} %bitcast.3), channel_id=1, source_target_pairs={{0,16},{16,0},{1,17},{17,1},{2,18},{18,2},{3,19},{19,3},{4,20},{20... | collective-permute-start | bytes 20 | tf_op jit(solution)/shard_map/ppermute | solution.py:378
  5.7 3.6 %collective-permute-start.10 = (bf16[2,640,128]{2,1,0:T(8,128)(2,1)S(1)}, bf16[2,640,128]{2,1,0:T(8,128)(2,1)S(1)}, u32[]{:S(2)}, u32[]{:S(2)}) collective-permute-start(bf16[2,640,128]{2,1,0:T(8,128)(2,1)S(1)} %get-tuple-element.67), channel_id=1, source_target_pairs={{0,12},{4,0},{8,4},{12,8},{1,13},{5,1},{9,5},{13,9},{2,14},{6,2},{... | collective-permute-start | bytes 983048 | tf_op jit(solution)/shard_map/ppermute | solution.py:365
  9.3 2.1 %split.4 = (bf16[2,4096,128]{2,1,0:T(8,128)(2,1)S(1)}, bf16[2,144,4096]{2,1,0:T(8,128)(2,1)S(1)}) custom-call(bf16[16384,128]{1,0:T(8,128)(2,1)} %bitcast.9), custom_call_target="tpu_custom_call" | custom-call | bytes 4194304 | tf_op jit(solution)/shard_map/split/pallas_call | solution.py:150
  11.4 18.7 %attend.6.refs_2_.a_ref = bf16[128,1024]{1,0:T(8,128)(2,1)S(1)} custom-call(s32[13]{0:T(128)S(1)} %get-tuple-element.66.table_ref, bf16[2,640,128]{2,1,0:T(8,128)(2,1)S(1)} %get-tuple-element.70.x_ref, bf16[2,4096,128]{2,1,0:T(8,128)(2,1)S(1)} %get-tuple-element.68.keys_ref.refs_0_, bf16[2,144,4096]{2,1,0:T(8,128)(2,1)S(1)} %get-tuple-element.69.values_ref.refs_1_), custom_call_target="tpu_custom_call" | custom-call | flops 4294967296 | bytes 4194304 | tf_op jit(solution)/shard_map/attend/pallas_call | solution.py:231
  30.1 2.3 %split.5 = (bf16[2,4096,128]{2,1,0:T(8,128)(2,1)S(1)}, bf16[2,144,4096]{2,1,0:T(8,128)(2,1)S(1)}) custom-call(bf16[16384,128]{1,0:T(8,128)(2,1)} %bitcast.10, bf16[2,4096,128]{2,1,0:T(8,128)(2,1)S(1)} %get-tuple-element.68.keys_ref.refs_0_, ...), custom_call_target="tpu_custom_call", output_to_operand_aliasing={{0}: (1, {}), {1}: (2, {})} | custom-call | bytes 4194304 | tf_op jit(solution)/shard_map/split/pallas_call | solution.py:150
  32.4 18.7 %attend.9.a_ref = bf16[128,1024]{1,0:T(8,128)(2,1)S(1)} custom-call(s32[13]{0:T(128)S(1)} %get-tuple-element.66.table_ref, bf16[2,640,128]{2,1,0:T(8,128)(2,1)S(1)} %get-tuple-element.82.x_ref, bf16[2,4096,128]{2,1,0:T(8,128)(2,1)S(1)} %get-tuple-element.71.keys_ref, bf16[2,144,4096]{2,1,0:T(8,128)(2,1)S(1)} %get-tuple-element.72.values_ref), custom_call_target="tpu_custom_call" | custom-call | flops 4294967296 | bytes 4194304 | tf_op jit(solution)/shard_map/attend/pallas_call | solution.py:231
  51.2 1.8 %project.17 = (bf16[128,2048]{1,0:T(8,128)(2,1)S(1)}, f32[128,2048]{1,0:T(8,128)S(1)}) custom-call(bf16[128,1024]{1,0:T(8,128)(2,1)S(1)} %attend.9.a_ref, bf16[1024,8192]{1,0:T(8,128)(2,1)S(1)} %bitcast.6), custom_call_target="tpu_custom_call" | custom-call | flops 1073741824 | bytes 8388608 | tf_op jit(solution)/shard_map/project/pallas_call | solution.py:264
  53.1 1.9 %project.16 = (bf16[128,2048]{1,0:T(8,128)(2,1)S(1)}, f32[128,2048]{1,0:T(8,128)S(1)}) custom-call(bf16[128,1024]{1,0:T(8,128)(2,1)S(1)} %attend.9.a_ref, bf16[1024,8192]{1,0:T(8,128)(2,1)S(1)} %bitcast.6), custom_call_target="tpu_custom_call" | custom-call | flops 1073741824 | bytes 8388608 | tf_op jit(solution)/shard_map/project/pallas_call | solution.py:264
  57.4 1.8 %project.18 = (bf16[128,2048]{1,0:T(8,128)(2,1)S(1)}, f32[128,2048]{1,0:T(8,128)S(1)}) custom-call(bf16[128,1024]{1,0:T(8,128)(2,1)S(1)} %attend.6.refs_2_.a_ref, bf16[1024,8192]{1,0:T(8,128)(2,1)S(1)} %bitcast.6), custom_call_target="tpu_custom_call" | custom-call | flops 1073741824 | bytes 8388608 | tf_op jit(solution)/shard_map/project/pallas_call | solution.py:264
  59.3 18.8 %attend.8 = bf16[128,1024]{1,0:T(8,128)(2,1)S(1)} custom-call(s32[13]{0:T(128)S(1)} %get-tuple-element.66.table_ref, bf16[2,640,128]{2,1,0:T(8,128)(2,1)S(1)} %collective-permute-done.15.x_ref, bf16[2,4096,128]{2,1,0:T(8,128)(2,1)S(1)} %get-tuple-element.71.keys_ref, bf16[2,144,4096]{2,1,0:T(8,128)(2,1)S(1)} %get-tuple-element.72.values_ref), custom_call_target="tpu_custom_call" | custom-call | flops 4294967296 | bytes 4194304 | tf_op jit(solution)/shard_map/attend/pallas_call | solution.py:231
  78.6 18.9 %attend.7 = bf16[128,1024]{1,0:T(8,128)(2,1)S(1)} custom-call(s32[13]{0:T(128)S(1)} %get-tuple-element.66.table_ref, bf16[2,640,128]{2,1,0:T(8,128)(2,1)S(1)} %collective-permute-done.10.x_ref, bf16[2,4096,128]{2,1,0:T(8,128)(2,1)S(1)} %get-tuple-element.71.keys_ref, bf16[2,144,4096]{2,1,0:T(8,128)(2,1)S(1)} %get-tuple-element.72.values_ref), custom_call_target="tpu_custom_call" | custom-call | flops 4294967296 | bytes 4194304 | tf_op jit(solution)/shard_map/attend/pallas_call | solution.py:231
  97.5 3.9 %collective-permute-start.16 = (bf16[128,1024]{1,0:T(8,128)(2,1)S(1)}, bf16[128,1024]{1,0:T(8,128)(2,1)S(1)}, u32[]{:S(2)}, u32[]{:S(2)}) collective-permute-start(bf16[128,1024]{1,0:T(8,128)(2,1)S(1)} %attend.8), channel_id=1, source_target_pairs={{0,12},{4,0},{8,4},{12,8},{1,13},{5,1},{9,5},{13,9},{2,14},{6,2},{... | collective-permute-start | bytes 786440 | tf_op jit(solution)/shard_map/ppermute | solution.py:372
  102.3 5.3 %collective-permute-done.16.a_ref = bf16[128,1024]{1,0:T(8,128)(2,1)S(1)} collective-permute-done((bf16[128,1024]{1,0:T(8,128)(2,1)S(1)}, bf16[128,1024]{1,0:T(8,128)(2,1)S(1)}, u32[]{:S(2)}, u32[]{:S(2)}) %collective-permute-start.16) | collective-permute-done | bytes 262176 | tf_op jit(solution)/shard_map/ppermute | solution.py:372
  109.7 7.5 %collective-permute-done.11.a_ref = bf16[128,1024]{1,0:T(8,128)(2,1)S(1)} collective-permute-done((bf16[128,1024]{1,0:T(8,128)(2,1)S(1)}, bf16[128,1024]{1,0:T(8,128)(2,1)S(1)}, u32[]{:S(2)}, u32[]{:S(2)}) %collective-permute-start.11) | collective-permute-done | bytes 262176 | tf_op jit(solution)/shard_map/ppermute | solution.py:372
  119.1 2.5 %project.14 = (bf16[128,2048]{1,0:T(8,128)(2,1)}, f32[128,2048]{1,0:T(8,128)S(1)}) custom-call(bf16[128,1024]{1,0:T(8,128)(2,1)S(1)} %collective-permute-done.16.a_ref, bf16[1024,8192]{1,0:T(8,128)(2,1)S(1)} %bitcast.6), custom_call_target="tpu_custom_call" | custom-call | flops 1073741824 | bytes 8388608 | tf_op jit(solution)/shard_map/project/pallas_call | solution.py:264
  121.6 2.5 %project.12 = (bf16[128,2048]{1,0:T(8,128)(2,1)}, f32[128,2048]{1,0:T(8,128)S(1)}) custom-call(bf16[128,1024]{1,0:T(8,128)(2,1)S(1)} %collective-permute-done.11.a_ref, bf16[1024,8192]{1,0:T(8,128)(2,1)S(1)} %bitcast.6), custom_call_target="tpu_custom_call" | custom-call | flops 1073741824 | bytes 8388608 | tf_op jit(solution)/shard_map/project/pallas_call | solution.py:264
  131.3 7.6 %collective-permute-done.25.far_ref = bf16[128,2048]{1,0:T(8,128)(2,1)S(1)} collective-permute-done((bf16[128,2048]{1,0:T(8,128)(2,1)S(1)}, bf16[128,2048]{1,0:T(8,128)(2,1)S(1)}, u32[]{:S(2)}, u32[]{:S(2)}) %collective-permute-start.25) | collective-permute-done | bytes 524320 | tf_op jit(solution)/shard_map/ppermute | solution.py:330
  146.2 4.1 %collective-permute-done.22.far_ref = bf16[128,2048]{1,0:T(8,128)(2,1)} collective-permute-done((bf16[128,2048]{1,0:T(8,128)(2,1)}, bf16[128,2048]{1,0:T(8,128)(2,1)}, u32[]{:S(2)}, u32[]{:S(2)}) %collective-permute-start.22) | collective-permute-done | bytes 524320 | tf_op jit(solution)/shard_map/ppermute | solution.py:330
  150.3 2.1 %finish.7.refs_0_ = bf16[512,2048]{1,0:T(8,128)(2,1)} custom-call(s32[13]{0:T(128)S(1)} %get-tuple-element.66.table_ref, s32[1,8]{1,0:T(1,128)S(1)} %copy-done.8, f32[128,2048]{1,0:T(8,128)S(1)} %get-tuple-element.83.kept_ref, bf16[128,2048]{1,0:T(8,128)(2,1)S(1)} %copy-done.7, ...), custom_call_target="tpu_custom_call", output_to_operand_aliasing={{}: (5, {})} | custom-call | bytes 5242880 | tf_op jit(solution)/shard_map/finish/pallas_call | solution.py:300
  152.4 9.1 %collective-permute-done.19.far_ref = bf16[128,2048]{1,0:T(8,128)(2,1)} collective-permute-done((bf16[128,2048]{1,0:T(8,128)(2,1)}, bf16[128,2048]{1,0:T(8,128)(2,1)}, u32[]{:S(2)}, u32[]{:S(2)}) %collective-permute-start.19) | collective-permute-done | bytes 524320 | tf_op jit(solution)/shard_map/ppermute | solution.py:330
  161.5 2.1 %finish.8.refs_0_ = bf16[512,2048]{1,0:T(8,128)(2,1)} custom-call(s32[13]{0:T(128)S(1)} %get-tuple-element.66.table_ref, s32[1,8]{1,0:T(1,128)S(1)} %copy-done.8, f32[128,2048]{1,0:T(8,128)S(1)} %copy-done.1, bf16[128,2048]{1,0:T(8,128)(2,1)} %collective-permute-done.17.core_ref, ...), custom_call_target="tpu_custom_call", output_to_operand_aliasing={{}: (5, {})} | custom-call | bytes 5242880 | tf_op jit(solution)/shard_map/finish/pallas_call | solution.py:300
  163.7 8.6 %collective-permute-done.14.far_ref = bf16[128,2048]{1,0:T(8,128)(2,1)} collective-permute-done((bf16[128,2048]{1,0:T(8,128)(2,1)}, bf16[128,2048]{1,0:T(8,128)(2,1)}, u32[]{:S(2)}, u32[]{:S(2)}) %collective-permute-start.14) | collective-permute-done | bytes 524320 | tf_op jit(solution)/shard_map/ppermute | solution.py:330
  172.3 2.1 %finish.9 = bf16[512,2048]{1,0:T(8,128)(2,1)} custom-call(s32[13]{0:T(128)S(1)} %get-tuple-element.66.table_ref, s32[1,8]{1,0:T(1,128)S(1)} %copy-done.8, f32[128,2048]{1,0:T(8,128)S(1)} %get-tuple-element.73.kept_ref, bf16[128,2048]{1,0:T(8,128)(2,1)} %collective-permute-done.12.core_ref, ...), custom_call_target="tpu_custom_call", output_to_operand_aliasing={{}: (5, {})} | custom-call | bytes 5242880 | tf_op jit(solution)/shard_map/finish/pallas_call | solution.py:300
  (62 shorter events, 21.7 us)
Async XLA Ops:
  2.7 125.3 %collective-permute-start.9 = (s32[]{:T(128)}, s32[]{:T(128)}, u32[]{:S(2)}, u32[]{:S(2)}) collective-permute-start(s32[]{:T(128)} %bitcast.3), channel_id=1, source_target_pairs={{0,16},{16,0},{1,17},{17,1},{2,18},{18,2},{3,19},{19,3},{4,20},{20... | collective-permute-start | bytes 20 | tf_op jit(solution)/shard_map/ppermute | solution.py:378
  5.7 72.5 %collective-permute-start.10 = (bf16[2,640,128]{2,1,0:T(8,128)(2,1)S(1)}, bf16[2,640,128]{2,1,0:T(8,128)(2,1)S(1)}, u32[]{:S(2)}, u32[]{:S(2)}) collective-permute-start(bf16[2,640,128]{2,1,0:T(8,128)(2,1)S(1)} %get-tuple-element.67), channel_id=1, source_target_pairs={{0,12},{4,0},{8,4},{12,8},{1,13},{5,1},{9,5},{13,9},{2,14},{6,2},{... | collective-permute-start | bytes 983048 | tf_op jit(solution)/shard_map/ppermute | solution.py:365
  9.3 50.0 %collective-permute-start.15 = (bf16[2,640,128]{2,1,0:T(8,128)(2,1)S(1)}, bf16[2,640,128]{2,1,0:T(8,128)(2,1)S(1)}, u32[]{:S(2)}, u32[]{:S(2)}) collective-permute-start(bf16[2,640,128]{2,1,0:T(8,128)(2,1)S(1)} %get-tuple-element.77), channel_id=1, source_target_pairs={{0,4},{4,8},{8,12},{12,0},{1,5},{5,9},{9,13},{13,1},{2,6},{6,10},{... | collective-permute-start | bytes 983048 | tf_op jit(solution)/shard_map/ppermute | solution.py:365
  11.4 39.8 %slice-start = ((s8[16777216]{0:T(1024)(128)(4,1)}), s8[4194304]{0:T(1024)(128)(4,1)S(1)}, s32[]{:S(2)}) async-start(s8[16777216]{0:T(1024)(128)(4,1)} %bitcast.5), calls=%async_computation | async-start | bytes 8388608
  11.4 39.8 %slice-start.1 = ((s8[16777216]{0:T(1024)(128)(4,1)}), s8[4194304]{0:T(1024)(128)(4,1)S(1)}, s32[]{:S(2)}) async-start(s8[16777216]{0:T(1024)(128)(4,1)} %bitcast.5), calls=%async_computation.1 | async-start | bytes 8388608
  30.1 21.0 %slice-start.2 = ((s8[16777216]{0:T(1024)(128)(4,1)}), s8[4194304]{0:T(1024)(128)(4,1)S(1)}, s32[]{:S(2)}) async-start(s8[16777216]{0:T(1024)(128)(4,1)} %bitcast.5), calls=%async_computation.2 | async-start | bytes 8388608
  32.4 18.8 %slice-start.3 = ((s8[16777216]{0:T(1024)(128)(4,1)}), s8[4194304]{0:T(1024)(128)(4,1)S(1)}, s32[]{:S(2)}) async-start(s8[16777216]{0:T(1024)(128)(4,1)} %bitcast.5), calls=%async_computation.3 | async-start | bytes 8388608
  53.0 44.5 %collective-permute-start.21 = (bf16[128,2048]{1,0:T(8,128)(2,1)S(1)}, bf16[128,2048]{1,0:T(8,128)(2,1)S(1)}, u32[]{:S(2)}, u32[]{:S(2)}) collective-permute-start(bf16[128,2048]{1,0:T(8,128)(2,1)S(1)} %get-tuple-element.86), channel_id=1, source_target_pairs={{0,1},{1,0},{2,3},{3,2},{4,5},{5,4},{6,7},{7,6},{8,9},{9,8},{10,11... | collective-permute-start | bytes 1572872 | tf_op jit(solution)/shard_map/ppermute | solution.py:326
  55.0 73.0 %collective-permute-start.20 = (bf16[128,2048]{1,0:T(8,128)(2,1)S(1)}, bf16[128,2048]{1,0:T(8,128)(2,1)S(1)}, u32[]{:S(2)}, u32[]{:S(2)}) collective-permute-start(bf16[128,2048]{1,0:T(8,128)(2,1)S(1)} %get-tuple-element.84), channel_id=1, source_target_pairs={{0,1},{1,0},{2,3},{3,2},{4,5},{5,4},{6,7},{7,6},{8,9},{9,8},{10,11... | collective-permute-start | bytes 1572872 | tf_op jit(solution)/shard_map/ppermute | solution.py:328
  59.2 50.2 %collective-permute-start.24 = (bf16[128,2048]{1,0:T(8,128)(2,1)S(1)}, bf16[128,2048]{1,0:T(8,128)(2,1)S(1)}, u32[]{:S(2)}, u32[]{:S(2)}) collective-permute-start(bf16[128,2048]{1,0:T(8,128)(2,1)S(1)} %get-tuple-element.90), channel_id=1, source_target_pairs={{0,1},{1,0},{2,3},{3,2},{4,5},{5,4},{6,7},{7,6},{8,9},{9,8},{10,11... | collective-permute-start | bytes 1572872 | tf_op jit(solution)/shard_map/ppermute | solution.py:326
  78.1 52.2 %collective-permute-start.23 = (bf16[128,2048]{1,0:T(8,128)(2,1)S(1)}, bf16[128,2048]{1,0:T(8,128)(2,1)S(1)}, u32[]{:S(2)}, u32[]{:S(2)}) collective-permute-start(bf16[128,2048]{1,0:T(8,128)(2,1)S(1)} %get-tuple-element.88), channel_id=1, source_target_pairs={{0,1},{1,0},{2,3},{3,2},{4,5},{5,4},{6,7},{7,6},{8,9},{9,8},{10,11... | collective-permute-start | bytes 1572872 | tf_op jit(solution)/shard_map/ppermute | solution.py:328
  97.5 10.1 %collective-permute-start.16 = (bf16[128,1024]{1,0:T(8,128)(2,1)S(1)}, bf16[128,1024]{1,0:T(8,128)(2,1)S(1)}, u32[]{:S(2)}, u32[]{:S(2)}) collective-permute-start(bf16[128,1024]{1,0:T(8,128)(2,1)S(1)} %attend.8), channel_id=1, source_target_pairs={{0,12},{4,0},{8,4},{12,8},{1,13},{5,1},{9,5},{13,9},{2,14},{6,2},{... | collective-permute-start | bytes 786440 | tf_op jit(solution)/shard_map/ppermute | solution.py:372
  107.6 9.6 %collective-permute-start.11 = (bf16[128,1024]{1,0:T(8,128)(2,1)S(1)}, bf16[128,1024]{1,0:T(8,128)(2,1)S(1)}, u32[]{:S(2)}, u32[]{:S(2)}) collective-permute-start(bf16[128,1024]{1,0:T(8,128)(2,1)S(1)} %attend.7), channel_id=1, source_target_pairs={{0,4},{4,8},{8,12},{12,0},{1,5},{5,9},{9,13},{13,1},{2,6},{6,10},{... | collective-permute-start | bytes 786440 | tf_op jit(solution)/shard_map/ppermute | solution.py:372
  109.5 14.7 %collective-permute-start.18 = (bf16[128,2048]{1,0:T(8,128)(2,1)S(1)}, bf16[128,2048]{1,0:T(8,128)(2,1)S(1)}, u32[]{:S(2)}, u32[]{:S(2)}) collective-permute-start(bf16[128,2048]{1,0:T(8,128)(2,1)S(1)} %get-tuple-element.81), channel_id=1, source_target_pairs={{0,1},{1,0},{2,3},{3,2},{4,5},{5,4},{6,7},{7,6},{8,9},{9,8},{10,11... | collective-permute-start | bytes 1572872 | tf_op jit(solution)/shard_map/ppermute | solution.py:326
  119.0 7.6 %collective-permute-start.13 = (bf16[128,2048]{1,0:T(8,128)(2,1)S(1)}, bf16[128,2048]{1,0:T(8,128)(2,1)S(1)}, u32[]{:S(2)}, u32[]{:S(2)}) collective-permute-start(bf16[128,2048]{1,0:T(8,128)(2,1)S(1)} %get-tuple-element.76), channel_id=1, source_target_pairs={{0,1},{1,0},{2,3},{3,2},{4,5},{5,4},{6,7},{7,6},{8,9},{9,8},{10,11... | collective-permute-start | bytes 1572872 | tf_op jit(solution)/shard_map/ppermute | solution.py:326
  124.1 14.8 %collective-permute-start.25 = (bf16[128,2048]{1,0:T(8,128)(2,1)S(1)}, bf16[128,2048]{1,0:T(8,128)(2,1)S(1)}, u32[]{:S(2)}, u32[]{:S(2)}) collective-permute-start(bf16[128,2048]{1,0:T(8,128)(2,1)S(1)} %add_convert_fusion.1), channel_id=1, source_target_pairs={{0,2},{1,3},{2,0},{3,1},{4,6},{5,7},{6,4},{7,5},{8,10},{9,11},{10,... | collective-permute-start | bytes 1572872 | tf_op jit(solution)/shard_map/ppermute | solution.py:330
  125.7 16.9 %copy-start.8 = (s32[1,8]{1,0:T(1,128)S(1)}, s32[1,8]{1,0:T(1,128)}, u32[]{:S(2)}) copy-start(s32[1,8]{1,0:T(1,128)} %counts_ref.7) | copy-start | bytes 100
  126.6 23.7 %collective-permute-start.22 = (bf16[128,2048]{1,0:T(8,128)(2,1)}, bf16[128,2048]{1,0:T(8,128)(2,1)}, u32[]{:S(2)}, u32[]{:S(2)}) collective-permute-start(bf16[128,2048]{1,0:T(8,128)(2,1)} %add_convert_fusion.2), channel_id=1, source_target_pairs={{0,2},{1,3},{2,0},{3,1},{4,6},{5,7},{6,4},{7,5},{8,10},{9,11},{10,... | collective-permute-start | bytes 1572872 | tf_op jit(solution)/shard_map/ppermute | solution.py:330
  128.0 24.4 %collective-permute-start.17 = (bf16[128,2048]{1,0:T(8,128)(2,1)}, bf16[128,2048]{1,0:T(8,128)(2,1)}, u32[]{:S(2)}, u32[]{:S(2)}) collective-permute-start(bf16[128,2048]{1,0:T(8,128)(2,1)} %get-tuple-element.79), channel_id=1, source_target_pairs={{0,1},{1,0},{2,3},{3,2},{4,5},{5,4},{6,7},{7,6},{8,9},{9,8},{10,11... | collective-permute-start | bytes 1572872 | tf_op jit(solution)/shard_map/ppermute | solution.py:328
  128.8 32.7 %collective-permute-start.19 = (bf16[128,2048]{1,0:T(8,128)(2,1)}, bf16[128,2048]{1,0:T(8,128)(2,1)}, u32[]{:S(2)}, u32[]{:S(2)}) collective-permute-start(bf16[128,2048]{1,0:T(8,128)(2,1)} %add_convert_fusion.3), channel_id=1, source_target_pairs={{0,2},{1,3},{2,0},{3,1},{4,6},{5,7},{6,4},{7,5},{8,10},{9,11},{10,... | collective-permute-start | bytes 1572872 | tf_op jit(solution)/shard_map/ppermute | solution.py:330
  131.1 32.6 %collective-permute-start.12 = (bf16[128,2048]{1,0:T(8,128)(2,1)}, bf16[128,2048]{1,0:T(8,128)(2,1)}, u32[]{:S(2)}, u32[]{:S(2)}) collective-permute-start(bf16[128,2048]{1,0:T(8,128)(2,1)} %get-tuple-element.74), channel_id=1, source_target_pairs={{0,1},{1,0},{2,3},{3,2},{4,5},{5,4},{6,7},{7,6},{8,9},{9,8},{10,11... | collective-permute-start | bytes 1572872 | tf_op jit(solution)/shard_map/ppermute | solution.py:328
  139.8 32.5 %collective-permute-start.14 = (bf16[128,2048]{1,0:T(8,128)(2,1)}, bf16[128,2048]{1,0:T(8,128)(2,1)}, u32[]{:S(2)}, u32[]{:S(2)}) collective-permute-start(bf16[128,2048]{1,0:T(8,128)(2,1)} %add_convert_fusion.4), channel_id=1, source_target_pairs={{0,2},{1,3},{2,0},{3,1},{4,6},{5,7},{6,4},{7,5},{8,10},{9,11},{10,... | collective-permute-start | bytes 1572872 | tf_op jit(solution)/shard_map/ppermute | solution.py:330
  144.7 5.6 %copy-start.7 = (bf16[128,2048]{1,0:T(8,128)(2,1)S(1)}, bf16[128,2048]{1,0:T(8,128)(2,1)}, u32[]{:S(2)}) copy-start(bf16[128,2048]{1,0:T(8,128)(2,1)} %copy-done.6) | copy-start | bytes 1572868
  150.3 11.2 %copy-start.1 = (f32[128,2048]{1,0:T(8,128)S(1)}, f32[128,2048]{1,0:T(8,128)}, u32[]{:S(2)}) copy-start(f32[128,2048]{1,0:T(8,128)} %copy-done) | copy-start | bytes 3145732
  (6 other events, 7.0 us)

commit v2 on v1

--- a/solution.py
+++ b/solution.py
@@ -18,7 +18,7 @@
 SMEM = pl.BlockSpec(memory_space=pltpu.SMEM)
 
 
-def pack_kernel(stored_hbm, ids_hbm, q_hbm, own_hbm, table_ref, *refs, route, heads, qlength):
+def pack_kernel(stored_hbm, ids_hbm, q_hbm, own_hbm, table_ref, failed_ref, *refs, route, heads, qlength):
     number = len(refs) - 5
     out_refs = refs[:number]
     stored_ref, ids_ref, q_ref, own_ref, sems = refs[number:]
@@ -31,7 +31,7 @@
     for copy in copies[:2]:
         copy.wait()
     places = []
-    for s, haystack in enumerate(route(stored_ref, table_ref)):
+    for s, haystack in enumerate(route(stored_ref, table_ref, failed_ref)):
         count = jnp.int32(0)
         found = [jnp.int32(-1)] * CAP
         for i in range(questions):
@@ -53,14 +53,13 @@
             out_ref[j, heads * qlength :, :] = own
 
 
-def route_first(replicas, stored_ref, table_ref):
+def route_first(replicas, stored_ref, table_ref, failed_ref):
+    failed_ref[0] = jnp.int32(0)
     me = lax.axis_index("replica")
-    for s in range(replicas):
-        table_ref[replicas * CAP + s] = jnp.int32(0)
     return [stored_ref[0, lax.rem(me + s, replicas)] for s in range(replicas)]
 
 
-def route_near(stored_ref, table_ref):
+def route_near(stored_ref, table_ref, failed_ref):
     me = lax.axis_index("replica")
 
     def held(replica):
@@ -85,11 +84,9 @@
     failed = jnp.int32(0)
     for _, _, done in plans:
         failed = jnp.where(done, failed, 1)
-    table_ref[8] = jnp.int32(0)
-    table_ref[9] = jnp.int32(1)
     table_ref[10] = plans[3][0][0]
     table_ref[11] = plans[1][0][1]
-    table_ref[12] = failed
+    failed_ref[0] = failed
     return held(me) + plans[0][1]
 
 
@@ -103,8 +100,8 @@
     out = pl.pallas_call(
         functools.partial(pack_kernel, route=route, heads=heads, qlength=qlength),
         in_specs=[pl.BlockSpec(memory_space=pltpu.HBM)] * 4,
-        out_specs=[SMEM] + [VMEM] * phases,
-        out_shape=[jax.ShapeDtypeStruct((phases * (CAP + 1) + 1,), jnp.int32)]
+        out_specs=[SMEM, SMEM] + [VMEM] * phases,
+        out_shape=[jax.ShapeDtypeStruct((size,), jnp.int32) for size in (phases * (CAP + 1), 1)]
         + [jax.ShapeDtypeStruct((CAP, rows, head_size), BF16)] * phases,
         scratch_shapes=[
             pltpu.SMEM(stored.shape, jnp.int32),
@@ -117,7 +114,7 @@
         cost_estimate=pl.CostEstimate(flops=0, bytes_accessed=4 << 20, transcendentals=0),
         name="pack",
     )(*arguments)
-    return out[0], out[1:]
+    return out[0], out[1], out[2:]
 
 
 def split_kernel(x_ref, *refs, slot):
@@ -168,7 +165,7 @@
 
 
 def attend_kernel(table_ref, x_ref, keys_ref, values_ref, o_ref, *, entry, heads, qlength, chunk):
-    slot = table_ref[entry]
+    slot = entry if isinstance(entry, int) else table_ref[entry[0]]
     k_ref, vt_ref = keys_ref.at[slot], values_ref.at[slot]
     context, head_size = k_ref.shape
     scale = LOG2E / math.sqrt(head_size)
@@ -243,14 +240,14 @@
     )(table, x, keys, values_t)
 
 
-def project_kernel(a_ref, w_ref, give_ref, keep_ref, *, flip, tile):
-    columns = keep_ref.shape[1]
+def project_kernel(a_ref, w_ref, *out_refs, flips, tile):
+    columns = out_refs[0].shape[1]
     me = lax.axis_index("tensor")
 
     def one(i, carry):
         out = pl.ds(pl.multiple_of(i * tile, tile), tile)
-        for ref, block in ((give_ref, me ^ flip ^ 1), (keep_ref, me ^ flip)):
-            source = pl.ds(pl.multiple_of(block * columns + i * tile, tile), tile)
+        for ref, flip in zip(out_refs, flips):
+            source = pl.ds(pl.multiple_of((me ^ flip) * columns + i * tile, tile), tile)
             product = jnp.dot(a_ref[...], w_ref[:, source], preferred_element_type=F32)
             ref[:, out] = product.astype(ref.dtype)
         return carry
@@ -258,34 +255,45 @@
     lax.fori_loop(0, columns // tile, one, 0)
 
 
-def project(rows, weight, flip, shares, tile):
+def project(rows, weight, shares, tile, flips, types):
     number, depth = rows.shape
     columns = weight.shape[1] // shares
     return pl.pallas_call(
-        functools.partial(project_kernel, flip=flip, tile=tile),
+        functools.partial(project_kernel, flips=flips, tile=tile),
         in_specs=[VMEM, VMEM],
-        out_specs=[VMEM, VMEM],
-        out_shape=[
-            jax.ShapeDtypeStruct((number, columns), BF16),
-            jax.ShapeDtypeStruct((number, columns), F32),
-        ],
+        out_specs=[VMEM] * len(flips),
+        out_shape=[jax.ShapeDtypeStruct((number, columns), kind) for kind in types],
         compiler_params=pltpu.CompilerParams(vmem_limit_bytes=12 << 20),
         cost_estimate=pl.CostEstimate(
-            flops=4 * number * depth * columns, bytes_accessed=4 * depth * columns, transcendentals=0
+            flops=2 * len(flips) * number * depth * columns,
+            bytes_accessed=2 * len(flips) * depth * columns,
+            transcendentals=0,
         ),
         name="project",
     )(rows, weight)
 
 
-def finish_kernel(table_ref, counts_ref, kept_ref, core_ref, far_ref, *refs, first, qlength):
+def finish_kernel(table_ref, counts_ref, a_ref, w_ref, core_ref, far_ref, *refs, first, qlength, tile):
     o_ref, block_ref, sems = refs[-3:]
+    number, _, columns = block_ref.shape
+    me = lax.axis_index("tensor")
+    places = [jnp.maximum(table_ref[first + i], 0) for i in range(number)]
+    counts = [counts_ref[0, place] for place in places]
+    t = lax.broadcasted_iota(jnp.int32, (qlength, tile), 0)
+
+    def one(j, carry):
+        out = pl.ds(pl.multiple_of(j * tile, tile), tile)
+        source = pl.ds(pl.multiple_of(me * columns + j * tile, tile), tile)
+        total = jnp.dot(a_ref[...], w_ref[:, source], preferred_element_type=F32)
+        total = total + core_ref[:, out].astype(F32) + far_ref[:, out].astype(F32)
+        for i in range(number):
+            block = total[i * qlength : (i + 1) * qlength, :]
+            block_ref[i, :, out] = jnp.where(t < counts[i], block, 0.0).astype(BF16)
+        return carry
+
+    lax.fori_loop(0, columns // tile, one, 0)
     copies = []
-    for i in range(block_ref.shape[0]):
-        place = jnp.maximum(table_ref[first + i], 0)
-        rows = slice(i * qlength, (i + 1) * qlength)
-        total = kept_ref[rows, :] + core_ref[rows, :].astype(F32) + far_ref[rows, :].astype(F32)
-        t = lax.broadcasted_iota(jnp.int32, total.shape, 0)
-        block_ref[i] = jnp.where(t < counts_ref[0, place], total, 0.0).astype(BF16)
+    for i, place in enumerate(places):
         target = o_ref.at[pl.ds(pl.multiple_of(place * qlength, qlength), qlength), :]
         copies.append(pltpu.make_async_copy(block_ref.at[i], target, sems.at[i]))
         copies[-1].start()
@@ -293,21 +301,25 @@
         copy.wait()
 
 
-def finish(table, counts, kept, from_core, from_far, first, previous, rows, qlength):
-    number, columns = kept.shape[0] // qlength, kept.shape[1]
+def finish(table, counts, results, weight, from_core, from_far, first, previous, rows, qlength, tile):
+    number, columns = results.shape[0] // qlength, from_far.shape[1]
     extra = [] if previous is None else [pltpu.with_memory_space_constraint(previous, pltpu.HBM)]
     hbm = pl.BlockSpec(memory_space=pltpu.HBM)
     return pl.pallas_call(
-        functools.partial(finish_kernel, first=first, qlength=qlength),
-        in_specs=[SMEM, SMEM, VMEM, VMEM, VMEM] + [hbm] * len(extra),
+        functools.partial(finish_kernel, first=first, qlength=qlength, tile=tile),
+        in_specs=[SMEM, SMEM, VMEM, VMEM, VMEM, VMEM] + [hbm] * len(extra),
         out_specs=hbm,
         out_shape=pltpu.HBM((rows, columns), BF16),
         scratch_shapes=[pltpu.VMEM((number, qlength, columns), BF16), pltpu.SemaphoreType.DMA((number,))],
-        input_output_aliases={5: 0} if extra else {},
-        compiler_params=pltpu.CompilerParams(vmem_limit_bytes=16 << 20),
-        cost_estimate=pl.CostEstimate(flops=0, bytes_accessed=20 * number * qlength * columns, transcendentals=0),
+        input_output_aliases={6: 0} if extra else {},
+        compiler_params=pltpu.CompilerParams(vmem_limit_bytes=12 << 20),
+        cost_estimate=pl.CostEstimate(
+            flops=2 * results.shape[0] * results.shape[1] * columns,
+            bytes_accessed=2 * results.shape[1] * columns,
+            transcendentals=0,
+        ),
         name="finish",
-    )(table, counts, kept, from_core, from_far, *extra)
+    )(table, counts, results, weight, from_core, from_far, *extra)
 
 
 def by_shift(shift, replicas):
@@ -322,21 +334,21 @@
     other_core = [(i, i ^ 1) for i in range(shares)]
     other_chip = [(i, i ^ 2) for i in range(shares)]
     tile = 512
-    far_give, far_keep = project(results, weight, 2, shares, tile)
+    far_give, far_keep = project(results, weight, shares, tile, (3, 2), (BF16, F32))
     far_core = lax.ppermute(far_give, "tensor", other_core)
-    near_give, near_keep = project(results, weight, 0, shares, tile)
+    (near_give,) = project(results, weight, shares, tile, (1,), (BF16,))
     near_core = lax.ppermute(near_give, "tensor", other_core)
     chip_sum = (far_keep + far_core.astype(F32)).astype(BF16)
     far = lax.ppermute(chip_sum, "tensor", other_chip)
-    return finish(table, counts, near_keep, near_core, far, first, out, rows, qlength)
+    return finish(table, counts, results, weight, near_core, far, first, out, rows, qlength, tile)
 
 
 def answer_by_first_slots(queries, own, keys, values_t, stored, ids, heads, qlength):
     replicas = stored.shape[1]
     route = functools.partial(route_first, replicas)
-    table, packed = pack(stored, ids, queries, own, replicas, route)
+    table, _, packed = pack(stored, ids, queries, own, replicas, route)
     arrived = [packed[0]] + [lax.ppermute(packed[s], "replica", by_shift(s, replicas)) for s in range(1, replicas)]
-    result = attend(table, replicas * CAP, jnp.concatenate(arrived), keys, values_t, heads, qlength)
+    result = attend(table, 0, jnp.concatenate(arrived), keys, values_t, heads, qlength)
     parts = result.reshape(replicas, CAP * qlength, -1)
     returned = [parts[0]] + [lax.ppermute(parts[s], "replica", by_shift(-s, replicas)) for s in range(1, replicas)]
     return table, jnp.concatenate(returned)
@@ -358,7 +370,7 @@
     stored = stored.T
 
     if small_slice(groups, replicas, shares) and replicas * CAP == questions and slots == 2:
-        table, packed = pack(stored, ids, queries, own, 4, route_near)
+        table, failed, packed = pack(stored, ids, queries, own, 4, route_near)
         arrived, returned = dict(enumerate(packed)), {}
         shifts = {2: 1, 3: -1}
         for s, shift in shifts.items():
@@ -367,22 +379,19 @@
             if s < 2:
                 previous, after = ((keys, values_t), returned[0]) if s else (None, None)
                 keys, values_t = split(pairs, context, slots, s, previous, after)
-            returned[s] = attend(table, 8 + s, arrived[s], keys, values_t, heads, qlength)
+            returned[s] = attend(table, s if s < 2 else (8 + s,), arrived[s], keys, values_t, heads, qlength)
             if s in shifts:
                 returned[s] = lax.ppermute(returned[s], "replica", by_shift(-shifts[s], replicas))
         out = None
         for s in range(4):
             out = project_out(table, token_counts, returned[s], out_weight, shares, s * CAP, out, rows, qlength)
-        failed = table[12]
-        if groups == 2:
-            failed = failed + lax.ppermute(failed, "groups", [(0, 1), (1, 0)])
 
         def again():
             keys, values_t = split(pairs, context, 1)
             table, results = answer_by_first_slots(queries, own, keys, values_t, stored, ids, heads, qlength)
             return project_out(table, token_counts, results, out_weight, shares, 0, None, rows, qlength)
 
-        return lax.cond(failed > 0, again, lambda: out)
+        return lax.cond(failed[0] > 0, again, lambda: out)
 
     keys, values_t = split(pairs, context, 1)
     table, results = answer_by_first_slots(queries, own, keys, values_t, stored, ids, heads, qlength)

time: 175 us -> 151 us (0.86)
  waiting for transfers between devices: 42.3 us -> 29.4 us
  local copies, waits for them, and re-layouts: 5.16 us -> 0.01 us
  starting transfers between devices: 17.1 us -> 14.5 us
  other arithmetic: 2.86 us -> 0.49 us
    ppermute x2, waiting for transfers between devices: 12.8 us -> 5.61 us  [on_device(): lax.ppermute(returned[s], 'replica', by_shift(-shifts[s], replicas))]
    ppermute x4, waiting for transfers between devices: 29.4 us -> 23.7 us  [project_out(): far = lax.ppermute(chip_sum, 'tensor', other_chip)]
    unnamed x26 -> x4, local copies, waits for them, and re-layouts: 4.51 us -> 0.01 us
    pallas_call x8, Pallas kernels: 16.1 us -> 12.6 us  [project(): pl.pallas_call(functools.partial(project_kernel, flips=flips, tile=tile),...]
    pallas_call x4, Pallas kernels: 7.83 us -> 10.9 us  [finish(): pl.pallas_call(functools.partial(finish_kernel, first=first, qlength=qlen...]
    ppermute x1 -> x0, starting transfers between devices: 2.97 us -> none  [on_device(): failed = failed + lax.ppermute(failed, 'groups', [(0, 1), (1, 0)])]
    convert_element_type x4, other arithmetic: 2.86 us -> 0.49 us  [project_out(): chip_sum = (far_keep + far_core.astype(F32)).astype(BF16)]
  transfers between devices with their start and end apart: 17 -> 16, of which waited for: 6 -> 4; matrix products, arithmetic and copies ran while one was open for 2% -> 0% of each run, Pallas kernels for 58% -> 51%
where the time goes in v2:
time: 151 us; the launch traced here: 150 us
  Pallas kernels  105 us (70%)
  waiting for transfers between devices  29.4 us (19%)
  starting transfers between devices  14.5 us (10%)
    pallas_call x4, Pallas kernels, attend(): pl.pallas_call(functools.partial(attend_kernel, entry=entry, heads=heads,...  74.9 us
    ppermute x4, waiting for transfers between devices, project_out(): far = lax.ppermute(chip_sum, 'tensor', other_chip)  23.7 us
    pallas_call x8, Pallas kernels, project(): pl.pallas_call(functools.partial(project_kernel, flips=flips, tile=tile),...  12.6 us
    pallas_call x4, Pallas kernels, finish(): pl.pallas_call(functools.partial(finish_kernel, first=first, qlength=qlen...  10.9 us
    ppermute x2, waiting for transfers between devices, on_device(): lax.ppermute(returned[s], 'replica', by_shift(-shifts[s], replicas))  5.61 us
    ppermute x2, starting transfers between devices, on_device(): arrived[s] = lax.ppermute(packed[s], 'replica', by_shift(shift, replicas))  5.17 us
    ppermute x4, starting transfers between devices, project_out(): far = lax.ppermute(chip_sum, 'tensor', other_chip)  5.14 us
    pallas_call x2, Pallas kernels, split(): pl.pallas_call(functools.partial(split_kernel, slot=slot), in_specs=[hbm]...  4.23 us
  transfers between devices with their start and end apart: 16, of which 4 were waited for; matrix products, arithmetic and copies ran while one was open for 0% of the time, Pallas kernels for 51%

profile of v2, /device:TPU:0, one launch (start us, length us, event | category | flops | bytes accessed | tf_op | source)
XLA Modules:
  0.0 150.4 jit_solution(2179023524546614656)
XLA Ops:
  0.0 2.1 %split.4 = (bf16[2,4096,128]{2,1,0:T(8,128)(2,1)S(1)}, bf16[2,144,4096]{2,1,0:T(8,128)(2,1)S(1)}) custom-call(bf16[16384,128]{1,0:T(8,128)(2,1)} %bitcast.5), custom_call_target="tpu_custom_call" | custom-call | bytes 4194304 | tf_op jit(solution)/shard_map/split/pallas_call | solution.py:147
  2.1 2.2 %pack.3 = (s32[12]{0:T(128)S(1)}, s32[1]{0:T(128)}, bf16[2,640,128]{2,1,0:T(8,128)(2,1)S(1)}, bf16[2,640,128]{2,1,0:T(8,128)(2,1)S(1)}, bf16[2,640,128]{2,1,0:T(...) custom-call(s32[2,4]{1,0:T(2,128)} %bitcast.10, s32[1,8]{1,0:T(1,128)} %bitcast.12, bf16[512,1024]{1,0:T(8,128)(2,1)} %q_hbm.1, ...), custom_call_target="tpu_custom_call" | custom-call | bytes 4194304 | tf_op jit(solution)/shard_map/pack/pallas_call | solution.py:100
  4.3 18.7 %attend.6.refs_2_.a_ref = bf16[128,1024]{1,0:T(8,128)(2,1)S(1)} custom-call(s32[12]{0:T(128)S(1)} %get-tuple-element.58.table_ref, bf16[2,640,128]{2,1,0:T(8,128)(2,1)S(1)} %get-tuple-element.62.x_ref, bf16[2,4096,128]{2,1,0:T(8,128)(2,1)S(1)} %get-tuple-element.60.keys_ref.refs_0_, bf16[2,144,4096]{2,1,0:T(8,128)(2,1)S(1)} %get-tuple-element.61.values_ref.refs_1_), custom_call_target="tpu_custom_call" | custom-call | flops 4294967296 | bytes 4194304 | tf_op jit(solution)/shard_map/attend/pallas_call | solution.py:228
  23.1 1.9 %project.19 = (bf16[128,2048]{1,0:T(8,128)(2,1)S(1)}, f32[128,2048]{1,0:T(8,128)S(1)}) custom-call(bf16[128,1024]{1,0:T(8,128)(2,1)S(1)} %attend.6.refs_2_.a_ref, bf16[1024,8192]{1,0:T(8,128)(2,1)S(1)} %copy-done), custom_call_target="tpu_custom_call" | custom-call | flops 1073741824 | bytes 8388608 | tf_op jit(solution)/shard_map/project/pallas_call | solution.py:261
  26.9 3.1 %collective-permute-start.14 = (bf16[2,640,128]{2,1,0:T(8,128)(2,1)S(1)}, bf16[2,640,128]{2,1,0:T(8,128)(2,1)S(1)}, u32[]{:S(2)}, u32[]{:S(2)}) collective-permute-start(bf16[2,640,128]{2,1,0:T(8,128)(2,1)S(1)} %get-tuple-element.67), channel_id=1, source_target_pairs={{0,4},{4,8},{8,12},{12,0},{1,5},{5,9},{9,13},{13,1},{2,6},{6,10},{... | collective-permute-start | bytes 983048 | tf_op jit(solution)/shard_map/ppermute | solution.py:377
  30.0 2.1 %split.5 = (bf16[2,4096,128]{2,1,0:T(8,128)(2,1)S(1)}, bf16[2,144,4096]{2,1,0:T(8,128)(2,1)S(1)}) custom-call(bf16[16384,128]{1,0:T(8,128)(2,1)} %bitcast.6, bf16[2,4096,128]{2,1,0:T(8,128)(2,1)S(1)} %get-tuple-element.60.keys_ref.refs_0_, ...), custom_call_target="tpu_custom_call", output_to_operand_aliasing={{0}: (1, {}), {1}: (2, {})} | custom-call | bytes 4194304 | tf_op jit(solution)/shard_map/split/pallas_call | solution.py:147
  32.1 18.8 %attend.9.a_ref = bf16[128,1024]{1,0:T(8,128)(2,1)S(1)} custom-call(s32[12]{0:T(128)S(1)} %get-tuple-element.58.table_ref, bf16[2,640,128]{2,1,0:T(8,128)(2,1)S(1)} %get-tuple-element.70.x_ref, bf16[2,4096,128]{2,1,0:T(8,128)(2,1)S(1)} %get-tuple-element.63.keys_ref, bf16[2,144,4096]{2,1,0:T(8,128)(2,1)S(1)} %get-tuple-element.64.values_ref), custom_call_target="tpu_custom_call" | custom-call | flops 4294967296 | bytes 4194304 | tf_op jit(solution)/shard_map/attend/pallas_call | solution.py:228
  50.9 1.9 %project.17 = (bf16[128,2048]{1,0:T(8,128)(2,1)S(1)}, f32[128,2048]{1,0:T(8,128)S(1)}) custom-call(bf16[128,1024]{1,0:T(8,128)(2,1)S(1)} %attend.9.a_ref, bf16[1024,8192]{1,0:T(8,128)(2,1)S(1)} %copy-done), custom_call_target="tpu_custom_call" | custom-call | flops 1073741824 | bytes 8388608 | tf_op jit(solution)/shard_map/project/pallas_call | solution.py:261
  54.8 2.1 %collective-permute-start.9 = (bf16[2,640,128]{2,1,0:T(8,128)(2,1)S(1)}, bf16[2,640,128]{2,1,0:T(8,128)(2,1)S(1)}, u32[]{:S(2)}, u32[]{:S(2)}) collective-permute-start(bf16[2,640,128]{2,1,0:T(8,128)(2,1)S(1)} %get-tuple-element.59), channel_id=1, source_target_pairs={{0,12},{4,0},{8,4},{12,8},{1,13},{5,1},{9,5},{13,9},{2,14},{6,2},{... | collective-permute-start | bytes 983048 | tf_op jit(solution)/shard_map/ppermute | solution.py:377
  56.8 18.7 %attend.8 = bf16[128,1024]{1,0:T(8,128)(2,1)S(1)} custom-call(s32[12]{0:T(128)S(1)} %get-tuple-element.58.table_ref, bf16[2,640,128]{2,1,0:T(8,128)(2,1)S(1)} %collective-permute-done.14.x_ref, bf16[2,4096,128]{2,1,0:T(8,128)(2,1)S(1)} %get-tuple-element.63.keys_ref, bf16[2,144,4096]{2,1,0:T(8,128)(2,1)S(1)} %get-tuple-element.64.values_ref), custom_call_target="tpu_custom_call" | custom-call | flops 4294967296 | bytes 4194304 | tf_op jit(solution)/shard_map/attend/pallas_call | solution.py:228
  75.5 2.3 %collective-permute-start.15 = (bf16[128,1024]{1,0:T(8,128)(2,1)S(1)}, bf16[128,1024]{1,0:T(8,128)(2,1)S(1)}, u32[]{:S(2)}, u32[]{:S(2)}) collective-permute-start(bf16[128,1024]{1,0:T(8,128)(2,1)S(1)} %attend.8), channel_id=1, source_target_pairs={{0,12},{4,0},{8,4},{12,8},{1,13},{5,1},{9,5},{13,9},{2,14},{6,2},{... | collective-permute-start | bytes 786440 | tf_op jit(solution)/shard_map/ppermute | solution.py:384
  77.8 18.8 %attend.7 = bf16[128,1024]{1,0:T(8,128)(2,1)S(1)} custom-call(s32[12]{0:T(128)S(1)} %get-tuple-element.58.table_ref, bf16[2,640,128]{2,1,0:T(8,128)(2,1)S(1)} %collective-permute-done.9.x_ref, bf16[2,4096,128]{2,1,0:T(8,128)(2,1)S(1)} %get-tuple-element.63.keys_ref, bf16[2,144,4096]{2,1,0:T(8,128)(2,1)S(1)} %get-tuple-element.64.values_ref), custom_call_target="tpu_custom_call" | custom-call | flops 4294967296 | bytes 4194304 | tf_op jit(solution)/shard_map/attend/pallas_call | solution.py:228
  96.8 1.5 %collective-permute-start.24 = (bf16[128,2048]{1,0:T(8,128)(2,1)S(1)}, bf16[128,2048]{1,0:T(8,128)(2,1)S(1)}, u32[]{:S(2)}, u32[]{:S(2)}) collective-permute-start(bf16[128,2048]{1,0:T(8,128)(2,1)S(1)} %add_convert_fusion.1), channel_id=1, source_target_pairs={{0,2},{1,3},{2,0},{3,1},{4,6},{5,7},{6,4},{7,5},{8,10},{9,11},{10,... | collective-permute-start | bytes 1572872 | tf_op jit(solution)/shard_map/ppermute | solution.py:342
  98.4 1.9 %project.15 = (bf16[128,2048]{1,0:T(8,128)(2,1)S(1)}, f32[128,2048]{1,0:T(8,128)S(1)}) custom-call(bf16[128,1024]{1,0:T(8,128)(2,1)S(1)} %collective-permute-done.15.a_ref, bf16[1024,8192]{1,0:T(8,128)(2,1)S(1)} %copy-done), custom_call_target="tpu_custom_call" | custom-call | flops 1073741824 | bytes 8388608 | tf_op jit(solution)/shard_map/project/pallas_call | solution.py:261
  100.5 5.6 %collective-permute-done.10.a_ref = bf16[128,1024]{1,0:T(8,128)(2,1)S(1)} collective-permute-done((bf16[128,1024]{1,0:T(8,128)(2,1)S(1)}, bf16[128,1024]{1,0:T(8,128)(2,1)S(1)}, u32[]{:S(2)}, u32[]{:S(2)}) %collective-permute-start.10) | collective-permute-done | bytes 262176 | tf_op jit(solution)/shard_map/ppermute | solution.py:384
  106.1 1.8 %project.13 = (bf16[128,2048]{1,0:T(8,128)(2,1)S(1)}, f32[128,2048]{1,0:T(8,128)S(1)}) custom-call(bf16[128,1024]{1,0:T(8,128)(2,1)S(1)} %collective-permute-done.10.a_ref, bf16[1024,8192]{1,0:T(8,128)(2,1)S(1)} %copy-done), custom_call_target="tpu_custom_call" | custom-call | flops 1073741824 | bytes 8388608 | tf_op jit(solution)/shard_map/project/pallas_call | solution.py:261
  110.6 1.5 %collective-permute-start.21 = (bf16[128,2048]{1,0:T(8,128)(2,1)S(1)}, bf16[128,2048]{1,0:T(8,128)(2,1)S(1)}, u32[]{:S(2)}, u32[]{:S(2)}) collective-permute-start(bf16[128,2048]{1,0:T(8,128)(2,1)S(1)} %add_convert_fusion.2), channel_id=1, source_target_pairs={{0,2},{1,3},{2,0},{3,1},{4,6},{5,7},{6,4},{7,5},{8,10},{9,11},{10,... | collective-permute-start | bytes 1572872 | tf_op jit(solution)/shard_map/ppermute | solution.py:342
  115.5 2.7 %finish.6.refs_0_ = bf16[512,2048]{1,0:T(8,128)(2,1)} custom-call(s32[12]{0:T(128)S(1)} %get-tuple-element.58.table_ref, s32[1,8]{1,0:T(1,128)S(1)} %copy-done.1, bf16[128,1024]{1,0:T(8,128)(2,1)S(1)} %attend.6.refs_2_.a_ref, bf16[1024,8192]{1,0:T(8,128)(2,1)S(1)} %copy-done, bf16[128,2048]{1,0:T(8,128)(2,1)S(1)} %collective-permute-done.22.core_ref, ...), custom_call_target="tpu_custom_call" | custom-call | flops 536870912 | bytes 4194304 | tf_op jit(solution)/shard_map/finish/pallas_call | solution.py:308
  118.3 7.2 %collective-permute-done.21.far_ref = bf16[128,2048]{1,0:T(8,128)(2,1)S(1)} collective-permute-done((bf16[128,2048]{1,0:T(8,128)(2,1)S(1)}, bf16[128,2048]{1,0:T(8,128)(2,1)S(1)}, u32[]{:S(2)}, u32[]{:S(2)}) %collective-permute-start.21) | collective-permute-done | bytes 524320 | tf_op jit(solution)/shard_map/ppermute | solution.py:342
  125.5 2.7 %finish.7.refs_0_ = bf16[512,2048]{1,0:T(8,128)(2,1)} custom-call(s32[12]{0:T(128)S(1)} %get-tuple-element.58.table_ref, s32[1,8]{1,0:T(1,128)S(1)} %copy-done.1, bf16[128,1024]{1,0:T(8,128)(2,1)S(1)} %attend.9.a_ref, bf16[1024,8192]{1,0:T(8,128)(2,1)S(1)} %copy-done, ...), custom_call_target="tpu_custom_call", output_to_operand_aliasing={{}: (6, {})} | custom-call | flops 536870912 | bytes 4194304 | tf_op jit(solution)/shard_map/finish/pallas_call | solution.py:308
  128.2 8.5 %collective-permute-done.18.far_ref = bf16[128,2048]{1,0:T(8,128)(2,1)S(1)} collective-permute-done((bf16[128,2048]{1,0:T(8,128)(2,1)S(1)}, bf16[128,2048]{1,0:T(8,128)(2,1)S(1)}, u32[]{:S(2)}, u32[]{:S(2)}) %collective-permute-start.18) | collective-permute-done | bytes 524320 | tf_op jit(solution)/shard_map/ppermute | solution.py:342
  136.7 2.7 %finish.8.refs_0_ = bf16[512,2048]{1,0:T(8,128)(2,1)} custom-call(s32[12]{0:T(128)S(1)} %get-tuple-element.58.table_ref, s32[1,8]{1,0:T(1,128)S(1)} %copy-done.1, bf16[128,1024]{1,0:T(8,128)(2,1)S(1)} %collective-permute-done.15.a_ref, bf16[1024,8192]{1,0:T(8,128)(2,1)S(1)} %copy-done, ...), custom_call_target="tpu_custom_call", output_to_operand_aliasing={{}: (6, {})} | custom-call | flops 536870912 | bytes 4194304 | tf_op jit(solution)/shard_map/finish/pallas_call | solution.py:308
  139.4 8.0 %collective-permute-done.13.far_ref = bf16[128,2048]{1,0:T(8,128)(2,1)S(1)} collective-permute-done((bf16[128,2048]{1,0:T(8,128)(2,1)S(1)}, bf16[128,2048]{1,0:T(8,128)(2,1)S(1)}, u32[]{:S(2)}, u32[]{:S(2)}) %collective-permute-start.13) | collective-permute-done | bytes 524320 | tf_op jit(solution)/shard_map/ppermute | solution.py:342
  147.5 2.7 %finish.9 = bf16[512,2048]{1,0:T(8,128)(2,1)} custom-call(s32[12]{0:T(128)S(1)} %get-tuple-element.58.table_ref, s32[1,8]{1,0:T(1,128)S(1)} %copy-done.1, bf16[128,1024]{1,0:T(8,128)(2,1)S(1)} %collective-permute-done.10.a_ref, bf16[1024,8192]{1,0:T(8,128)(2,1)S(1)} %copy-done, ...), custom_call_target="tpu_custom_call", output_to_operand_aliasing={{}: (6, {})} | custom-call | flops 536870912 | bytes 4194304 | tf_op jit(solution)/shard_map/finish/pallas_call | solution.py:308
  (36 shorter events, 9.7 us)
Async XLA Ops:
  2.1 20.9 %copy-start = (bf16[1024,8192]{1,0:T(8,128)(2,1)S(1)}, bf16[1024,8192]{1,0:T(8,128)(2,1)}, u32[]{:S(2)}) copy-start(bf16[1024,8192]{1,0:T(8,128)(2,1)} %w_ref.23) | copy-start | bytes 50331652
  24.9 71.7 %collective-permute-start.23 = (bf16[128,2048]{1,0:T(8,128)(2,1)S(1)}, bf16[128,2048]{1,0:T(8,128)(2,1)S(1)}, u32[]{:S(2)}, u32[]{:S(2)}) collective-permute-start(bf16[128,2048]{1,0:T(8,128)(2,1)S(1)} %get-tuple-element.74), channel_id=1, source_target_pairs={{0,1},{1,0},{2,3},{3,2},{4,5},{5,4},{6,7},{7,6},{8,9},{9,8},{10,11... | collective-permute-start | bytes 1572872 | tf_op jit(solution)/shard_map/ppermute | solution.py:338
  26.8 85.4 %collective-permute-start.22 = (bf16[128,2048]{1,0:T(8,128)(2,1)S(1)}, bf16[128,2048]{1,0:T(8,128)(2,1)S(1)}, u32[]{:S(2)}, u32[]{:S(2)}) collective-permute-start(bf16[128,2048]{1,0:T(8,128)(2,1)S(1)} %project.18), channel_id=1, source_target_pairs={{0,1},{1,0},{2,3},{3,2},{4,5},{5,4},{6,7},{7,6},{8,9},{9,8},{10,11... | collective-permute-start | bytes 1572872 | tf_op jit(solution)/shard_map/ppermute | solution.py:340
  26.9 27.9 %collective-permute-start.14 = (bf16[2,640,128]{2,1,0:T(8,128)(2,1)S(1)}, bf16[2,640,128]{2,1,0:T(8,128)(2,1)S(1)}, u32[]{:S(2)}, u32[]{:S(2)}) collective-permute-start(bf16[2,640,128]{2,1,0:T(8,128)(2,1)S(1)} %get-tuple-element.67), channel_id=1, source_target_pairs={{0,4},{4,8},{8,12},{12,0},{1,5},{5,9},{9,13},{13,1},{2,6},{6,10},{... | collective-permute-start | bytes 983048 | tf_op jit(solution)/shard_map/ppermute | solution.py:377
  52.8 47.4 %collective-permute-start.20 = (bf16[128,2048]{1,0:T(8,128)(2,1)S(1)}, bf16[128,2048]{1,0:T(8,128)(2,1)S(1)}, u32[]{:S(2)}, u32[]{:S(2)}) collective-permute-start(bf16[128,2048]{1,0:T(8,128)(2,1)S(1)} %get-tuple-element.72), channel_id=1, source_target_pairs={{0,1},{1,0},{2,3},{3,2},{4,5},{5,4},{6,7},{7,6},{8,9},{9,8},{10,11... | collective-permute-start | bytes 1572872 | tf_op jit(solution)/shard_map/ppermute | solution.py:338
  54.2 59.0 %collective-permute-start.19 = (bf16[128,2048]{1,0:T(8,128)(2,1)S(1)}, bf16[128,2048]{1,0:T(8,128)(2,1)S(1)}, u32[]{:S(2)}, u32[]{:S(2)}) collective-permute-start(bf16[128,2048]{1,0:T(8,128)(2,1)S(1)} %project.16), channel_id=1, source_target_pairs={{0,1},{1,0},{2,3},{3,2},{4,5},{5,4},{6,7},{7,6},{8,9},{9,8},{10,11... | collective-permute-start | bytes 1572872 | tf_op jit(solution)/shard_map/ppermute | solution.py:340
  54.8 20.8 %collective-permute-start.9 = (bf16[2,640,128]{2,1,0:T(8,128)(2,1)S(1)}, bf16[2,640,128]{2,1,0:T(8,128)(2,1)S(1)}, u32[]{:S(2)}, u32[]{:S(2)}) collective-permute-start(bf16[2,640,128]{2,1,0:T(8,128)(2,1)S(1)} %get-tuple-element.59), channel_id=1, source_target_pairs={{0,12},{4,0},{8,4},{12,8},{1,13},{5,1},{9,5},{13,9},{2,14},{6,2},{... | collective-permute-start | bytes 983048 | tf_op jit(solution)/shard_map/ppermute | solution.py:377
  75.5 21.3 %collective-permute-start.15 = (bf16[128,1024]{1,0:T(8,128)(2,1)S(1)}, bf16[128,1024]{1,0:T(8,128)(2,1)S(1)}, u32[]{:S(2)}, u32[]{:S(2)}) collective-permute-start(bf16[128,1024]{1,0:T(8,128)(2,1)S(1)} %attend.8), channel_id=1, source_target_pairs={{0,12},{4,0},{8,4},{12,8},{1,13},{5,1},{9,5},{13,9},{2,14},{6,2},{... | collective-permute-start | bytes 786440 | tf_op jit(solution)/shard_map/ppermute | solution.py:384
  96.6 9.5 %collective-permute-start.10 = (bf16[128,1024]{1,0:T(8,128)(2,1)S(1)}, bf16[128,1024]{1,0:T(8,128)(2,1)S(1)}, u32[]{:S(2)}, u32[]{:S(2)}) collective-permute-start(bf16[128,1024]{1,0:T(8,128)(2,1)S(1)} %attend.7), channel_id=1, source_target_pairs={{0,4},{4,8},{8,12},{12,0},{1,5},{5,9},{9,13},{13,1},{2,6},{6,10},{... | collective-permute-start | bytes 786440 | tf_op jit(solution)/shard_map/ppermute | solution.py:384
  96.8 16.5 %collective-permute-start.24 = (bf16[128,2048]{1,0:T(8,128)(2,1)S(1)}, bf16[128,2048]{1,0:T(8,128)(2,1)S(1)}, u32[]{:S(2)}, u32[]{:S(2)}) collective-permute-start(bf16[128,2048]{1,0:T(8,128)(2,1)S(1)} %add_convert_fusion.1), channel_id=1, source_target_pairs={{0,2},{1,3},{2,0},{3,1},{4,6},{5,7},{6,4},{7,5},{8,10},{9,11},{10,... | collective-permute-start | bytes 1572872 | tf_op jit(solution)/shard_map/ppermute | solution.py:342
  100.2 10.4 %collective-permute-start.17 = (bf16[128,2048]{1,0:T(8,128)(2,1)S(1)}, bf16[128,2048]{1,0:T(8,128)(2,1)S(1)}, u32[]{:S(2)}, u32[]{:S(2)}) collective-permute-start(bf16[128,2048]{1,0:T(8,128)(2,1)S(1)} %get-tuple-element.69), channel_id=1, source_target_pairs={{0,1},{1,0},{2,3},{3,2},{4,5},{5,4},{6,7},{7,6},{8,9},{9,8},{10,11... | collective-permute-start | bytes 1572872 | tf_op jit(solution)/shard_map/ppermute | solution.py:338
  107.9 4.6 %collective-permute-start.12 = (bf16[128,2048]{1,0:T(8,128)(2,1)S(1)}, bf16[128,2048]{1,0:T(8,128)(2,1)S(1)}, u32[]{:S(2)}, u32[]{:S(2)}) collective-permute-start(bf16[128,2048]{1,0:T(8,128)(2,1)S(1)} %get-tuple-element.66), channel_id=1, source_target_pairs={{0,1},{1,0},{2,3},{3,2},{4,5},{5,4},{6,7},{7,6},{8,9},{9,8},{10,11... | collective-permute-start | bytes 1572872 | tf_op jit(solution)/shard_map/ppermute | solution.py:338
  110.6 14.9 %collective-permute-start.21 = (bf16[128,2048]{1,0:T(8,128)(2,1)S(1)}, bf16[128,2048]{1,0:T(8,128)(2,1)S(1)}, u32[]{:S(2)}, u32[]{:S(2)}) collective-permute-start(bf16[128,2048]{1,0:T(8,128)(2,1)S(1)} %add_convert_fusion.2), channel_id=1, source_target_pairs={{0,2},{1,3},{2,0},{3,1},{4,6},{5,7},{6,4},{7,5},{8,10},{9,11},{10,... | collective-permute-start | bytes 1572872 | tf_op jit(solution)/shard_map/ppermute | solution.py:342
  112.1 3.4 %copy-start.1 = (s32[1,8]{1,0:T(1,128)S(1)}, s32[1,8]{1,0:T(1,128)}, u32[]{:S(2)}) copy-start(s32[1,8]{1,0:T(1,128)} %counts_ref.7) | copy-start | bytes 100
  112.3 15.9 %collective-permute-start.16 = (bf16[128,2048]{1,0:T(8,128)(2,1)S(1)}, bf16[128,2048]{1,0:T(8,128)(2,1)S(1)}, u32[]{:S(2)}, u32[]{:S(2)}) collective-permute-start(bf16[128,2048]{1,0:T(8,128)(2,1)S(1)} %project.14), channel_id=1, source_target_pairs={{0,1},{1,0},{2,3},{3,2},{4,5},{5,4},{6,7},{7,6},{8,9},{9,8},{10,11... | collective-permute-start | bytes 1572872 | tf_op jit(solution)/shard_map/ppermute | solution.py:340
  112.5 24.2 %collective-permute-start.18 = (bf16[128,2048]{1,0:T(8,128)(2,1)S(1)}, bf16[128,2048]{1,0:T(8,128)(2,1)S(1)}, u32[]{:S(2)}, u32[]{:S(2)}) collective-permute-start(bf16[128,2048]{1,0:T(8,128)(2,1)S(1)} %add_convert_fusion.3), channel_id=1, source_target_pairs={{0,2},{1,3},{2,0},{3,1},{4,6},{5,7},{6,4},{7,5},{8,10},{9,11},{10,... | collective-permute-start | bytes 1572872 | tf_op jit(solution)/shard_map/ppermute | solution.py:342
  113.3 26.2 %collective-permute-start.11 = (bf16[128,2048]{1,0:T(8,128)(2,1)S(1)}, bf16[128,2048]{1,0:T(8,128)(2,1)S(1)}, u32[]{:S(2)}, u32[]{:S(2)}) collective-permute-start(bf16[128,2048]{1,0:T(8,128)(2,1)S(1)} %project.12), channel_id=1, source_target_pairs={{0,1},{1,0},{2,3},{3,2},{4,5},{5,4},{6,7},{7,6},{8,9},{9,8},{10,11... | collective-permute-start | bytes 1572872 | tf_op jit(solution)/shard_map/ppermute | solution.py:340
  113.3 34.1 %collective-permute-start.13 = (bf16[128,2048]{1,0:T(8,128)(2,1)S(1)}, bf16[128,2048]{1,0:T(8,128)(2,1)S(1)}, u32[]{:S(2)}, u32[]{:S(2)}) collective-permute-start(bf16[128,2048]{1,0:T(8,128)(2,1)S(1)} %add_convert_fusion.4), channel_id=1, source_target_pairs={{0,2},{1,3},{2,0},{3,1},{4,6},{5,7},{6,4},{7,5},{8,10},{9,11},{10,... | collective-permute-start | bytes 1572872 | tf_op jit(solution)/shard_map/ppermute | solution.py:342

commit v3 on v2

--- a/solution.py
+++ b/solution.py
@@ -18,15 +18,16 @@
 SMEM = pl.BlockSpec(memory_space=pltpu.SMEM)
 
 
-def pack_kernel(stored_hbm, ids_hbm, q_hbm, own_hbm, table_ref, failed_ref, *refs, route, heads, qlength):
-    number = len(refs) - 5
-    out_refs = refs[:number]
-    stored_ref, ids_ref, q_ref, own_ref, sems = refs[number:]
+def pack_kernel(stored_hbm, ids_hbm, q_hbm, own_hbm, kv_hbm, table_ref, failed_ref, *refs, route, heads, qlength):
+    number = len(refs) - 10
+    out_refs, (k_ref, vt_ref) = refs[:number], refs[number : number + 2]
+    stored_ref, ids_ref, q_ref, own_ref, sems, pairs_ref, wide_ref, kv_sems = refs[number + 2 :]
     head_size = own_ref.shape[1]
     questions = ids_ref.shape[1]
     pairs = ((stored_hbm, stored_ref), (ids_hbm, ids_ref), (q_hbm, q_ref), (own_hbm, own_ref))
     copies = [pltpu.make_async_copy(source, target, sems.at[i]) for i, (source, target) in enumerate(pairs)]
-    for copy in copies:
+    kv_copies = split_copies(kv_hbm, pairs_ref, kv_sems, 0)
+    for copy in copies + kv_copies:
         copy.start()
     for copy in copies[:2]:
         copy.wait()
@@ -51,6 +52,7 @@
                 out_ref[j, h * qlength : (h + 1) * qlength, :] = rows[:, h * head_size : (h + 1) * head_size]
             own = own_ref[pl.ds(pl.multiple_of(place * 2 * qlength, 2 * qlength), 2 * qlength), :]
             out_ref[j, heads * qlength :, :] = own
+    split_arrived(kv_copies, k_ref, vt_ref, pairs_ref, wide_ref, 0)
 
 
 def route_first(replicas, stored_ref, table_ref, failed_ref):
@@ -90,44 +92,47 @@
     return held(me) + plans[0][1]
 
 
-def pack(stored, ids, queries, own, phases, route):
+def pack(stored, ids, queries, own, pairs, context, slots, phases, route):
     questions = ids.shape[1]
     head_size = own.shape[1]
     qlength = queries.shape[0] // questions
     heads = queries.shape[1] // head_size
     rows = heads * qlength + 2 * qlength
-    arguments = [pltpu.with_memory_space_constraint(x, pltpu.HBM) for x in (stored, ids, queries, own)]
+    arguments = [pltpu.with_memory_space_constraint(x, pltpu.HBM) for x in (stored, ids, queries, own, pairs)]
+    split_out, split_scratch = split_shapes(context, head_size, slots)
     out = pl.pallas_call(
         functools.partial(pack_kernel, route=route, heads=heads, qlength=qlength),
-        in_specs=[pl.BlockSpec(memory_space=pltpu.HBM)] * 4,
-        out_specs=[SMEM, SMEM] + [VMEM] * phases,
+        in_specs=[pl.BlockSpec(memory_space=pltpu.HBM)] * 5,
+        out_specs=[SMEM, SMEM] + [VMEM] * (phases + 2),
         out_shape=[jax.ShapeDtypeStruct((size,), jnp.int32) for size in (phases * (CAP + 1), 1)]
-        + [jax.ShapeDtypeStruct((CAP, rows, head_size), BF16)] * phases,
+        + [jax.ShapeDtypeStruct((CAP, rows, head_size), BF16)] * phases
+        + split_out,
         scratch_shapes=[
             pltpu.SMEM(stored.shape, jnp.int32),
             pltpu.SMEM(ids.shape, jnp.int32),
             pltpu.VMEM(queries.shape, BF16),
             pltpu.VMEM(own.shape, BF16),
             pltpu.SemaphoreType.DMA((4,)),
+            *split_scratch,
         ],
         compiler_params=pltpu.CompilerParams(vmem_limit_bytes=16 << 20),
         cost_estimate=pl.CostEstimate(flops=0, bytes_accessed=4 << 20, transcendentals=0),
         name="pack",
     )(*arguments)
-    return out[0], out[1], out[2:]
-
-
-def split_kernel(x_ref, *refs, slot):
-    k_ref, vt_ref, pairs_ref, wide_ref, sems = refs[-5:]
-    parts, block, head_size = pairs_ref.shape
-    half = block // 2
-    depth, context = vt_ref.shape[1:]
-    copies = [
+    return out[0], out[1], out[2:-2], out[-2:]
+
+
+def split_copies(x_ref, pairs_ref, sems, slot):
+    parts, block, _ = pairs_ref.shape
+    return [
         pltpu.make_async_copy(x_ref.at[pl.ds((slot * parts + i) * block, block), :], pairs_ref.at[i], sems.at[i])
         for i in range(parts)
     ]
-    for copy in copies:
-        copy.start()
+
+
+def split_arrived(copies, k_ref, vt_ref, pairs_ref, wide_ref, slot):
+    half, head_size = pairs_ref.shape[1] // 2, pairs_ref.shape[2]
+    depth, context = vt_ref.shape[1:]
     vt_ref[slot, head_size:, :] = jnp.ones((depth - head_size, context), BF16)
     for i, copy in enumerate(copies):
         copy.wait()
@@ -138,30 +143,43 @@
         vt_ref[slot, :head_size, i * half : (i + 1) * half] = values.T.astype(BF16)
 
 
-def split(pairs, context, slots, slot=0, previous=None, after=None):
-    head_size = pairs.shape[1]
+def split_shapes(context, head_size, slots):
     parts = 8
     block = 2 * context // parts
+    out_shape = [
+        jax.ShapeDtypeStruct((slots, context, head_size), BF16),
+        jax.ShapeDtypeStruct((slots, head_size + 16, context), BF16),
+    ]
+    scratch_shapes = [
+        pltpu.VMEM((parts, block, head_size), BF16),
+        pltpu.VMEM((2, block, head_size), F32),
+        pltpu.SemaphoreType.DMA((parts,)),
+    ]
+    return out_shape, scratch_shapes
+
+
+def split_kernel(x_ref, keys_ref, values_ref, after_ref, k_ref, vt_ref, pairs_ref, wide_ref, sems, *, slot):
+    copies = split_copies(x_ref, pairs_ref, sems, slot)
+    for copy in copies:
+        copy.start()
+    split_arrived(copies, k_ref, vt_ref, pairs_ref, wide_ref, slot)
+
+
+def split(pairs, keys, values_t, slot, after):
+    slots, context, head_size = keys.shape
+    out_shape, scratch_shapes = split_shapes(context, head_size, slots)
     hbm = pl.BlockSpec(memory_space=pltpu.HBM)
-    extra = [] if previous is None else [*previous, after]
     return pl.pallas_call(
         functools.partial(split_kernel, slot=slot),
-        in_specs=[hbm] + ([VMEM, VMEM, pl.BlockSpec(memory_space=pl.ANY)] if extra else []),
+        in_specs=[hbm, VMEM, VMEM, pl.BlockSpec(memory_space=pl.ANY)],
         out_specs=[VMEM, VMEM],
-        out_shape=[
-            jax.ShapeDtypeStruct((slots, context, head_size), BF16),
-            jax.ShapeDtypeStruct((slots, head_size + 16, context), BF16),
-        ],
-        scratch_shapes=[
-            pltpu.VMEM((parts, block, head_size), BF16),
-            pltpu.VMEM((2, block, head_size), F32),
-            pltpu.SemaphoreType.DMA((parts,)),
-        ],
-        input_output_aliases={1: 0, 2: 1} if extra else {},
+        out_shape=out_shape,
+        scratch_shapes=scratch_shapes,
+        input_output_aliases={1: 0, 2: 1},
         compiler_params=pltpu.CompilerParams(vmem_limit_bytes=16 << 20),
         cost_estimate=pl.CostEstimate(flops=0, bytes_accessed=8 * context * head_size, transcendentals=0),
         name="split",
-    )(pltpu.with_memory_space_constraint(pairs, pltpu.HBM), *extra)
+    )(pltpu.with_memory_space_constraint(pairs, pltpu.HBM), keys, values_t, after)
 
 
 def attend_kernel(table_ref, x_ref, keys_ref, values_ref, o_ref, *, entry, heads, qlength, chunk):
@@ -219,7 +237,7 @@
 
         return carry
 
-    lax.fori_loop(0, x_ref.shape[0], one, 0)
+    lax.fori_loop(0, x_ref.shape[0], one, 0, unroll=x_ref.shape[0] == CAP)
 
 
 def attend(table, entry, x, keys, values_t, heads, qlength):
@@ -273,19 +291,16 @@
     )(rows, weight)
 
 
-def finish_kernel(table_ref, counts_ref, a_ref, w_ref, core_ref, far_ref, *refs, first, qlength, tile):
+def finish_kernel(table_ref, counts_ref, kept_ref, core_ref, far_ref, *refs, first, qlength, tile):
     o_ref, block_ref, sems = refs[-3:]
     number, _, columns = block_ref.shape
-    me = lax.axis_index("tensor")
     places = [jnp.maximum(table_ref[first + i], 0) for i in range(number)]
     counts = [counts_ref[0, place] for place in places]
     t = lax.broadcasted_iota(jnp.int32, (qlength, tile), 0)
 
     def one(j, carry):
         out = pl.ds(pl.multiple_of(j * tile, tile), tile)
-        source = pl.ds(pl.multiple_of(me * columns + j * tile, tile), tile)
-        total = jnp.dot(a_ref[...], w_ref[:, source], preferred_element_type=F32)
-        total = total + core_ref[:, out].astype(F32) + far_ref[:, out].astype(F32)
+        total = kept_ref[:, out] + core_ref[:, out].astype(F32) + far_ref[:, out].astype(F32)
         for i in range(number):
             block = total[i * qlength : (i + 1) * qlength, :]
             block_ref[i, :, out] = jnp.where(t < counts[i], block, 0.0).astype(BF16)
@@ -301,25 +316,21 @@
         copy.wait()
 
 
-def finish(table, counts, results, weight, from_core, from_far, first, previous, rows, qlength, tile):
-    number, columns = results.shape[0] // qlength, from_far.shape[1]
+def finish(table, counts, kept, from_core, from_far, first, previous, rows, qlength, tile):
+    number, columns = kept.shape[0] // qlength, kept.shape[1]
     extra = [] if previous is None else [pltpu.with_memory_space_constraint(previous, pltpu.HBM)]
     hbm = pl.BlockSpec(memory_space=pltpu.HBM)
     return pl.pallas_call(
         functools.partial(finish_kernel, first=first, qlength=qlength, tile=tile),
-        in_specs=[SMEM, SMEM, VMEM, VMEM, VMEM, VMEM] + [hbm] * len(extra),
+        in_specs=[SMEM, SMEM, VMEM, VMEM, VMEM] + [hbm] * len(extra),
         out_specs=hbm,
         out_shape=pltpu.HBM((rows, columns), BF16),
         scratch_shapes=[pltpu.VMEM((number, qlength, columns), BF16), pltpu.SemaphoreType.DMA((number,))],
-        input_output_aliases={6: 0} if extra else {},
+        input_output_aliases={5: 0} if extra else {},
         compiler_params=pltpu.CompilerParams(vmem_limit_bytes=12 << 20),
-        cost_estimate=pl.CostEstimate(
-            flops=2 * results.shape[0] * results.shape[1] * columns,
-            bytes_accessed=2 * results.shape[1] * columns,
-            transcendentals=0,
-        ),
+        cost_estimate=pl.CostEstimate(flops=0, bytes_accessed=10 * kept.shape[0] * columns, transcendentals=0),
         name="finish",
-    )(table, counts, results, weight, from_core, from_far, *extra)
+    )(table, counts, kept, from_core, from_far, *extra)
 
 
 def by_shift(shift, replicas):
@@ -340,13 +351,14 @@
     near_core = lax.ppermute(near_give, "tensor", other_core)
     chip_sum = (far_keep + far_core.astype(F32)).astype(BF16)
     far = lax.ppermute(chip_sum, "tensor", other_chip)
-    return finish(table, counts, results, weight, near_core, far, first, out, rows, qlength, tile)
-
-
-def answer_by_first_slots(queries, own, keys, values_t, stored, ids, heads, qlength):
+    (near_keep,) = project(results, weight, shares, tile, (0,), (F32,))
+    return finish(table, counts, near_keep, near_core, far, first, out, rows, qlength, tile)
+
+
+def answer_by_first_slots(queries, own, pairs, context, stored, ids, heads, qlength):
     replicas = stored.shape[1]
     route = functools.partial(route_first, replicas)
-    table, _, packed = pack(stored, ids, queries, own, replicas, route)
+    table, _, packed, (keys, values_t) = pack(stored, ids, queries, own, pairs, context, 1, replicas, route)
     arrived = [packed[0]] + [lax.ppermute(packed[s], "replica", by_shift(s, replicas)) for s in range(1, replicas)]
     result = attend(table, 0, jnp.concatenate(arrived), keys, values_t, heads, qlength)
     parts = result.reshape(replicas, CAP * qlength, -1)
@@ -370,15 +382,16 @@
     stored = stored.T
 
     if small_slice(groups, replicas, shares) and replicas * CAP == questions and slots == 2:
-        table, failed, packed = pack(stored, ids, queries, own, 4, route_near)
+        table, failed, packed, (keys, values_t) = pack(
+            stored, ids, queries, own, pairs, context, slots, 4, route_near
+        )
         arrived, returned = dict(enumerate(packed)), {}
         shifts = {2: 1, 3: -1}
         for s, shift in shifts.items():
             arrived[s] = lax.ppermute(packed[s], "replica", by_shift(shift, replicas))
         for s in range(4):
-            if s < 2:
-                previous, after = ((keys, values_t), returned[0]) if s else (None, None)
-                keys, values_t = split(pairs, context, slots, s, previous, after)
+            if s == 1:
+                keys, values_t = split(pairs, keys, values_t, 1, returned[0])
             returned[s] = attend(table, s if s < 2 else (8 + s,), arrived[s], keys, values_t, heads, qlength)
             if s in shifts:
                 returned[s] = lax.ppermute(returned[s], "replica", by_shift(-shifts[s], replicas))
@@ -387,14 +400,12 @@
             out = project_out(table, token_counts, returned[s], out_weight, shares, s * CAP, out, rows, qlength)
 
         def again():
-            keys, values_t = split(pairs, context, 1)
-            table, results = answer_by_first_slots(queries, own, keys, values_t, stored, ids, heads, qlength)
+            table, results = answer_by_first_slots(queries, own, pairs, context, stored, ids, heads, qlength)
             return project_out(table, token_counts, results, out_weight, shares, 0, None, rows, qlength)
 
         return lax.cond(failed[0] > 0, again, lambda: out)
 
-    keys, values_t = split(pairs, context, 1)
-    table, results = answer_by_first_slots(queries, own, keys, values_t, stored, ids, heads, qlength)
+    table, results = answer_by_first_slots(queries, own, pairs, context, stored, ids, heads, qlength)
     blocks = results.reshape(replicas * CAP, qlength, -1)
     match = table[None, : replicas * CAP] == jnp.arange(questions, dtype=jnp.int32)[:, None]
     position = jnp.argmax(match.astype(jnp.int32), axis=1)

time: 151 us -> 149 us (0.987)
  waiting for transfers between devices: 29.4 us -> 27.4 us
    pallas_call x8 -> x12, Pallas kernels: 12.6 us -> 17.9 us  [project(): pl.pallas_call(functools.partial(project_kernel, flips=flips, tile=tile),...]
    pallas_call x4, Pallas kernels: 10.9 us -> 6.3 us  [finish(): pl.pallas_call(functools.partial(finish_kernel, first=first, qlength=qlen...]
    pallas_call x2 -> x1, Pallas kernels: 4.23 us -> 2.11 us  [split(): pl.pallas_call(functools.partial(split_kernel, slot=slot), in_specs=[hbm,...]
    ppermute x4, waiting for transfers between devices: 23.7 us -> 21.9 us  [project_out(): far = lax.ppermute(chip_sum, 'tensor', other_chip)]
    pallas_call x1, Pallas kernels: 2.2 us -> 3.79 us  [pack(): pl.pallas_call(functools.partial(pack_kernel, route=route, heads=heads, q...]
  transfers between devices with their start and end apart: 16 -> 16, of which waited for: 4 -> 4; matrix products, arithmetic and copies ran while one was open for 0% -> 0% of each run, Pallas kernels for 51% -> 53%
where the time goes in v3:
time: 149 us
  Pallas kernels  105 us (70%)
  waiting for transfers between devices  27.4 us (18%)
  starting transfers between devices  14.5 us (10%)
    pallas_call x4, Pallas kernels, attend(): pl.pallas_call(functools.partial(attend_kernel, entry=entry, heads=heads,...  75.2 us
    ppermute x4, waiting for transfers between devices, project_out(): far = lax.ppermute(chip_sum, 'tensor', other_chip)  21.9 us
    pallas_call x12, Pallas kernels, project(): pl.pallas_call(functools.partial(project_kernel, flips=flips, tile=tile),...  17.9 us
    pallas_call x4, Pallas kernels, finish(): pl.pallas_call(functools.partial(finish_kernel, first=first, qlength=qlen...  6.3 us
    ppermute x4, starting transfers between devices, project_out(): far = lax.ppermute(chip_sum, 'tensor', other_chip)  5.52 us
    ppermute x2, waiting for transfers between devices, on_device(): lax.ppermute(returned[s], 'replica', by_shift(-shifts[s], replicas))  5.48 us
    ppermute x2, starting transfers between devices, on_device(): arrived[s] = lax.ppermute(packed[s], 'replica', by_shift(shift, replicas))  5.11 us
    pallas_call x1, Pallas kernels, pack(): pl.pallas_call(functools.partial(pack_kernel, route=route, heads=heads, q...  3.79 us
  transfers between devices with their start and end apart: 16, of which 4 were waited for; matrix products, arithmetic and copies ran while one was open for 0% of the time, Pallas kernels for 53%

profile of v3, /device:TPU:0, one launch (start us, length us, event | category | flops | bytes accessed | tf_op | source)
XLA Modules:
  0.0 148.8 jit_solution(853003373054137611)
XLA Ops:
  0.0 3.8 %pack.3 = (s32[12]{0:T(128)S(1)}, s32[1]{0:T(128)}, bf16[2,640,128]{2,1,0:T(8,128)(2,1)S(1)}, bf16[2,640,128]{2,1,0:T(8,128)(2,1)S(1)}, bf16[2,640,128]{2,1,0:T(...) custom-call(s32[2,4]{1,0:T(2,128)} %bitcast.10, ...), custom_call_target="tpu_custom_call" | custom-call | bytes 4194304 | tf_op jit(solution)/shard_map/pack/pallas_call | solution.py:103
  3.8 18.7 %attend.6.after_ref.a_ref = bf16[128,1024]{1,0:T(8,128)(2,1)S(1)} custom-call(s32[12]{0:T(128)S(1)} %get-tuple-element.58.table_ref, bf16[2,640,128]{2,1,0:T(8,128)(2,1)S(1)} %get-tuple-element.62.x_ref, bf16[2,4096,128]{2,1,0:T(8,128)(2,1)S(1)} %get-tuple-element.60.keys_ref, bf16[2,144,4096]{2,1,0:T(8,128)(2,1)S(1)} %get-tuple-element.61.values_ref), custom_call_target="tpu_custom_call" | custom-call | flops 4294967296 | bytes 4194304 | tf_op jit(solution)/shard_map/attend/pallas_call | solution.py:246
  22.5 1.9 %project.29 = (bf16[128,2048]{1,0:T(8,128)(2,1)S(1)}, f32[128,2048]{1,0:T(8,128)S(1)}) custom-call(bf16[128,1024]{1,0:T(8,128)(2,1)S(1)} %attend.6.after_ref.a_ref, bf16[1024,8192]{1,0:T(8,128)(2,1)S(1)} %copy-done), custom_call_target="tpu_custom_call" | custom-call | flops 1073741824 | bytes 8388608 | tf_op jit(solution)/shard_map/project/pallas_call | solution.py:279
  26.3 3.1 %collective-permute-start.14 = (bf16[2,640,128]{2,1,0:T(8,128)(2,1)S(1)}, bf16[2,640,128]{2,1,0:T(8,128)(2,1)S(1)}, u32[]{:S(2)}, u32[]{:S(2)}) collective-permute-start(bf16[2,640,128]{2,1,0:T(8,128)(2,1)S(1)} %get-tuple-element.67), channel_id=1, source_target_pairs={{0,4},{4,8},{8,12},{12,0},{1,5},{5,9},{9,13},{13,1},{2,6},{6,10},{... | collective-permute-start | bytes 983048 | tf_op jit(solution)/shard_map/ppermute | solution.py:391
  29.4 2.1 %split.1 = (bf16[2,4096,128]{2,1,0:T(8,128)(2,1)S(1)}, bf16[2,144,4096]{2,1,0:T(8,128)(2,1)S(1)}) custom-call(bf16[16384,128]{1,0:T(8,128)(2,1)} %bitcast.6, bf16[2,4096,128]{2,1,0:T(8,128)(2,1)S(1)} %get-tuple-element.60.keys_ref, bf16[2,144,4096]{2,1,0:T(8,128)(2,1)S(1)} %get-tuple-element.61.values_ref, ...), custom_call_target="tpu_custom_call", output_to_operand_aliasing={{0}: (1, {}), {1}: (2, {})} | custom-call | bytes 4194304 | tf_op jit(solution)/shard_map/split/pallas_call | solution.py:172
  31.5 18.9 %attend.9.a_ref = bf16[128,1024]{1,0:T(8,128)(2,1)S(1)} custom-call(s32[12]{0:T(128)S(1)} %get-tuple-element.58.table_ref, bf16[2,640,128]{2,1,0:T(8,128)(2,1)S(1)} %get-tuple-element.70.x_ref, bf16[2,4096,128]{2,1,0:T(8,128)(2,1)S(1)} %get-tuple-element.63.keys_ref, bf16[2,144,4096]{2,1,0:T(8,128)(2,1)S(1)} %get-tuple-element.64.values_ref), custom_call_target="tpu_custom_call" | custom-call | flops 4294967296 | bytes 4194304 | tf_op jit(solution)/shard_map/attend/pallas_call | solution.py:246
  50.4 1.9 %project.26 = (bf16[128,2048]{1,0:T(8,128)(2,1)S(1)}, f32[128,2048]{1,0:T(8,128)S(1)}) custom-call(bf16[128,1024]{1,0:T(8,128)(2,1)S(1)} %attend.9.a_ref, bf16[1024,8192]{1,0:T(8,128)(2,1)S(1)} %copy-done), custom_call_target="tpu_custom_call" | custom-call | flops 1073741824 | bytes 8388608 | tf_op jit(solution)/shard_map/project/pallas_call | solution.py:279
  54.2 2.1 %collective-permute-start.9 = (bf16[2,640,128]{2,1,0:T(8,128)(2,1)S(1)}, bf16[2,640,128]{2,1,0:T(8,128)(2,1)S(1)}, u32[]{:S(2)}, u32[]{:S(2)}) collective-permute-start(bf16[2,640,128]{2,1,0:T(8,128)(2,1)S(1)} %get-tuple-element.59), channel_id=1, source_target_pairs={{0,12},{4,0},{8,4},{12,8},{1,13},{5,1},{9,5},{13,9},{2,14},{6,2},{... | collective-permute-start | bytes 983048 | tf_op jit(solution)/shard_map/ppermute | solution.py:391
  56.3 18.7 %attend.8 = bf16[128,1024]{1,0:T(8,128)(2,1)S(1)} custom-call(s32[12]{0:T(128)S(1)} %get-tuple-element.58.table_ref, bf16[2,640,128]{2,1,0:T(8,128)(2,1)S(1)} %collective-permute-done.14.x_ref, bf16[2,4096,128]{2,1,0:T(8,128)(2,1)S(1)} %get-tuple-element.63.keys_ref, bf16[2,144,4096]{2,1,0:T(8,128)(2,1)S(1)} %get-tuple-element.64.values_ref), custom_call_target="tpu_custom_call" | custom-call | flops 4294967296 | bytes 4194304 | tf_op jit(solution)/shard_map/attend/pallas_call | solution.py:246
  75.0 2.0 %collective-permute-start.15 = (bf16[128,1024]{1,0:T(8,128)(2,1)S(1)}, bf16[128,1024]{1,0:T(8,128)(2,1)S(1)}, u32[]{:S(2)}, u32[]{:S(2)}) collective-permute-start(bf16[128,1024]{1,0:T(8,128)(2,1)S(1)} %attend.8), channel_id=1, source_target_pairs={{0,12},{4,0},{8,4},{12,8},{1,13},{5,1},{9,5},{13,9},{2,14},{6,2},{... | collective-permute-start | bytes 786440 | tf_op jit(solution)/shard_map/ppermute | solution.py:397
  77.1 18.9 %attend.7 = bf16[128,1024]{1,0:T(8,128)(2,1)S(1)} custom-call(s32[12]{0:T(128)S(1)} %get-tuple-element.58.table_ref, bf16[2,640,128]{2,1,0:T(8,128)(2,1)S(1)} %collective-permute-done.9.x_ref, bf16[2,4096,128]{2,1,0:T(8,128)(2,1)S(1)} %get-tuple-element.63.keys_ref, bf16[2,144,4096]{2,1,0:T(8,128)(2,1)S(1)} %get-tuple-element.64.values_ref), custom_call_target="tpu_custom_call" | custom-call | flops 4294967296 | bytes 4194304 | tf_op jit(solution)/shard_map/attend/pallas_call | solution.py:246
  96.3 1.8 %collective-permute-start.24 = (bf16[128,2048]{1,0:T(8,128)(2,1)S(1)}, bf16[128,2048]{1,0:T(8,128)(2,1)S(1)}, u32[]{:S(2)}, u32[]{:S(2)}) collective-permute-start(bf16[128,2048]{1,0:T(8,128)(2,1)S(1)} %add_convert_fusion.1), channel_id=1, source_target_pairs={{0,2},{1,3},{2,0},{3,1},{4,6},{5,7},{6,4},{7,5},{8,10},{9,11},{10,... | collective-permute-start | bytes 1572872 | tf_op jit(solution)/shard_map/ppermute | solution.py:353
  98.1 1.9 %project.23 = (bf16[128,2048]{1,0:T(8,128)(2,1)S(1)}, f32[128,2048]{1,0:T(8,128)S(1)}) custom-call(bf16[128,1024]{1,0:T(8,128)(2,1)S(1)} %collective-permute-done.15.a_ref, bf16[1024,8192]{1,0:T(8,128)(2,1)S(1)} %copy-done), custom_call_target="tpu_custom_call" | custom-call | flops 1073741824 | bytes 8388608 | tf_op jit(solution)/shard_map/project/pallas_call | solution.py:279
  100.1 5.5 %collective-permute-done.10.a_ref = bf16[128,1024]{1,0:T(8,128)(2,1)S(1)} collective-permute-done((bf16[128,1024]{1,0:T(8,128)(2,1)S(1)}, bf16[128,1024]{1,0:T(8,128)(2,1)S(1)}, u32[]{:S(2)}, u32[]{:S(2)}) %collective-permute-start.10) | collective-permute-done | bytes 262176 | tf_op jit(solution)/shard_map/ppermute | solution.py:397
  105.6 1.9 %project.20 = (bf16[128,2048]{1,0:T(8,128)(2,1)S(1)}, f32[128,2048]{1,0:T(8,128)S(1)}) custom-call(bf16[128,1024]{1,0:T(8,128)(2,1)S(1)} %collective-permute-done.10.a_ref, bf16[1024,8192]{1,0:T(8,128)(2,1)S(1)} %copy-done), custom_call_target="tpu_custom_call" | custom-call | flops 1073741824 | bytes 8388608 | tf_op jit(solution)/shard_map/project/pallas_call | solution.py:279
  110.2 1.6 %collective-permute-start.21 = (bf16[128,2048]{1,0:T(8,128)(2,1)S(1)}, bf16[128,2048]{1,0:T(8,128)(2,1)S(1)}, u32[]{:S(2)}, u32[]{:S(2)}) collective-permute-start(bf16[128,2048]{1,0:T(8,128)(2,1)S(1)} %add_convert_fusion.2), channel_id=1, source_target_pairs={{0,2},{1,3},{2,0},{3,1},{4,6},{5,7},{6,4},{7,5},{8,10},{9,11},{10,... | collective-permute-start | bytes 1572872 | tf_op jit(solution)/shard_map/ppermute | solution.py:353
  112.9 1.6 %collective-permute-start.13 = (bf16[128,2048]{1,0:T(8,128)(2,1)S(1)}, bf16[128,2048]{1,0:T(8,128)(2,1)S(1)}, u32[]{:S(2)}, u32[]{:S(2)}) collective-permute-start(bf16[128,2048]{1,0:T(8,128)(2,1)S(1)} %add_convert_fusion.4), channel_id=1, source_target_pairs={{0,2},{1,3},{2,0},{3,1},{4,6},{5,7},{6,4},{7,5},{8,10},{9,11},{10,... | collective-permute-start | bytes 1572872 | tf_op jit(solution)/shard_map/ppermute | solution.py:353
  120.4 1.6 %finish.6.refs_0_ = bf16[512,2048]{1,0:T(8,128)(2,1)} custom-call(s32[12]{0:T(128)S(1)} %get-tuple-element.58.table_ref, s32[1,8]{1,0:T(1,128)S(1)} %copy-done.1, f32[128,2048]{1,0:T(8,128)S(1)} %project.27.kept_ref, bf16[128,2048]{1,0:T(8,128)(2,1)S(1)} %collective-permute-done.22.core_ref, bf16[128,2048]{1,0:T(8,128)(2,1)S(1)} %collective-permute-done.24.far_ref), custom_call_target="tpu_custom_call" | custom-call | bytes 2621440 | tf_op jit(solution)/shard_map/finish/pallas_call | solution.py:323
  122.0 3.1 %collective-permute-done.21.far_ref = bf16[128,2048]{1,0:T(8,128)(2,1)S(1)} collective-permute-done((bf16[128,2048]{1,0:T(8,128)(2,1)S(1)}, bf16[128,2048]{1,0:T(8,128)(2,1)S(1)}, u32[]{:S(2)}, u32[]{:S(2)}) %collective-permute-start.21) | collective-permute-done | bytes 524320 | tf_op jit(solution)/shard_map/ppermute | solution.py:353
  125.1 1.6 %finish.7.refs_0_ = bf16[512,2048]{1,0:T(8,128)(2,1)} custom-call(s32[12]{0:T(128)S(1)} %get-tuple-element.58.table_ref, s32[1,8]{1,0:T(1,128)S(1)} %copy-done.1, f32[128,2048]{1,0:T(8,128)S(1)} %project.24.kept_ref, bf16[128,2048]{1,0:T(8,128)(2,1)S(1)} %collective-permute-done.19.core_ref, ...), custom_call_target="tpu_custom_call", output_to_operand_aliasing={{}: (5, {})} | custom-call | bytes 2621440 | tf_op jit(solution)/shard_map/finish/pallas_call | solution.py:323
  126.7 9.6 %collective-permute-done.18.far_ref = bf16[128,2048]{1,0:T(8,128)(2,1)S(1)} collective-permute-done((bf16[128,2048]{1,0:T(8,128)(2,1)S(1)}, bf16[128,2048]{1,0:T(8,128)(2,1)S(1)}, u32[]{:S(2)}, u32[]{:S(2)}) %collective-permute-start.18) | collective-permute-done | bytes 524320 | tf_op jit(solution)/shard_map/ppermute | solution.py:353
  136.3 1.6 %finish.8.refs_0_ = bf16[512,2048]{1,0:T(8,128)(2,1)} custom-call(s32[12]{0:T(128)S(1)} %get-tuple-element.58.table_ref, s32[1,8]{1,0:T(1,128)S(1)} %copy-done.1, f32[128,2048]{1,0:T(8,128)S(1)} %project.21.kept_ref, bf16[128,2048]{1,0:T(8,128)(2,1)S(1)} %collective-permute-done.16.core_ref, ...), custom_call_target="tpu_custom_call", output_to_operand_aliasing={{}: (5, {})} | custom-call | bytes 2621440 | tf_op jit(solution)/shard_map/finish/pallas_call | solution.py:323
  137.9 9.2 %collective-permute-done.13.far_ref = bf16[128,2048]{1,0:T(8,128)(2,1)S(1)} collective-permute-done((bf16[128,2048]{1,0:T(8,128)(2,1)S(1)}, bf16[128,2048]{1,0:T(8,128)(2,1)S(1)}, u32[]{:S(2)}, u32[]{:S(2)}) %collective-permute-start.13) | collective-permute-done | bytes 524320 | tf_op jit(solution)/shard_map/ppermute | solution.py:353
  147.1 1.6 %finish.9 = bf16[512,2048]{1,0:T(8,128)(2,1)} custom-call(s32[12]{0:T(128)S(1)} %get-tuple-element.58.table_ref, s32[1,8]{1,0:T(1,128)S(1)} %copy-done.1, f32[128,2048]{1,0:T(8,128)S(1)} %project.18.kept_ref, bf16[128,2048]{1,0:T(8,128)(2,1)S(1)} %collective-permute-done.11.core_ref, ...), custom_call_target="tpu_custom_call", output_to_operand_aliasing={{}: (5, {})} | custom-call | bytes 2621440 | tf_op jit(solution)/shard_map/finish/pallas_call | solution.py:323
  (39 shorter events, 13.3 us)
Async XLA Ops:
  0.0 22.5 %copy-start = (bf16[1024,8192]{1,0:T(8,128)(2,1)S(1)}, bf16[1024,8192]{1,0:T(8,128)(2,1)}, u32[]{:S(2)}) copy-start(bf16[1024,8192]{1,0:T(8,128)(2,1)} %w_ref.23) | copy-start | bytes 50331652
  24.4 71.6 %collective-permute-start.23 = (bf16[128,2048]{1,0:T(8,128)(2,1)S(1)}, bf16[128,2048]{1,0:T(8,128)(2,1)S(1)}, u32[]{:S(2)}, u32[]{:S(2)}) collective-permute-start(bf16[128,2048]{1,0:T(8,128)(2,1)S(1)} %get-tuple-element.74), channel_id=1, source_target_pairs={{0,1},{1,0},{2,3},{3,2},{4,5},{5,4},{6,7},{7,6},{8,9},{9,8},{10,11... | collective-permute-start | bytes 1572872 | tf_op jit(solution)/shard_map/ppermute | solution.py:349
  26.3 86.1 %collective-permute-start.22 = (bf16[128,2048]{1,0:T(8,128)(2,1)S(1)}, bf16[128,2048]{1,0:T(8,128)(2,1)S(1)}, u32[]{:S(2)}, u32[]{:S(2)}) collective-permute-start(bf16[128,2048]{1,0:T(8,128)(2,1)S(1)} %project.28), channel_id=1, source_target_pairs={{0,1},{1,0},{2,3},{3,2},{4,5},{5,4},{6,7},{7,6},{8,9},{9,8},{10,11... | collective-permute-start | bytes 1572872 | tf_op jit(solution)/shard_map/ppermute | solution.py:351
  26.3 27.9 %collective-permute-start.14 = (bf16[2,640,128]{2,1,0:T(8,128)(2,1)S(1)}, bf16[2,640,128]{2,1,0:T(8,128)(2,1)S(1)}, u32[]{:S(2)}, u32[]{:S(2)}) collective-permute-start(bf16[2,640,128]{2,1,0:T(8,128)(2,1)S(1)} %get-tuple-element.67), channel_id=1, source_target_pairs={{0,4},{4,8},{8,12},{12,0},{1,5},{5,9},{9,13},{13,1},{2,6},{6,10},{... | collective-permute-start | bytes 983048 | tf_op jit(solution)/shard_map/ppermute | solution.py:391
  52.3 47.7 %collective-permute-start.20 = (bf16[128,2048]{1,0:T(8,128)(2,1)S(1)}, bf16[128,2048]{1,0:T(8,128)(2,1)S(1)}, u32[]{:S(2)}, u32[]{:S(2)}) collective-permute-start(bf16[128,2048]{1,0:T(8,128)(2,1)S(1)} %get-tuple-element.72), channel_id=1, source_target_pairs={{0,1},{1,0},{2,3},{3,2},{4,5},{5,4},{6,7},{7,6},{8,9},{9,8},{10,11... | collective-permute-start | bytes 1572872 | tf_op jit(solution)/shard_map/ppermute | solution.py:349
  53.7 59.2 %collective-permute-start.19 = (bf16[128,2048]{1,0:T(8,128)(2,1)S(1)}, bf16[128,2048]{1,0:T(8,128)(2,1)S(1)}, u32[]{:S(2)}, u32[]{:S(2)}) collective-permute-start(bf16[128,2048]{1,0:T(8,128)(2,1)S(1)} %project.25), channel_id=1, source_target_pairs={{0,1},{1,0},{2,3},{3,2},{4,5},{5,4},{6,7},{7,6},{8,9},{9,8},{10,11... | collective-permute-start | bytes 1572872 | tf_op jit(solution)/shard_map/ppermute | solution.py:351
  54.2 20.8 %collective-permute-start.9 = (bf16[2,640,128]{2,1,0:T(8,128)(2,1)S(1)}, bf16[2,640,128]{2,1,0:T(8,128)(2,1)S(1)}, u32[]{:S(2)}, u32[]{:S(2)}) collective-permute-start(bf16[2,640,128]{2,1,0:T(8,128)(2,1)S(1)} %get-tuple-element.59), channel_id=1, source_target_pairs={{0,12},{4,0},{8,4},{12,8},{1,13},{5,1},{9,5},{13,9},{2,14},{6,2},{... | collective-permute-start | bytes 983048 | tf_op jit(solution)/shard_map/ppermute | solution.py:391
  75.0 21.2 %collective-permute-start.15 = (bf16[128,1024]{1,0:T(8,128)(2,1)S(1)}, bf16[128,1024]{1,0:T(8,128)(2,1)S(1)}, u32[]{:S(2)}, u32[]{:S(2)}) collective-permute-start(bf16[128,1024]{1,0:T(8,128)(2,1)S(1)} %attend.8), channel_id=1, source_target_pairs={{0,12},{4,0},{8,4},{12,8},{1,13},{5,1},{9,5},{13,9},{2,14},{6,2},{... | collective-permute-start | bytes 786440 | tf_op jit(solution)/shard_map/ppermute | solution.py:397
  96.0 9.6 %collective-permute-start.10 = (bf16[128,1024]{1,0:T(8,128)(2,1)S(1)}, bf16[128,1024]{1,0:T(8,128)(2,1)S(1)}, u32[]{:S(2)}, u32[]{:S(2)}) collective-permute-start(bf16[128,1024]{1,0:T(8,128)(2,1)S(1)} %attend.7), channel_id=1, source_target_pairs={{0,4},{4,8},{8,12},{12,0},{1,5},{5,9},{9,13},{13,1},{2,6},{6,10},{... | collective-permute-start | bytes 786440 | tf_op jit(solution)/shard_map/ppermute | solution.py:397
  96.3 16.6 %collective-permute-start.24 = (bf16[128,2048]{1,0:T(8,128)(2,1)S(1)}, bf16[128,2048]{1,0:T(8,128)(2,1)S(1)}, u32[]{:S(2)}, u32[]{:S(2)}) collective-permute-start(bf16[128,2048]{1,0:T(8,128)(2,1)S(1)} %add_convert_fusion.1), channel_id=1, source_target_pairs={{0,2},{1,3},{2,0},{3,1},{4,6},{5,7},{6,4},{7,5},{8,10},{9,11},{10,... | collective-permute-start | bytes 1572872 | tf_op jit(solution)/shard_map/ppermute | solution.py:353
  99.9 10.3 %collective-permute-start.17 = (bf16[128,2048]{1,0:T(8,128)(2,1)S(1)}, bf16[128,2048]{1,0:T(8,128)(2,1)S(1)}, u32[]{:S(2)}, u32[]{:S(2)}) collective-permute-start(bf16[128,2048]{1,0:T(8,128)(2,1)S(1)} %get-tuple-element.69), channel_id=1, source_target_pairs={{0,1},{1,0},{2,3},{3,2},{4,5},{5,4},{6,7},{7,6},{8,9},{9,8},{10,11... | collective-permute-start | bytes 1572872 | tf_op jit(solution)/shard_map/ppermute | solution.py:349
  107.5 4.4 %collective-permute-start.12 = (bf16[128,2048]{1,0:T(8,128)(2,1)S(1)}, bf16[128,2048]{1,0:T(8,128)(2,1)S(1)}, u32[]{:S(2)}, u32[]{:S(2)}) collective-permute-start(bf16[128,2048]{1,0:T(8,128)(2,1)S(1)} %get-tuple-element.66), channel_id=1, source_target_pairs={{0,1},{1,0},{2,3},{3,2},{4,5},{5,4},{6,7},{7,6},{8,9},{9,8},{10,11... | collective-permute-start | bytes 1572872 | tf_op jit(solution)/shard_map/ppermute | solution.py:349
  110.2 14.9 %collective-permute-start.21 = (bf16[128,2048]{1,0:T(8,128)(2,1)S(1)}, bf16[128,2048]{1,0:T(8,128)(2,1)S(1)}, u32[]{:S(2)}, u32[]{:S(2)}) collective-permute-start(bf16[128,2048]{1,0:T(8,128)(2,1)S(1)} %add_convert_fusion.2), channel_id=1, source_target_pairs={{0,2},{1,3},{2,0},{3,1},{4,6},{5,7},{6,4},{7,5},{8,10},{9,11},{10,... | collective-permute-start | bytes 1572872 | tf_op jit(solution)/shard_map/ppermute | solution.py:353
  111.9 14.7 %collective-permute-start.16 = (bf16[128,2048]{1,0:T(8,128)(2,1)S(1)}, bf16[128,2048]{1,0:T(8,128)(2,1)S(1)}, u32[]{:S(2)}, u32[]{:S(2)}) collective-permute-start(bf16[128,2048]{1,0:T(8,128)(2,1)S(1)} %project.22), channel_id=1, source_target_pairs={{0,1},{1,0},{2,3},{3,2},{4,5},{5,4},{6,7},{7,6},{8,9},{9,8},{10,11... | collective-permute-start | bytes 1572872 | tf_op jit(solution)/shard_map/ppermute | solution.py:351
  112.3 24.0 %collective-permute-start.18 = (bf16[128,2048]{1,0:T(8,128)(2,1)S(1)}, bf16[128,2048]{1,0:T(8,128)(2,1)S(1)}, u32[]{:S(2)}, u32[]{:S(2)}) collective-permute-start(bf16[128,2048]{1,0:T(8,128)(2,1)S(1)} %add_convert_fusion.3), channel_id=1, source_target_pairs={{0,2},{1,3},{2,0},{3,1},{4,6},{5,7},{6,4},{7,5},{8,10},{9,11},{10,... | collective-permute-start | bytes 1572872 | tf_op jit(solution)/shard_map/ppermute | solution.py:353
  112.9 25.0 %collective-permute-start.11 = (bf16[128,2048]{1,0:T(8,128)(2,1)S(1)}, bf16[128,2048]{1,0:T(8,128)(2,1)S(1)}, u32[]{:S(2)}, u32[]{:S(2)}) collective-permute-start(bf16[128,2048]{1,0:T(8,128)(2,1)S(1)} %project.19), channel_id=1, source_target_pairs={{0,1},{1,0},{2,3},{3,2},{4,5},{5,4},{6,7},{7,6},{8,9},{9,8},{10,11... | collective-permute-start | bytes 1572872 | tf_op jit(solution)/shard_map/ppermute | solution.py:351
  112.9 34.2 %collective-permute-start.13 = (bf16[128,2048]{1,0:T(8,128)(2,1)S(1)}, bf16[128,2048]{1,0:T(8,128)(2,1)S(1)}, u32[]{:S(2)}, u32[]{:S(2)}) collective-permute-start(bf16[128,2048]{1,0:T(8,128)(2,1)S(1)} %add_convert_fusion.4), channel_id=1, source_target_pairs={{0,2},{1,3},{2,0},{3,1},{4,6},{5,7},{6,4},{7,5},{8,10},{9,11},{10,... | collective-permute-start | bytes 1572872 | tf_op jit(solution)/shard_map/ppermute | solution.py:353
  119.1 1.3 copy-start.1

commit v4 on v3

--- a/solution.py
+++ b/solution.py
@@ -182,70 +182,85 @@
     )(pltpu.with_memory_space_constraint(pairs, pltpu.HBM), keys, values_t, after)
 
 
-def attend_kernel(table_ref, x_ref, keys_ref, values_ref, o_ref, *, entry, heads, qlength, chunk):
-    slot = entry if isinstance(entry, int) else table_ref[entry[0]]
+def attend_kernel(*refs, entry, heads, qlength, chunk):
+    if isinstance(entry, int):
+        x_ref, keys_ref, values_ref, o_ref = refs
+        slot = entry
+    else:
+        table_ref, x_ref, keys_ref, values_ref, o_ref = refs
+        slot = table_ref[entry[0]]
     k_ref, vt_ref = keys_ref.at[slot], values_ref.at[slot]
     context, head_size = k_ref.shape
     scale = LOG2E / math.sqrt(head_size)
     rows = heads * qlength
 
-    def one(i, carry):
+    def start(i):
         qt = x_ref[i, :rows, :].T
         own = x_ref[i, rows:, :]
         near = jnp.dot(own, qt, preferred_element_type=F32) * scale
         u2 = lax.broadcasted_iota(jnp.int32, near.shape, 0)
         t = lax.broadcasted_iota(jnp.int32, near.shape, 1) % qlength
         near = jnp.where((u2 % 2 == 0) & (u2 <= 2 * t), near, -jnp.inf)
-        near_top = jnp.max(near, axis=0, keepdims=True)
-        own_t = own.astype(F32).T.astype(BF16)
-        own_vt = jnp.concatenate([own_t, jnp.ones((16, own.shape[0]), BF16)], axis=0)
+        own_vt = jnp.concatenate([own.astype(F32).T.astype(BF16), jnp.ones((16, own.shape[0]), BF16)], axis=0)
 
         def mix_near(top):
             weights = pltpu.roll(jnp.exp2(near - top), 1, 0).astype(BF16)
             return jnp.dot(own_vt, weights, preferred_element_type=F32)
 
-        def store(mixed):
-            result = (mixed[:head_size] / mixed[head_size : head_size + 1]).T.astype(BF16)
-            for h in range(heads):
-                o_ref[pl.ds(pl.multiple_of(i * qlength, qlength), qlength), h * head_size : (h + 1) * head_size] = (
-                    result[h * qlength : (h + 1) * qlength, :]
-                )
-
+        return qt, jnp.max(near, axis=0, keepdims=True), mix_near
+
+    def store(i, mixed):
+        result = (mixed[:head_size] / mixed[head_size : head_size + 1]).T.astype(BF16)
+        target = pl.ds(i * qlength if isinstance(i, int) else pl.multiple_of(i * qlength, qlength), qlength)
+        for h in range(heads):
+            o_ref[target, h * head_size : (h + 1) * head_size] = result[h * qlength : (h + 1) * qlength, :]
+
+    def shifted(i):
+        qt, top, mix_near = start(i)
         scores = jnp.dot(k_ref[...], qt, preferred_element_type=F32) * scale
-        weights = jnp.exp2(scores - near_top).astype(BF16)
-        mixed = jnp.dot(vt_ref[...], weights, preferred_element_type=F32) + mix_near(near_top)
-        store(mixed)
-        total = jnp.max(mixed[head_size : head_size + 1])
-
-        @pl.when(jnp.logical_not(total < TOTAL_MAX))
-        def _():
-            def part(j):
-                keys = k_ref[pl.ds(pl.multiple_of(j * chunk, chunk), chunk), :]
-                return jnp.dot(keys, qt, preferred_element_type=F32) * scale
-
-            def raise_top(j, top):
-                return jnp.maximum(top, jnp.max(part(j), axis=0, keepdims=True))
-
-            top = lax.fori_loop(0, context // chunk, raise_top, near_top)
-
-            def add(j, mixed):
-                weights = jnp.exp2(part(j) - top).astype(BF16)
-                values = vt_ref[:, pl.ds(pl.multiple_of(j * chunk, chunk), chunk)]
-                return mixed + jnp.dot(values, weights, preferred_element_type=F32)
-
-            store(lax.fori_loop(0, context // chunk, add, mix_near(top)))
-
+        weights = jnp.exp2(scores - top).astype(BF16)
+        mixed = jnp.dot(vt_ref[...], weights, preferred_element_type=F32) + mix_near(top)
+        store(i, mixed)
+        return jnp.where(mixed[head_size : head_size + 1] < TOTAL_MAX, 0.0, 1.0)
+
+    def by_maximum(i, carry):
+        qt, top, mix_near = start(i)
+
+        def part(j):
+            keys = k_ref[pl.ds(pl.multiple_of(j * chunk, chunk), chunk), :]
+            return jnp.dot(keys, qt, preferred_element_type=F32) * scale
+
+        def raise_top(j, top):
+            return jnp.maximum(top, jnp.max(part(j), axis=0, keepdims=True))
+
+        top = lax.fori_loop(0, context // chunk, raise_top, top)
+
+        def add(j, mixed):
+            weights = jnp.exp2(part(j) - top).astype(BF16)
+            values = vt_ref[:, pl.ds(pl.multiple_of(j * chunk, chunk), chunk)]
+            return mixed + jnp.dot(values, weights, preferred_element_type=F32)
+
+        store(i, lax.fori_loop(0, context // chunk, add, mix_near(top)))
         return carry
 
-    lax.fori_loop(0, x_ref.shape[0], one, 0, unroll=x_ref.shape[0] == CAP)
+    number = x_ref.shape[0]
+    if number == CAP:
+        large = functools.reduce(jnp.maximum, [shifted(i) for i in range(number)])
+    else:
+        large = lax.fori_loop(0, number, lambda i, large: jnp.maximum(large, shifted(i)), jnp.zeros((1, rows), F32))
+
+    @pl.when(jnp.max(large) > 0.5)
+    def _():
+        lax.fori_loop(0, number, by_maximum, 0)
 
 
 def attend(table, entry, x, keys, values_t, heads, qlength):
     number, _, head_size = x.shape
     context = keys.shape[1]
+    tables = [] if isinstance(entry, int) else [table]
     return pl.pallas_call(
         functools.partial(attend_kernel, entry=entry, heads=heads, qlength=qlength, chunk=512),
-        in_specs=[SMEM, VMEM, VMEM, VMEM],
+        in_specs=[SMEM] * len(tables) + [VMEM, VMEM, VMEM],
         out_specs=VMEM,
         out_shape=jax.ShapeDtypeStruct((number * qlength, heads * head_size), BF16),
         compiler_params=pltpu.CompilerParams(vmem_limit_bytes=20 << 20),
@@ -255,7 +270,7 @@
             transcendentals=number * qlength * heads * context,
         ),
         name="attend",
-    )(table, x, keys, values_t)
+    )(*tables, x, keys, values_t)
 
 
 def project_kernel(a_ref, w_ref, *out_refs, flips, tile):

time: 149 us -> 149 us (level)
  no operation moved by 1% of the time
where the time goes in v4:
time: 149 us
  Pallas kernels  105 us (70%)
  waiting for transfers between devices  27.4 us (18%)
  starting transfers between devices  14.7 us (10%)
    pallas_call x4, Pallas kernels, attend(): pl.pallas_call(functools.partial(attend_kernel, entry=entry, heads=heads,...  74.9 us
    ppermute x4, waiting for transfers between devices, project_out(): far = lax.ppermute(chip_sum, 'tensor', other_chip)  21.8 us
    pallas_call x12, Pallas kernels, project(): pl.pallas_call(functools.partial(project_kernel, flips=flips, tile=tile),...  17.9 us
    pallas_call x4, Pallas kernels, finish(): pl.pallas_call(functools.partial(finish_kernel, first=first, qlength=qlen...  6.31 us
    ppermute x4, starting transfers between devices, project_out(): far = lax.ppermute(chip_sum, 'tensor', other_chip)  5.52 us
    ppermute x2, waiting for transfers between devices, on_device(): lax.ppermute(returned[s], 'replica', by_shift(-shifts[s], replicas))  5.49 us
    ppermute x2, starting transfers between devices, on_device(): arrived[s] = lax.ppermute(packed[s], 'replica', by_shift(shift, replicas))  5.09 us
    pallas_call x1, Pallas kernels, pack(): pl.pallas_call(functools.partial(pack_kernel, route=route, heads=heads, q...  3.79 us
  transfers between devices with their start and end apart: 16, of which 4 were waited for; matrix products, arithmetic and copies ran while one was open for 0% of the time, Pallas kernels for 53%

profile of v4, /device:TPU:0, one launch (start us, length us, event | category | flops | bytes accessed | tf_op | source)
XLA Modules:
  0.0 148.7 jit_solution(11818268942443621031)
XLA Ops:
  0.0 3.8 %pack.3 = (s32[12]{0:T(128)S(1)}, s32[1]{0:T(128)}, bf16[2,640,128]{2,1,0:T(8,128)(2,1)S(1)}, bf16[2,640,128]{2,1,0:T(8,128)(2,1)S(1)}, bf16[2,640,128]{2,1,0:T(...) custom-call(s32[2,4]{1,0:T(2,128)} %bitcast.10, ...), custom_call_target="tpu_custom_call" | custom-call | bytes 4194304 | tf_op jit(solution)/shard_map/pack/pallas_call | solution.py:103
  3.8 18.4 %attend.6.after_ref.a_ref = bf16[128,1024]{1,0:T(8,128)(2,1)S(1)} custom-call(bf16[2,640,128]{2,1,0:T(8,128)(2,1)S(1)} %get-tuple-element.62.refs_0_, bf16[2,4096,128]{2,1,0:T(8,128)(2,1)S(1)} %get-tuple-element.60.refs_1_.keys_ref, bf16[2,144,4096]{2,1,0:T(8,128)(2,1)S(1)} %get-tuple-element.61.refs_2_.values_ref), custom_call_target="tpu_custom_call" | custom-call | flops 4294967296 | bytes 4194304 | tf_op jit(solution)/shard_map/attend/pallas_call | solution.py:261
  22.2 1.9 %project.29 = (bf16[128,2048]{1,0:T(8,128)(2,1)S(1)}, f32[128,2048]{1,0:T(8,128)S(1)}) custom-call(bf16[128,1024]{1,0:T(8,128)(2,1)S(1)} %attend.6.after_ref.a_ref, bf16[1024,8192]{1,0:T(8,128)(2,1)S(1)} %copy-done), custom_call_target="tpu_custom_call" | custom-call | flops 1073741824 | bytes 8388608 | tf_op jit(solution)/shard_map/project/pallas_call | solution.py:294
  26.0 3.1 %collective-permute-start.14 = (bf16[2,640,128]{2,1,0:T(8,128)(2,1)S(1)}, bf16[2,640,128]{2,1,0:T(8,128)(2,1)S(1)}, u32[]{:S(2)}, u32[]{:S(2)}) collective-permute-start(bf16[2,640,128]{2,1,0:T(8,128)(2,1)S(1)} %get-tuple-element.67), channel_id=1, source_target_pairs={{0,4},{4,8},{8,12},{12,0},{1,5},{5,9},{9,13},{13,1},{2,6},{6,10},{... | collective-permute-start | bytes 983048 | tf_op jit(solution)/shard_map/ppermute | solution.py:406
  29.1 2.1 %split.1 = (bf16[2,4096,128]{2,1,0:T(8,128)(2,1)S(1)}, bf16[2,144,4096]{2,1,0:T(8,128)(2,1)S(1)}) custom-call(bf16[16384,128]{1,0:T(8,128)(2,1)} %bitcast.6, bf16[2,4096,128]{2,1,0:T(8,128)(2,1)S(1)} %get-tuple-element.60.refs_1_.keys_ref, ...), custom_call_target="tpu_custom_call", output_to_operand_aliasing={{0}: (1, {}), {1}: (2, {})} | custom-call | bytes 4194304 | tf_op jit(solution)/shard_map/split/pallas_call | solution.py:172
  31.2 18.6 %attend.9.a_ref = bf16[128,1024]{1,0:T(8,128)(2,1)S(1)} custom-call(bf16[2,640,128]{2,1,0:T(8,128)(2,1)S(1)} %get-tuple-element.70.refs_0_, bf16[2,4096,128]{2,1,0:T(8,128)(2,1)S(1)} %get-tuple-element.63.refs_2_.refs_1_, bf16[2,144,4096]{2,1,0:T(8,128)(2,1)S(1)} %get-tuple-element.64.refs_3_.refs_2_), custom_call_target="tpu_custom_call" | custom-call | flops 4294967296 | bytes 4194304 | tf_op jit(solution)/shard_map/attend/pallas_call | solution.py:261
  49.8 1.9 %project.26 = (bf16[128,2048]{1,0:T(8,128)(2,1)S(1)}, f32[128,2048]{1,0:T(8,128)S(1)}) custom-call(bf16[128,1024]{1,0:T(8,128)(2,1)S(1)} %attend.9.a_ref, bf16[1024,8192]{1,0:T(8,128)(2,1)S(1)} %copy-done), custom_call_target="tpu_custom_call" | custom-call | flops 1073741824 | bytes 8388608 | tf_op jit(solution)/shard_map/project/pallas_call | solution.py:294
  53.6 2.0 %collective-permute-start.9 = (bf16[2,640,128]{2,1,0:T(8,128)(2,1)S(1)}, bf16[2,640,128]{2,1,0:T(8,128)(2,1)S(1)}, u32[]{:S(2)}, u32[]{:S(2)}) collective-permute-start(bf16[2,640,128]{2,1,0:T(8,128)(2,1)S(1)} %get-tuple-element.59), channel_id=1, source_target_pairs={{0,12},{4,0},{8,4},{12,8},{1,13},{5,1},{9,5},{13,9},{2,14},{6,2},{... | collective-permute-start | bytes 983048 | tf_op jit(solution)/shard_map/ppermute | solution.py:406
  55.6 19.0 %attend.8 = bf16[128,1024]{1,0:T(8,128)(2,1)S(1)} custom-call(s32[12]{0:T(128)S(1)} %get-tuple-element.58.refs_0_.table_ref, bf16[2,640,128]{2,1,0:T(8,128)(2,1)S(1)} %collective-permute-done.14.refs_1_, bf16[2,4096,128]{2,1,0:T(8,128)(2,1)S(1)} %get-tuple-element.63.refs_2_.refs_1_, bf16[2,144,4096]{2,1,0:T(8,128)(2,1)S(1)} %get-tuple-element.64.refs_3_.refs_2_), custom_call_target="tpu_custom_call" | custom-call | flops 4294967296 | bytes 4194304 | tf_op jit(solution)/shard_map/attend/pallas_call | solution.py:261
  74.6 2.1 %collective-permute-start.15 = (bf16[128,1024]{1,0:T(8,128)(2,1)S(1)}, bf16[128,1024]{1,0:T(8,128)(2,1)S(1)}, u32[]{:S(2)}, u32[]{:S(2)}) collective-permute-start(bf16[128,1024]{1,0:T(8,128)(2,1)S(1)} %attend.8), channel_id=1, source_target_pairs={{0,12},{4,0},{8,4},{12,8},{1,13},{5,1},{9,5},{13,9},{2,14},{6,2},{... | collective-permute-start | bytes 786440 | tf_op jit(solution)/shard_map/ppermute | solution.py:412
  76.7 19.0 %attend.7 = bf16[128,1024]{1,0:T(8,128)(2,1)S(1)} custom-call(s32[12]{0:T(128)S(1)} %get-tuple-element.58.refs_0_.table_ref, bf16[2,640,128]{2,1,0:T(8,128)(2,1)S(1)} %collective-permute-done.9.refs_1_, bf16[2,4096,128]{2,1,0:T(8,128)(2,1)S(1)} %get-tuple-element.63.refs_2_.refs_1_, bf16[2,144,4096]{2,1,0:T(8,128)(2,1)S(1)} %get-tuple-element.64.refs_3_.refs_2_), custom_call_target="tpu_custom_call" | custom-call | flops 4294967296 | bytes 4194304 | tf_op jit(solution)/shard_map/attend/pallas_call | solution.py:261
  96.1 1.8 %collective-permute-start.24 = (bf16[128,2048]{1,0:T(8,128)(2,1)S(1)}, bf16[128,2048]{1,0:T(8,128)(2,1)S(1)}, u32[]{:S(2)}, u32[]{:S(2)}) collective-permute-start(bf16[128,2048]{1,0:T(8,128)(2,1)S(1)} %add_convert_fusion.1), channel_id=1, source_target_pairs={{0,2},{1,3},{2,0},{3,1},{4,6},{5,7},{6,4},{7,5},{8,10},{9,11},{10,... | collective-permute-start | bytes 1572872 | tf_op jit(solution)/shard_map/ppermute | solution.py:368
  97.9 1.9 %project.23 = (bf16[128,2048]{1,0:T(8,128)(2,1)S(1)}, f32[128,2048]{1,0:T(8,128)S(1)}) custom-call(bf16[128,1024]{1,0:T(8,128)(2,1)S(1)} %collective-permute-done.15.a_ref, bf16[1024,8192]{1,0:T(8,128)(2,1)S(1)} %copy-done), custom_call_target="tpu_custom_call" | custom-call | flops 1073741824 | bytes 8388608 | tf_op jit(solution)/shard_map/project/pallas_call | solution.py:294
  100.0 5.5 %collective-permute-done.10.a_ref = bf16[128,1024]{1,0:T(8,128)(2,1)S(1)} collective-permute-done((bf16[128,1024]{1,0:T(8,128)(2,1)S(1)}, bf16[128,1024]{1,0:T(8,128)(2,1)S(1)}, u32[]{:S(2)}, u32[]{:S(2)}) %collective-permute-start.10) | collective-permute-done | bytes 262176 | tf_op jit(solution)/shard_map/ppermute | solution.py:412
  105.5 1.9 %project.20 = (bf16[128,2048]{1,0:T(8,128)(2,1)S(1)}, f32[128,2048]{1,0:T(8,128)S(1)}) custom-call(bf16[128,1024]{1,0:T(8,128)(2,1)S(1)} %collective-permute-done.10.a_ref, bf16[1024,8192]{1,0:T(8,128)(2,1)S(1)} %copy-done), custom_call_target="tpu_custom_call" | custom-call | flops 1073741824 | bytes 8388608 | tf_op jit(solution)/shard_map/project/pallas_call | solution.py:294
  110.0 1.6 %collective-permute-start.21 = (bf16[128,2048]{1,0:T(8,128)(2,1)S(1)}, bf16[128,2048]{1,0:T(8,128)(2,1)S(1)}, u32[]{:S(2)}, u32[]{:S(2)}) collective-permute-start(bf16[128,2048]{1,0:T(8,128)(2,1)S(1)} %add_convert_fusion.2), channel_id=1, source_target_pairs={{0,2},{1,3},{2,0},{3,1},{4,6},{5,7},{6,4},{7,5},{8,10},{9,11},{10,... | collective-permute-start | bytes 1572872 | tf_op jit(solution)/shard_map/ppermute | solution.py:368
  112.8 1.6 %collective-permute-start.13 = (bf16[128,2048]{1,0:T(8,128)(2,1)S(1)}, bf16[128,2048]{1,0:T(8,128)(2,1)S(1)}, u32[]{:S(2)}, u32[]{:S(2)}) collective-permute-start(bf16[128,2048]{1,0:T(8,128)(2,1)S(1)} %add_convert_fusion.4), channel_id=1, source_target_pairs={{0,2},{1,3},{2,0},{3,1},{4,6},{5,7},{6,4},{7,5},{8,10},{9,11},{10,... | collective-permute-start | bytes 1572872 | tf_op jit(solution)/shard_map/ppermute | solution.py:368
  120.3 1.6 %finish.6.refs_0_ = bf16[512,2048]{1,0:T(8,128)(2,1)} custom-call(s32[12]{0:T(128)S(1)} %get-tuple-element.58.refs_0_.table_ref, s32[1,8]{1,0:T(1,128)S(1)} %copy-done.1, f32[128,2048]{1,0:T(8,128)S(1)} %project.27.kept_ref, bf16[128,2048]{1,0:T(8,128)(2,1)S(1)} %collective-permute-done.22.core_ref, bf16[128,2048]{1,0:T(8,128)(2,1)S(1)} %collective-permute-done.24.far_ref), custom_call_target="tpu_custom_call" | custom-call | bytes 2621440 | tf_op jit(solution)/shard_map/finish/pallas_call | solution.py:338
  121.9 3.0 %collective-permute-done.21.far_ref = bf16[128,2048]{1,0:T(8,128)(2,1)S(1)} collective-permute-done((bf16[128,2048]{1,0:T(8,128)(2,1)S(1)}, bf16[128,2048]{1,0:T(8,128)(2,1)S(1)}, u32[]{:S(2)}, u32[]{:S(2)}) %collective-permute-start.21) | collective-permute-done | bytes 524320 | tf_op jit(solution)/shard_map/ppermute | solution.py:368
  124.9 1.6 %finish.7.refs_0_ = bf16[512,2048]{1,0:T(8,128)(2,1)} custom-call(s32[12]{0:T(128)S(1)} %get-tuple-element.58.refs_0_.table_ref, s32[1,8]{1,0:T(1,128)S(1)} %copy-done.1, f32[128,2048]{1,0:T(8,128)S(1)} %project.24.kept_ref, bf16[128,2048]{1,0:T(8,128)(2,1)S(1)} %collective-permute-done.19.core_ref, ...), custom_call_target="tpu_custom_call", output_to_operand_aliasing={{}: (5, {})} | custom-call | bytes 2621440 | tf_op jit(solution)/shard_map/finish/pallas_call | solution.py:338
  126.5 9.6 %collective-permute-done.18.far_ref = bf16[128,2048]{1,0:T(8,128)(2,1)S(1)} collective-permute-done((bf16[128,2048]{1,0:T(8,128)(2,1)S(1)}, bf16[128,2048]{1,0:T(8,128)(2,1)S(1)}, u32[]{:S(2)}, u32[]{:S(2)}) %collective-permute-start.18) | collective-permute-done | bytes 524320 | tf_op jit(solution)/shard_map/ppermute | solution.py:368
  136.1 1.6 %finish.8.refs_0_ = bf16[512,2048]{1,0:T(8,128)(2,1)} custom-call(s32[12]{0:T(128)S(1)} %get-tuple-element.58.refs_0_.table_ref, s32[1,8]{1,0:T(1,128)S(1)} %copy-done.1, f32[128,2048]{1,0:T(8,128)S(1)} %project.21.kept_ref, bf16[128,2048]{1,0:T(8,128)(2,1)S(1)} %collective-permute-done.16.core_ref, ...), custom_call_target="tpu_custom_call", output_to_operand_aliasing={{}: (5, {})} | custom-call | bytes 2621440 | tf_op jit(solution)/shard_map/finish/pallas_call | solution.py:338
  137.7 9.2 %collective-permute-done.13.far_ref = bf16[128,2048]{1,0:T(8,128)(2,1)S(1)} collective-permute-done((bf16[128,2048]{1,0:T(8,128)(2,1)S(1)}, bf16[128,2048]{1,0:T(8,128)(2,1)S(1)}, u32[]{:S(2)}, u32[]{:S(2)}) %collective-permute-start.13) | collective-permute-done | bytes 524320 | tf_op jit(solution)/shard_map/ppermute | solution.py:368
  146.9 1.6 %finish.9 = bf16[512,2048]{1,0:T(8,128)(2,1)} custom-call(s32[12]{0:T(128)S(1)} %get-tuple-element.58.refs_0_.table_ref, s32[1,8]{1,0:T(1,128)S(1)} %copy-done.1, f32[128,2048]{1,0:T(8,128)S(1)} %project.18.kept_ref, bf16[128,2048]{1,0:T(8,128)(2,1)S(1)} %collective-permute-done.11.core_ref, ...), custom_call_target="tpu_custom_call", output_to_operand_aliasing={{}: (5, {})} | custom-call | bytes 2621440 | tf_op jit(solution)/shard_map/finish/pallas_call | solution.py:338
  (39 shorter events, 13.6 us)
Async XLA Ops:
  0.0 22.2 %copy-start = (bf16[1024,8192]{1,0:T(8,128)(2,1)S(1)}, bf16[1024,8192]{1,0:T(8,128)(2,1)}, u32[]{:S(2)}) copy-start(bf16[1024,8192]{1,0:T(8,128)(2,1)} %w_ref.23) | copy-start | bytes 50331652
  24.1 71.6 %collective-permute-start.23 = (bf16[128,2048]{1,0:T(8,128)(2,1)S(1)}, bf16[128,2048]{1,0:T(8,128)(2,1)S(1)}, u32[]{:S(2)}, u32[]{:S(2)}) collective-permute-start(bf16[128,2048]{1,0:T(8,128)(2,1)S(1)} %get-tuple-element.74), channel_id=1, source_target_pairs={{0,1},{1,0},{2,3},{3,2},{4,5},{5,4},{6,7},{7,6},{8,9},{9,8},{10,11... | collective-permute-start | bytes 1572872 | tf_op jit(solution)/shard_map/ppermute | solution.py:364
  25.9 86.2 %collective-permute-start.22 = (bf16[128,2048]{1,0:T(8,128)(2,1)S(1)}, bf16[128,2048]{1,0:T(8,128)(2,1)S(1)}, u32[]{:S(2)}, u32[]{:S(2)}) collective-permute-start(bf16[128,2048]{1,0:T(8,128)(2,1)S(1)} %project.28), channel_id=1, source_target_pairs={{0,1},{1,0},{2,3},{3,2},{4,5},{5,4},{6,7},{7,6},{8,9},{9,8},{10,11... | collective-permute-start | bytes 1572872 | tf_op jit(solution)/shard_map/ppermute | solution.py:366
  26.0 27.6 %collective-permute-start.14 = (bf16[2,640,128]{2,1,0:T(8,128)(2,1)S(1)}, bf16[2,640,128]{2,1,0:T(8,128)(2,1)S(1)}, u32[]{:S(2)}, u32[]{:S(2)}) collective-permute-start(bf16[2,640,128]{2,1,0:T(8,128)(2,1)S(1)} %get-tuple-element.67), channel_id=1, source_target_pairs={{0,4},{4,8},{8,12},{12,0},{1,5},{5,9},{9,13},{13,1},{2,6},{6,10},{... | collective-permute-start | bytes 983048 | tf_op jit(solution)/shard_map/ppermute | solution.py:406
  51.6 48.1 %collective-permute-start.20 = (bf16[128,2048]{1,0:T(8,128)(2,1)S(1)}, bf16[128,2048]{1,0:T(8,128)(2,1)S(1)}, u32[]{:S(2)}, u32[]{:S(2)}) collective-permute-start(bf16[128,2048]{1,0:T(8,128)(2,1)S(1)} %get-tuple-element.72), channel_id=1, source_target_pairs={{0,1},{1,0},{2,3},{3,2},{4,5},{5,4},{6,7},{7,6},{8,9},{9,8},{10,11... | collective-permute-start | bytes 1572872 | tf_op jit(solution)/shard_map/ppermute | solution.py:364
  53.0 59.7 %collective-permute-start.19 = (bf16[128,2048]{1,0:T(8,128)(2,1)S(1)}, bf16[128,2048]{1,0:T(8,128)(2,1)S(1)}, u32[]{:S(2)}, u32[]{:S(2)}) collective-permute-start(bf16[128,2048]{1,0:T(8,128)(2,1)S(1)} %project.25), channel_id=1, source_target_pairs={{0,1},{1,0},{2,3},{3,2},{4,5},{5,4},{6,7},{7,6},{8,9},{9,8},{10,11... | collective-permute-start | bytes 1572872 | tf_op jit(solution)/shard_map/ppermute | solution.py:366
  53.6 21.0 %collective-permute-start.9 = (bf16[2,640,128]{2,1,0:T(8,128)(2,1)S(1)}, bf16[2,640,128]{2,1,0:T(8,128)(2,1)S(1)}, u32[]{:S(2)}, u32[]{:S(2)}) collective-permute-start(bf16[2,640,128]{2,1,0:T(8,128)(2,1)S(1)} %get-tuple-element.59), channel_id=1, source_target_pairs={{0,12},{4,0},{8,4},{12,8},{1,13},{5,1},{9,5},{13,9},{2,14},{6,2},{... | collective-permute-start | bytes 983048 | tf_op jit(solution)/shard_map/ppermute | solution.py:406
  74.6 21.5 %collective-permute-start.15 = (bf16[128,1024]{1,0:T(8,128)(2,1)S(1)}, bf16[128,1024]{1,0:T(8,128)(2,1)S(1)}, u32[]{:S(2)}, u32[]{:S(2)}) collective-permute-start(bf16[128,1024]{1,0:T(8,128)(2,1)S(1)} %attend.8), channel_id=1, source_target_pairs={{0,12},{4,0},{8,4},{12,8},{1,13},{5,1},{9,5},{13,9},{2,14},{6,2},{... | collective-permute-start | bytes 786440 | tf_op jit(solution)/shard_map/ppermute | solution.py:412
  95.7 9.8 %collective-permute-start.10 = (bf16[128,1024]{1,0:T(8,128)(2,1)S(1)}, bf16[128,1024]{1,0:T(8,128)(2,1)S(1)}, u32[]{:S(2)}, u32[]{:S(2)}) collective-permute-start(bf16[128,1024]{1,0:T(8,128)(2,1)S(1)} %attend.7), channel_id=1, source_target_pairs={{0,4},{4,8},{8,12},{12,0},{1,5},{5,9},{9,13},{13,1},{2,6},{6,10},{... | collective-permute-start | bytes 786440 | tf_op jit(solution)/shard_map/ppermute | solution.py:412
  96.1 16.7 %collective-permute-start.24 = (bf16[128,2048]{1,0:T(8,128)(2,1)S(1)}, bf16[128,2048]{1,0:T(8,128)(2,1)S(1)}, u32[]{:S(2)}, u32[]{:S(2)}) collective-permute-start(bf16[128,2048]{1,0:T(8,128)(2,1)S(1)} %add_convert_fusion.1), channel_id=1, source_target_pairs={{0,2},{1,3},{2,0},{3,1},{4,6},{5,7},{6,4},{7,5},{8,10},{9,11},{10,... | collective-permute-start | bytes 1572872 | tf_op jit(solution)/shard_map/ppermute | solution.py:368
  99.8 10.3 %collective-permute-start.17 = (bf16[128,2048]{1,0:T(8,128)(2,1)S(1)}, bf16[128,2048]{1,0:T(8,128)(2,1)S(1)}, u32[]{:S(2)}, u32[]{:S(2)}) collective-permute-start(bf16[128,2048]{1,0:T(8,128)(2,1)S(1)} %get-tuple-element.69), channel_id=1, source_target_pairs={{0,1},{1,0},{2,3},{3,2},{4,5},{5,4},{6,7},{7,6},{8,9},{9,8},{10,11... | collective-permute-start | bytes 1572872 | tf_op jit(solution)/shard_map/ppermute | solution.py:364
  107.3 4.4 %collective-permute-start.12 = (bf16[128,2048]{1,0:T(8,128)(2,1)S(1)}, bf16[128,2048]{1,0:T(8,128)(2,1)S(1)}, u32[]{:S(2)}, u32[]{:S(2)}) collective-permute-start(bf16[128,2048]{1,0:T(8,128)(2,1)S(1)} %get-tuple-element.66), channel_id=1, source_target_pairs={{0,1},{1,0},{2,3},{3,2},{4,5},{5,4},{6,7},{7,6},{8,9},{9,8},{10,11... | collective-permute-start | bytes 1572872 | tf_op jit(solution)/shard_map/ppermute | solution.py:364
  110.0 14.9 %collective-permute-start.21 = (bf16[128,2048]{1,0:T(8,128)(2,1)S(1)}, bf16[128,2048]{1,0:T(8,128)(2,1)S(1)}, u32[]{:S(2)}, u32[]{:S(2)}) collective-permute-start(bf16[128,2048]{1,0:T(8,128)(2,1)S(1)} %add_convert_fusion.2), channel_id=1, source_target_pairs={{0,2},{1,3},{2,0},{3,1},{4,6},{5,7},{6,4},{7,5},{8,10},{9,11},{10,... | collective-permute-start | bytes 1572872 | tf_op jit(solution)/shard_map/ppermute | solution.py:368
  111.8 14.7 %collective-permute-start.16 = (bf16[128,2048]{1,0:T(8,128)(2,1)S(1)}, bf16[128,2048]{1,0:T(8,128)(2,1)S(1)}, u32[]{:S(2)}, u32[]{:S(2)}) collective-permute-start(bf16[128,2048]{1,0:T(8,128)(2,1)S(1)} %project.22), channel_id=1, source_target_pairs={{0,1},{1,0},{2,3},{3,2},{4,5},{5,4},{6,7},{7,6},{8,9},{9,8},{10,11... | collective-permute-start | bytes 1572872 | tf_op jit(solution)/shard_map/ppermute | solution.py:366
  112.2 23.9 %collective-permute-start.18 = (bf16[128,2048]{1,0:T(8,128)(2,1)S(1)}, bf16[128,2048]{1,0:T(8,128)(2,1)S(1)}, u32[]{:S(2)}, u32[]{:S(2)}) collective-permute-start(bf16[128,2048]{1,0:T(8,128)(2,1)S(1)} %add_convert_fusion.3), channel_id=1, source_target_pairs={{0,2},{1,3},{2,0},{3,1},{4,6},{5,7},{6,4},{7,5},{8,10},{9,11},{10,... | collective-permute-start | bytes 1572872 | tf_op jit(solution)/shard_map/ppermute | solution.py:368
  112.8 24.9 %collective-permute-start.11 = (bf16[128,2048]{1,0:T(8,128)(2,1)S(1)}, bf16[128,2048]{1,0:T(8,128)(2,1)S(1)}, u32[]{:S(2)}, u32[]{:S(2)}) collective-permute-start(bf16[128,2048]{1,0:T(8,128)(2,1)S(1)} %project.19), channel_id=1, source_target_pairs={{0,1},{1,0},{2,3},{3,2},{4,5},{5,4},{6,7},{7,6},{8,9},{9,8},{10,11... | collective-permute-start | bytes 1572872 | tf_op jit(solution)/shard_map/ppermute | solution.py:366
  112.8 34.1 %collective-permute-start.13 = (bf16[128,2048]{1,0:T(8,128)(2,1)S(1)}, bf16[128,2048]{1,0:T(8,128)(2,1)S(1)}, u32[]{:S(2)}, u32[]{:S(2)}) collective-permute-start(bf16[128,2048]{1,0:T(8,128)(2,1)S(1)} %add_convert_fusion.4), channel_id=1, source_target_pairs={{0,2},{1,3},{2,0},{3,1},{4,6},{5,7},{6,4},{7,5},{8,10},{9,11},{10,... | collective-permute-start | bytes 1572872 | tf_op jit(solution)/shard_map/ppermute | solution.py:368
  118.9 1.3 copy-start.1

commit v5 on v4

--- a/solution.py
+++ b/solution.py
@@ -18,21 +18,23 @@
 SMEM = pl.BlockSpec(memory_space=pltpu.SMEM)
 
 
-def pack_kernel(stored_hbm, ids_hbm, q_hbm, own_hbm, kv_hbm, table_ref, failed_ref, *refs, route, heads, qlength):
-    number = len(refs) - 10
+def pack_kernel(
+    stored_hbm, ids_hbm, counts_hbm, q_hbm, own_hbm, kv_hbm, table_ref, failed_ref, slots_ref, *refs, route, heads, qlength
+):
+    number = len(refs) - 11
     out_refs, (k_ref, vt_ref) = refs[:number], refs[number : number + 2]
-    stored_ref, ids_ref, q_ref, own_ref, sems, pairs_ref, wide_ref, kv_sems = refs[number + 2 :]
+    stored_ref, ids_ref, counts_ref, q_ref, own_ref, sems, pairs_ref, wide_ref, kv_sems = refs[number + 2 :]
     head_size = own_ref.shape[1]
     questions = ids_ref.shape[1]
-    pairs = ((stored_hbm, stored_ref), (ids_hbm, ids_ref), (q_hbm, q_ref), (own_hbm, own_ref))
+    pairs = ((stored_hbm, stored_ref), (ids_hbm, ids_ref), (counts_hbm, counts_ref), (q_hbm, q_ref), (own_hbm, own_ref))
     copies = [pltpu.make_async_copy(source, target, sems.at[i]) for i, (source, target) in enumerate(pairs)]
     kv_copies = split_copies(kv_hbm, pairs_ref, kv_sems, 0)
     for copy in copies + kv_copies:
         copy.start()
-    for copy in copies[:2]:
+    for copy in copies[:3]:
         copy.wait()
     places = []
-    for s, haystack in enumerate(route(stored_ref, table_ref, failed_ref)):
+    for s, haystack in enumerate(route(stored_ref, slots_ref, failed_ref)):
         count = jnp.int32(0)
         found = [jnp.int32(-1)] * CAP
         for i in range(questions):
@@ -43,7 +45,9 @@
         for j in range(CAP):
             table_ref[s * CAP + j] = found[j]
         places.append([jnp.maximum(place, 0) for place in found])
-    for copy in copies[2:]:
+        for j, place in enumerate(places[s]):
+            table_ref[(number + s) * CAP + j] = counts_ref[0, place]
+    for copy in copies[3:]:
         copy.wait()
     for s, out_ref in enumerate(out_refs):
         for j, place in enumerate(places[s]):
@@ -55,13 +59,14 @@
     split_arrived(kv_copies, k_ref, vt_ref, pairs_ref, wide_ref, 0)
 
 
-def route_first(replicas, stored_ref, table_ref, failed_ref):
+def route_first(replicas, stored_ref, slots_ref, failed_ref):
     failed_ref[0] = jnp.int32(0)
+    slots_ref[...] = jnp.zeros_like(slots_ref)
     me = lax.axis_index("replica")
     return [stored_ref[0, lax.rem(me + s, replicas)] for s in range(replicas)]
 
 
-def route_near(stored_ref, table_ref, failed_ref):
+def route_near(stored_ref, slots_ref, failed_ref):
     me = lax.axis_index("replica")
 
     def held(replica):
@@ -86,40 +91,42 @@
     failed = jnp.int32(0)
     for _, _, done in plans:
         failed = jnp.where(done, failed, 1)
-    table_ref[10] = plans[3][0][0]
-    table_ref[11] = plans[1][0][1]
+    for i, slot in enumerate((plans[3][0][0], plans[1][0][1])):
+        slots_ref[i] = jnp.full(slots_ref.shape[1:], slot, jnp.int32).astype(F32)
     failed_ref[0] = failed
     return held(me) + plans[0][1]
 
 
-def pack(stored, ids, queries, own, pairs, context, slots, phases, route):
+def pack(stored, ids, counts, queries, own, pairs, context, slots, phases, route):
     questions = ids.shape[1]
     head_size = own.shape[1]
     qlength = queries.shape[0] // questions
     heads = queries.shape[1] // head_size
     rows = heads * qlength + 2 * qlength
-    arguments = [pltpu.with_memory_space_constraint(x, pltpu.HBM) for x in (stored, ids, queries, own, pairs)]
+    arguments = [pltpu.with_memory_space_constraint(x, pltpu.HBM) for x in (stored, ids, counts, queries, own, pairs)]
     split_out, split_scratch = split_shapes(context, head_size, slots)
     out = pl.pallas_call(
         functools.partial(pack_kernel, route=route, heads=heads, qlength=qlength),
-        in_specs=[pl.BlockSpec(memory_space=pltpu.HBM)] * 5,
-        out_specs=[SMEM, SMEM] + [VMEM] * (phases + 2),
-        out_shape=[jax.ShapeDtypeStruct((size,), jnp.int32) for size in (phases * (CAP + 1), 1)]
+        in_specs=[pl.BlockSpec(memory_space=pltpu.HBM)] * 6,
+        out_specs=[SMEM, SMEM] + [VMEM] * (phases + 3),
+        out_shape=[jax.ShapeDtypeStruct((size,), jnp.int32) for size in (2 * phases * CAP, 1)]
+        + [jax.ShapeDtypeStruct((2, 8, 128), F32)]
         + [jax.ShapeDtypeStruct((CAP, rows, head_size), BF16)] * phases
         + split_out,
         scratch_shapes=[
             pltpu.SMEM(stored.shape, jnp.int32),
             pltpu.SMEM(ids.shape, jnp.int32),
+            pltpu.SMEM(counts.shape, jnp.int32),
             pltpu.VMEM(queries.shape, BF16),
             pltpu.VMEM(own.shape, BF16),
-            pltpu.SemaphoreType.DMA((4,)),
+            pltpu.SemaphoreType.DMA((5,)),
             *split_scratch,
         ],
         compiler_params=pltpu.CompilerParams(vmem_limit_bytes=16 << 20),
         cost_estimate=pl.CostEstimate(flops=0, bytes_accessed=4 << 20, transcendentals=0),
         name="pack",
     )(*arguments)
-    return out[0], out[1], out[2:-2], out[-2:]
+    return *out[:3], out[3:-2], out[-2:]
 
 
 def split_copies(x_ref, pairs_ref, sems, slot):
@@ -187,8 +194,8 @@
         x_ref, keys_ref, values_ref, o_ref = refs
         slot = entry
     else:
-        table_ref, x_ref, keys_ref, values_ref, o_ref = refs
-        slot = table_ref[entry[0]]
+        slots_ref, x_ref, keys_ref, values_ref, o_ref = refs
+        slot = jnp.max(slots_ref[entry[0]]).astype(jnp.int32)
     k_ref, vt_ref = keys_ref.at[slot], values_ref.at[slot]
     context, head_size = k_ref.shape
     scale = LOG2E / math.sqrt(head_size)
@@ -254,13 +261,13 @@
         lax.fori_loop(0, number, by_maximum, 0)
 
 
-def attend(table, entry, x, keys, values_t, heads, qlength):
+def attend(slots, entry, x, keys, values_t, heads, qlength):
     number, _, head_size = x.shape
     context = keys.shape[1]
-    tables = [] if isinstance(entry, int) else [table]
+    tables = [] if isinstance(entry, int) else [slots]
     return pl.pallas_call(
         functools.partial(attend_kernel, entry=entry, heads=heads, qlength=qlength, chunk=512),
-        in_specs=[SMEM] * len(tables) + [VMEM, VMEM, VMEM],
+        in_specs=[VMEM] * (len(tables) + 3),
         out_specs=VMEM,
         out_shape=jax.ShapeDtypeStruct((number * qlength, heads * head_size), BF16),
         compiler_params=pltpu.CompilerParams(vmem_limit_bytes=20 << 20),
@@ -306,11 +313,11 @@
     )(rows, weight)
 
 
-def finish_kernel(table_ref, counts_ref, kept_ref, core_ref, far_ref, *refs, first, qlength, tile):
+def finish_kernel(table_ref, kept_ref, core_ref, far_ref, *refs, first, qlength, tile):
     o_ref, block_ref, sems = refs[-3:]
     number, _, columns = block_ref.shape
     places = [jnp.maximum(table_ref[first + i], 0) for i in range(number)]
-    counts = [counts_ref[0, place] for place in places]
+    counts = [table_ref[table_ref.shape[0] // 2 + first + i] for i in range(number)]
     t = lax.broadcasted_iota(jnp.int32, (qlength, tile), 0)
 
     def one(j, carry):
@@ -331,21 +338,21 @@
         copy.wait()
 
 
-def finish(table, counts, kept, from_core, from_far, first, previous, rows, qlength, tile):
+def finish(table, kept, from_core, from_far, first, previous, rows, qlength, tile):
     number, columns = kept.shape[0] // qlength, kept.shape[1]
     extra = [] if previous is None else [pltpu.with_memory_space_constraint(previous, pltpu.HBM)]
     hbm = pl.BlockSpec(memory_space=pltpu.HBM)
     return pl.pallas_call(
         functools.partial(finish_kernel, first=first, qlength=qlength, tile=tile),
-        in_specs=[SMEM, SMEM, VMEM, VMEM, VMEM] + [hbm] * len(extra),
+        in_specs=[SMEM, VMEM, VMEM, VMEM] + [hbm] * len(extra),
         out_specs=hbm,
         out_shape=pltpu.HBM((rows, columns), BF16),
         scratch_shapes=[pltpu.VMEM((number, qlength, columns), BF16), pltpu.SemaphoreType.DMA((number,))],
-        input_output_aliases={5: 0} if extra else {},
+        input_output_aliases={4: 0} if extra else {},
         compiler_params=pltpu.CompilerParams(vmem_limit_bytes=12 << 20),
         cost_estimate=pl.CostEstimate(flops=0, bytes_accessed=10 * kept.shape[0] * columns, transcendentals=0),
         name="finish",
-    )(table, counts, kept, from_core, from_far, *extra)
+    )(table, kept, from_core, from_far, *extra)
 
 
 def by_shift(shift, replicas):
@@ -356,7 +363,7 @@
     return groups <= 2 and replicas == 4 and shares == 4
 
 
-def project_out(table, counts, results, weight, shares, first, out, rows, qlength):
+def project_out(table, results, weight, shares, first, out, rows, qlength):
     other_core = [(i, i ^ 1) for i in range(shares)]
     other_chip = [(i, i ^ 2) for i in range(shares)]
     tile = 512
@@ -367,15 +374,17 @@
     chip_sum = (far_keep + far_core.astype(F32)).astype(BF16)
     far = lax.ppermute(chip_sum, "tensor", other_chip)
     (near_keep,) = project(results, weight, shares, tile, (0,), (F32,))
-    return finish(table, counts, near_keep, near_core, far, first, out, rows, qlength, tile)
-
-
-def answer_by_first_slots(queries, own, pairs, context, stored, ids, heads, qlength):
+    return finish(table, near_keep, near_core, far, first, out, rows, qlength, tile)
+
+
+def answer_by_first_slots(queries, own, pairs, context, stored, ids, counts, heads, qlength):
     replicas = stored.shape[1]
     route = functools.partial(route_first, replicas)
-    table, _, packed, (keys, values_t) = pack(stored, ids, queries, own, pairs, context, 1, replicas, route)
+    table, _, _, packed, (keys, values_t) = pack(
+        stored, ids, counts, queries, own, pairs, context, 1, replicas, route
+    )
     arrived = [packed[0]] + [lax.ppermute(packed[s], "replica", by_shift(s, replicas)) for s in range(1, replicas)]
-    result = attend(table, 0, jnp.concatenate(arrived), keys, values_t, heads, qlength)
+    result = attend(None, 0, jnp.concatenate(arrived), keys, values_t, heads, qlength)
     parts = result.reshape(replicas, CAP * qlength, -1)
     returned = [parts[0]] + [lax.ppermute(parts[s], "replica", by_shift(-s, replicas)) for s in range(1, replicas)]
     return table, jnp.concatenate(returned)
@@ -397,8 +406,8 @@
     stored = stored.T
 
     if small_slice(groups, replicas, shares) and replicas * CAP == questions and slots == 2:
-        table, failed, packed, (keys, values_t) = pack(
-            stored, ids, queries, own, pairs, context, slots, 4, route_near
+        table, failed, chosen, packed, (keys, values_t) = pack(
+            stored, ids, token_counts, queries, own, pairs, context, slots, 4, route_near
         )
         arrived, returned = dict(enumerate(packed)), {}
         shifts = {2: 1, 3: -1}
@@ -407,20 +416,20 @@
         for s in range(4):
             if s == 1:
                 keys, values_t = split(pairs, keys, values_t, 1, returned[0])
-            returned[s] = attend(table, s if s < 2 else (8 + s,), arrived[s], keys, values_t, heads, qlength)
+            returned[s] = attend(chosen, s if s < 2 else (s - 2,), arrived[s], keys, values_t, heads, qlength)
             if s in shifts:
                 returned[s] = lax.ppermute(returned[s], "replica", by_shift(-shifts[s], replicas))
         out = None
         for s in range(4):
-            out = project_out(table, token_counts, returned[s], out_weight, shares, s * CAP, out, rows, qlength)
+            out = project_out(table, returned[s], out_weight, shares, s * CAP, out, rows, qlength)
 
         def again():
-            table, results = answer_by_first_slots(queries, own, pairs, context, stored, ids, heads, qlength)
-            return project_out(table, token_counts, results, out_weight, shares, 0, None, rows, qlength)
+            table, results = answer_by_first_slots(queries, own, pairs, context, stored, ids, token_counts, heads, qlength)
+            return project_out(table, results, out_weight, shares, 0, None, rows, qlength)
 
         return lax.cond(failed[0] > 0, again, lambda: out)
 
-    table, results = answer_by_first_slots(queries, own, pairs, context, stored, ids, heads, qlength)
+    table, results = answer_by_first_slots(queries, own, pairs, context, stored, ids, token_counts, heads, qlength)
     blocks = results.reshape(replicas * CAP, qlength, -1)
     match = table[None, : replicas * CAP] == jnp.arange(questions, dtype=jnp.int32)[:, None]
     position = jnp.argmax(match.astype(jnp.int32), axis=1)

time: 149 us -> 148 us (level)
  no operation moved by 1% of the time
where the time goes in v5:
time: 148 us
  Pallas kernels  104 us (70%)
  waiting for transfers between devices  27.5 us (19%)
  starting transfers between devices  14.6 us (10%)
    pallas_call x4, Pallas kernels, attend(): pl.pallas_call(functools.partial(attend_kernel, entry=entry, heads=heads,...  73.9 us
    ppermute x4, waiting for transfers between devices, project_out(): far = lax.ppermute(chip_sum, 'tensor', other_chip)  21.9 us
    pallas_call x12, Pallas kernels, project(): pl.pallas_call(functools.partial(project_kernel, flips=flips, tile=tile),...  17.7 us
    pallas_call x4, Pallas kernels, finish(): pl.pallas_call(functools.partial(finish_kernel, first=first, qlength=qlen...  6.32 us
    ppermute x2, waiting for transfers between devices, on_device(): lax.ppermute(returned[s], 'replica', by_shift(-shifts[s], replicas))  5.5 us
    ppermute x4, starting transfers between devices, project_out(): far = lax.ppermute(chip_sum, 'tensor', other_chip)  5.5 us
    ppermute x2, starting transfers between devices, on_device(): arrived[s] = lax.ppermute(packed[s], 'replica', by_shift(shift, replicas))  5.04 us
    pallas_call x1, Pallas kernels, pack(): pl.pallas_call(functools.partial(pack_kernel, route=route, heads=heads, q...  3.79 us
  transfers between devices with their start and end apart: 16, of which 4 were waited for; matrix products, arithmetic and copies ran while one was open for 0% of the time, Pallas kernels for 53%

profile of v5, /device:TPU:0, one launch (start us, length us, event | category | flops | bytes accessed | tf_op | source)
XLA Modules:
  0.0 147.6 jit_solution(8379838805109105088)
XLA Ops:
  0.0 3.8 %pack.3 = (s32[16]{0:T(128)S(1)}, s32[1]{0:T(128)}, f32[2,8,128]{2,1,0:T(8,128)S(1)}, bf16[2,640,128]{2,1,0:T(8,128)(2,1)S(1)}, bf16[2,640,128]{2,1,0:T(8,128)(2...) custom-call(s32[2,4]{1,0:T(2,128)} %bitcast.10, ...), custom_call_target="tpu_custom_call" | custom-call | bytes 4194304 | tf_op jit(solution)/shard_map/pack/pallas_call | solution.py:108
  3.8 18.4 %attend.6.after_ref.a_ref = bf16[128,1024]{1,0:T(8,128)(2,1)S(1)} custom-call(bf16[2,640,128]{2,1,0:T(8,128)(2,1)S(1)} %get-tuple-element.64.refs_0_, bf16[2,4096,128]{2,1,0:T(8,128)(2,1)S(1)} %get-tuple-element.62.refs_1_.keys_ref, bf16[2,144,4096]{2,1,0:T(8,128)(2,1)S(1)} %get-tuple-element.63.refs_2_.values_ref), custom_call_target="tpu_custom_call" | custom-call | flops 4294967296 | bytes 4194304 | tf_op jit(solution)/shard_map/attend/pallas_call | solution.py:268
  22.2 1.8 %project.29 = (bf16[128,2048]{1,0:T(8,128)(2,1)S(1)}, f32[128,2048]{1,0:T(8,128)S(1)}) custom-call(bf16[128,1024]{1,0:T(8,128)(2,1)S(1)} %attend.6.after_ref.a_ref, bf16[1024,8192]{1,0:T(8,128)(2,1)S(1)} %copy-done), custom_call_target="tpu_custom_call" | custom-call | flops 1073741824 | bytes 8388608 | tf_op jit(solution)/shard_map/project/pallas_call | solution.py:301
  26.0 3.0 %collective-permute-start.14 = (bf16[2,640,128]{2,1,0:T(8,128)(2,1)S(1)}, bf16[2,640,128]{2,1,0:T(8,128)(2,1)S(1)}, u32[]{:S(2)}, u32[]{:S(2)}) collective-permute-start(bf16[2,640,128]{2,1,0:T(8,128)(2,1)S(1)} %get-tuple-element.69), channel_id=1, source_target_pairs={{0,4},{4,8},{8,12},{12,0},{1,5},{5,9},{9,13},{13,1},{2,6},{6,10},{... | collective-permute-start | bytes 983048 | tf_op jit(solution)/shard_map/ppermute | solution.py:415
  29.0 2.1 %split.1 = (bf16[2,4096,128]{2,1,0:T(8,128)(2,1)S(1)}, bf16[2,144,4096]{2,1,0:T(8,128)(2,1)S(1)}) custom-call(bf16[16384,128]{1,0:T(8,128)(2,1)} %bitcast.6, bf16[2,4096,128]{2,1,0:T(8,128)(2,1)S(1)} %get-tuple-element.62.refs_1_.keys_ref, ...), custom_call_target="tpu_custom_call", output_to_operand_aliasing={{0}: (1, {}), {1}: (2, {})} | custom-call | bytes 4194304 | tf_op jit(solution)/shard_map/split/pallas_call | solution.py:179
  31.1 18.6 %attend.9.a_ref = bf16[128,1024]{1,0:T(8,128)(2,1)S(1)} custom-call(bf16[2,640,128]{2,1,0:T(8,128)(2,1)S(1)} %get-tuple-element.72.refs_0_, bf16[2,4096,128]{2,1,0:T(8,128)(2,1)S(1)} %get-tuple-element.65.refs_2_.refs_1_, bf16[2,144,4096]{2,1,0:T(8,128)(2,1)S(1)} %get-tuple-element.66.refs_3_.refs_2_), custom_call_target="tpu_custom_call" | custom-call | flops 4294967296 | bytes 4194304 | tf_op jit(solution)/shard_map/attend/pallas_call | solution.py:268
  49.7 1.8 %project.26 = (bf16[128,2048]{1,0:T(8,128)(2,1)S(1)}, f32[128,2048]{1,0:T(8,128)S(1)}) custom-call(bf16[128,1024]{1,0:T(8,128)(2,1)S(1)} %attend.9.a_ref, bf16[1024,8192]{1,0:T(8,128)(2,1)S(1)} %copy-done), custom_call_target="tpu_custom_call" | custom-call | flops 1073741824 | bytes 8388608 | tf_op jit(solution)/shard_map/project/pallas_call | solution.py:301
  53.5 2.0 %collective-permute-start.9 = (bf16[2,640,128]{2,1,0:T(8,128)(2,1)S(1)}, bf16[2,640,128]{2,1,0:T(8,128)(2,1)S(1)}, u32[]{:S(2)}, u32[]{:S(2)}) collective-permute-start(bf16[2,640,128]{2,1,0:T(8,128)(2,1)S(1)} %get-tuple-element.61), channel_id=1, source_target_pairs={{0,12},{4,0},{8,4},{12,8},{1,13},{5,1},{9,5},{13,9},{2,14},{6,2},{... | collective-permute-start | bytes 983048 | tf_op jit(solution)/shard_map/ppermute | solution.py:415
  55.5 18.5 %attend.8 = bf16[128,1024]{1,0:T(8,128)(2,1)S(1)} custom-call(f32[2,8,128]{2,1,0:T(8,128)S(1)} %get-tuple-element.60.refs_0_, bf16[2,640,128]{2,1,0:T(8,128)(2,1)S(1)} %collective-permute-done.14.refs_1_, bf16[2,4096,128]{2,1,0:T(8,128)(2,1)S(1)} %get-tuple-element.65.refs_2_.refs_1_, bf16[2,144,4096]{2,1,0:T(8,128)(2,1)S(1)} %get-tuple-element.66.refs_3_.refs_2_), custom_call_target="tpu_custom_call" | custom-call | flops 4294967296 | bytes 4194304 | tf_op jit(solution)/shard_map/attend/pallas_call | solution.py:268
  74.0 2.1 %collective-permute-start.15 = (bf16[128,1024]{1,0:T(8,128)(2,1)S(1)}, bf16[128,1024]{1,0:T(8,128)(2,1)S(1)}, u32[]{:S(2)}, u32[]{:S(2)}) collective-permute-start(bf16[128,1024]{1,0:T(8,128)(2,1)S(1)} %attend.8), channel_id=1, source_target_pairs={{0,12},{4,0},{8,4},{12,8},{1,13},{5,1},{9,5},{13,9},{2,14},{6,2},{... | collective-permute-start | bytes 786440 | tf_op jit(solution)/shard_map/ppermute | solution.py:421
  76.1 18.5 %attend.7 = bf16[128,1024]{1,0:T(8,128)(2,1)S(1)} custom-call(f32[2,8,128]{2,1,0:T(8,128)S(1)} %get-tuple-element.60.refs_0_, bf16[2,640,128]{2,1,0:T(8,128)(2,1)S(1)} %collective-permute-done.9.refs_1_, bf16[2,4096,128]{2,1,0:T(8,128)(2,1)S(1)} %get-tuple-element.65.refs_2_.refs_1_, bf16[2,144,4096]{2,1,0:T(8,128)(2,1)S(1)} %get-tuple-element.66.refs_3_.refs_2_), custom_call_target="tpu_custom_call" | custom-call | flops 4294967296 | bytes 4194304 | tf_op jit(solution)/shard_map/attend/pallas_call | solution.py:268
  95.0 1.8 %collective-permute-start.24 = (bf16[128,2048]{1,0:T(8,128)(2,1)S(1)}, bf16[128,2048]{1,0:T(8,128)(2,1)S(1)}, u32[]{:S(2)}, u32[]{:S(2)}) collective-permute-start(bf16[128,2048]{1,0:T(8,128)(2,1)S(1)} %add_convert_fusion.1), channel_id=1, source_target_pairs={{0,2},{1,3},{2,0},{3,1},{4,6},{5,7},{6,4},{7,5},{8,10},{9,11},{10,... | collective-permute-start | bytes 1572872 | tf_op jit(solution)/shard_map/ppermute | solution.py:375
  96.8 1.8 %project.23 = (bf16[128,2048]{1,0:T(8,128)(2,1)S(1)}, f32[128,2048]{1,0:T(8,128)S(1)}) custom-call(bf16[128,1024]{1,0:T(8,128)(2,1)S(1)} %collective-permute-done.15.a_ref, bf16[1024,8192]{1,0:T(8,128)(2,1)S(1)} %copy-done), custom_call_target="tpu_custom_call" | custom-call | flops 1073741824 | bytes 8388608 | tf_op jit(solution)/shard_map/project/pallas_call | solution.py:301
  98.9 5.5 %collective-permute-done.10.a_ref = bf16[128,1024]{1,0:T(8,128)(2,1)S(1)} collective-permute-done((bf16[128,1024]{1,0:T(8,128)(2,1)S(1)}, bf16[128,1024]{1,0:T(8,128)(2,1)S(1)}, u32[]{:S(2)}, u32[]{:S(2)}) %collective-permute-start.10) | collective-permute-done | bytes 262176 | tf_op jit(solution)/shard_map/ppermute | solution.py:421
  104.4 1.9 %project.20 = (bf16[128,2048]{1,0:T(8,128)(2,1)S(1)}, f32[128,2048]{1,0:T(8,128)S(1)}) custom-call(bf16[128,1024]{1,0:T(8,128)(2,1)S(1)} %collective-permute-done.10.a_ref, bf16[1024,8192]{1,0:T(8,128)(2,1)S(1)} %copy-done), custom_call_target="tpu_custom_call" | custom-call | flops 1073741824 | bytes 8388608 | tf_op jit(solution)/shard_map/project/pallas_call | solution.py:301
  108.9 1.6 %collective-permute-start.21 = (bf16[128,2048]{1,0:T(8,128)(2,1)S(1)}, bf16[128,2048]{1,0:T(8,128)(2,1)S(1)}, u32[]{:S(2)}, u32[]{:S(2)}) collective-permute-start(bf16[128,2048]{1,0:T(8,128)(2,1)S(1)} %add_convert_fusion.2), channel_id=1, source_target_pairs={{0,2},{1,3},{2,0},{3,1},{4,6},{5,7},{6,4},{7,5},{8,10},{9,11},{10,... | collective-permute-start | bytes 1572872 | tf_op jit(solution)/shard_map/ppermute | solution.py:375
  111.7 1.6 %collective-permute-start.13 = (bf16[128,2048]{1,0:T(8,128)(2,1)S(1)}, bf16[128,2048]{1,0:T(8,128)(2,1)S(1)}, u32[]{:S(2)}, u32[]{:S(2)}) collective-permute-start(bf16[128,2048]{1,0:T(8,128)(2,1)S(1)} %add_convert_fusion.4), channel_id=1, source_target_pairs={{0,2},{1,3},{2,0},{3,1},{4,6},{5,7},{6,4},{7,5},{8,10},{9,11},{10,... | collective-permute-start | bytes 1572872 | tf_op jit(solution)/shard_map/ppermute | solution.py:375
  119.1 1.6 %finish.6.refs_0_ = bf16[512,2048]{1,0:T(8,128)(2,1)} custom-call(s32[16]{0:T(128)S(1)} %get-tuple-element.59.table_ref, f32[128,2048]{1,0:T(8,128)S(1)} %project.27.kept_ref, bf16[128,2048]{1,0:T(8,128)(2,1)S(1)} %collective-permute-done.22.core_ref, bf16[128,2048]{1,0:T(8,128)(2,1)S(1)} %collective-permute-done.24.far_ref), custom_call_target="tpu_custom_call" | custom-call | bytes 2621440 | tf_op jit(solution)/shard_map/finish/pallas_call | solution.py:345
  120.7 3.1 %collective-permute-done.21.far_ref = bf16[128,2048]{1,0:T(8,128)(2,1)S(1)} collective-permute-done((bf16[128,2048]{1,0:T(8,128)(2,1)S(1)}, bf16[128,2048]{1,0:T(8,128)(2,1)S(1)}, u32[]{:S(2)}, u32[]{:S(2)}) %collective-permute-start.21) | collective-permute-done | bytes 524320 | tf_op jit(solution)/shard_map/ppermute | solution.py:375
  123.8 1.6 %finish.7.refs_0_ = bf16[512,2048]{1,0:T(8,128)(2,1)} custom-call(s32[16]{0:T(128)S(1)} %get-tuple-element.59.table_ref, f32[128,2048]{1,0:T(8,128)S(1)} %project.24.kept_ref, bf16[128,2048]{1,0:T(8,128)(2,1)S(1)} %collective-permute-done.19.core_ref, bf16[128,2048]{1,0:T(8,128)(2,1)S(1)} %collective-permute-done.21.far_ref, ...), custom_call_target="tpu_custom_call", output_to_operand_aliasing={{}: (4, {})} | custom-call | bytes 2621440 | tf_op jit(solution)/shard_map/finish/pallas_call | solution.py:345
  125.4 9.6 %collective-permute-done.18.far_ref = bf16[128,2048]{1,0:T(8,128)(2,1)S(1)} collective-permute-done((bf16[128,2048]{1,0:T(8,128)(2,1)S(1)}, bf16[128,2048]{1,0:T(8,128)(2,1)S(1)}, u32[]{:S(2)}, u32[]{:S(2)}) %collective-permute-start.18) | collective-permute-done | bytes 524320 | tf_op jit(solution)/shard_map/ppermute | solution.py:375
  135.0 1.6 %finish.8.refs_0_ = bf16[512,2048]{1,0:T(8,128)(2,1)} custom-call(s32[16]{0:T(128)S(1)} %get-tuple-element.59.table_ref, f32[128,2048]{1,0:T(8,128)S(1)} %project.21.kept_ref, bf16[128,2048]{1,0:T(8,128)(2,1)S(1)} %collective-permute-done.16.core_ref, bf16[128,2048]{1,0:T(8,128)(2,1)S(1)} %collective-permute-done.18.far_ref, ...), custom_call_target="tpu_custom_call", output_to_operand_aliasing={{}: (4, {})} | custom-call | bytes 2621440 | tf_op jit(solution)/shard_map/finish/pallas_call | solution.py:345
  136.6 9.1 %collective-permute-done.13.far_ref = bf16[128,2048]{1,0:T(8,128)(2,1)S(1)} collective-permute-done((bf16[128,2048]{1,0:T(8,128)(2,1)S(1)}, bf16[128,2048]{1,0:T(8,128)(2,1)S(1)}, u32[]{:S(2)}, u32[]{:S(2)}) %collective-permute-start.13) | collective-permute-done | bytes 524320 | tf_op jit(solution)/shard_map/ppermute | solution.py:375
  145.8 1.6 %finish.9 = bf16[512,2048]{1,0:T(8,128)(2,1)} custom-call(s32[16]{0:T(128)S(1)} %get-tuple-element.59.table_ref, f32[128,2048]{1,0:T(8,128)S(1)} %project.18.kept_ref, bf16[128,2048]{1,0:T(8,128)(2,1)S(1)} %collective-permute-done.11.core_ref, bf16[128,2048]{1,0:T(8,128)(2,1)S(1)} %collective-permute-done.13.far_ref, ...), custom_call_target="tpu_custom_call", output_to_operand_aliasing={{}: (4, {})} | custom-call | bytes 2621440 | tf_op jit(solution)/shard_map/finish/pallas_call | solution.py:345
  (37 shorter events, 13.4 us)
Async XLA Ops:
  0.0 22.2 %copy-start = (bf16[1024,8192]{1,0:T(8,128)(2,1)S(1)}, bf16[1024,8192]{1,0:T(8,128)(2,1)}, u32[]{:S(2)}) copy-start(bf16[1024,8192]{1,0:T(8,128)(2,1)} %w_ref.23) | copy-start | bytes 50331652
  24.1 70.5 %collective-permute-start.23 = (bf16[128,2048]{1,0:T(8,128)(2,1)S(1)}, bf16[128,2048]{1,0:T(8,128)(2,1)S(1)}, u32[]{:S(2)}, u32[]{:S(2)}) collective-permute-start(bf16[128,2048]{1,0:T(8,128)(2,1)S(1)} %get-tuple-element.76), channel_id=1, source_target_pairs={{0,1},{1,0},{2,3},{3,2},{4,5},{5,4},{6,7},{7,6},{8,9},{9,8},{10,11... | collective-permute-start | bytes 1572872 | tf_op jit(solution)/shard_map/ppermute | solution.py:371
  25.9 85.2 %collective-permute-start.22 = (bf16[128,2048]{1,0:T(8,128)(2,1)S(1)}, bf16[128,2048]{1,0:T(8,128)(2,1)S(1)}, u32[]{:S(2)}, u32[]{:S(2)}) collective-permute-start(bf16[128,2048]{1,0:T(8,128)(2,1)S(1)} %project.28), channel_id=1, source_target_pairs={{0,1},{1,0},{2,3},{3,2},{4,5},{5,4},{6,7},{7,6},{8,9},{9,8},{10,11... | collective-permute-start | bytes 1572872 | tf_op jit(solution)/shard_map/ppermute | solution.py:373
  26.0 27.5 %collective-permute-start.14 = (bf16[2,640,128]{2,1,0:T(8,128)(2,1)S(1)}, bf16[2,640,128]{2,1,0:T(8,128)(2,1)S(1)}, u32[]{:S(2)}, u32[]{:S(2)}) collective-permute-start(bf16[2,640,128]{2,1,0:T(8,128)(2,1)S(1)} %get-tuple-element.69), channel_id=1, source_target_pairs={{0,4},{4,8},{8,12},{12,0},{1,5},{5,9},{9,13},{13,1},{2,6},{6,10},{... | collective-permute-start | bytes 983048 | tf_op jit(solution)/shard_map/ppermute | solution.py:415
  51.6 47.1 %collective-permute-start.20 = (bf16[128,2048]{1,0:T(8,128)(2,1)S(1)}, bf16[128,2048]{1,0:T(8,128)(2,1)S(1)}, u32[]{:S(2)}, u32[]{:S(2)}) collective-permute-start(bf16[128,2048]{1,0:T(8,128)(2,1)S(1)} %get-tuple-element.74), channel_id=1, source_target_pairs={{0,1},{1,0},{2,3},{3,2},{4,5},{5,4},{6,7},{7,6},{8,9},{9,8},{10,11... | collective-permute-start | bytes 1572872 | tf_op jit(solution)/shard_map/ppermute | solution.py:371
  52.9 58.7 %collective-permute-start.19 = (bf16[128,2048]{1,0:T(8,128)(2,1)S(1)}, bf16[128,2048]{1,0:T(8,128)(2,1)S(1)}, u32[]{:S(2)}, u32[]{:S(2)}) collective-permute-start(bf16[128,2048]{1,0:T(8,128)(2,1)S(1)} %project.25), channel_id=1, source_target_pairs={{0,1},{1,0},{2,3},{3,2},{4,5},{5,4},{6,7},{7,6},{8,9},{9,8},{10,11... | collective-permute-start | bytes 1572872 | tf_op jit(solution)/shard_map/ppermute | solution.py:373
  53.5 20.5 %collective-permute-start.9 = (bf16[2,640,128]{2,1,0:T(8,128)(2,1)S(1)}, bf16[2,640,128]{2,1,0:T(8,128)(2,1)S(1)}, u32[]{:S(2)}, u32[]{:S(2)}) collective-permute-start(bf16[2,640,128]{2,1,0:T(8,128)(2,1)S(1)} %get-tuple-element.61), channel_id=1, source_target_pairs={{0,12},{4,0},{8,4},{12,8},{1,13},{5,1},{9,5},{13,9},{2,14},{6,2},{... | collective-permute-start | bytes 983048 | tf_op jit(solution)/shard_map/ppermute | solution.py:415
  74.0 21.0 %collective-permute-start.15 = (bf16[128,1024]{1,0:T(8,128)(2,1)S(1)}, bf16[128,1024]{1,0:T(8,128)(2,1)S(1)}, u32[]{:S(2)}, u32[]{:S(2)}) collective-permute-start(bf16[128,1024]{1,0:T(8,128)(2,1)S(1)} %attend.8), channel_id=1, source_target_pairs={{0,12},{4,0},{8,4},{12,8},{1,13},{5,1},{9,5},{13,9},{2,14},{6,2},{... | collective-permute-start | bytes 786440 | tf_op jit(solution)/shard_map/ppermute | solution.py:421
  94.6 9.8 %collective-permute-start.10 = (bf16[128,1024]{1,0:T(8,128)(2,1)S(1)}, bf16[128,1024]{1,0:T(8,128)(2,1)S(1)}, u32[]{:S(2)}, u32[]{:S(2)}) collective-permute-start(bf16[128,1024]{1,0:T(8,128)(2,1)S(1)} %attend.7), channel_id=1, source_target_pairs={{0,4},{4,8},{8,12},{12,0},{1,5},{5,9},{9,13},{13,1},{2,6},{6,10},{... | collective-permute-start | bytes 786440 | tf_op jit(solution)/shard_map/ppermute | solution.py:421
  95.0 16.7 %collective-permute-start.24 = (bf16[128,2048]{1,0:T(8,128)(2,1)S(1)}, bf16[128,2048]{1,0:T(8,128)(2,1)S(1)}, u32[]{:S(2)}, u32[]{:S(2)}) collective-permute-start(bf16[128,2048]{1,0:T(8,128)(2,1)S(1)} %add_convert_fusion.1), channel_id=1, source_target_pairs={{0,2},{1,3},{2,0},{3,1},{4,6},{5,7},{6,4},{7,5},{8,10},{9,11},{10,... | collective-permute-start | bytes 1572872 | tf_op jit(solution)/shard_map/ppermute | solution.py:375
  98.7 10.3 %collective-permute-start.17 = (bf16[128,2048]{1,0:T(8,128)(2,1)S(1)}, bf16[128,2048]{1,0:T(8,128)(2,1)S(1)}, u32[]{:S(2)}, u32[]{:S(2)}) collective-permute-start(bf16[128,2048]{1,0:T(8,128)(2,1)S(1)} %get-tuple-element.71), channel_id=1, source_target_pairs={{0,1},{1,0},{2,3},{3,2},{4,5},{5,4},{6,7},{7,6},{8,9},{9,8},{10,11... | collective-permute-start | bytes 1572872 | tf_op jit(solution)/shard_map/ppermute | solution.py:371
  106.2 4.4 %collective-permute-start.12 = (bf16[128,2048]{1,0:T(8,128)(2,1)S(1)}, bf16[128,2048]{1,0:T(8,128)(2,1)S(1)}, u32[]{:S(2)}, u32[]{:S(2)}) collective-permute-start(bf16[128,2048]{1,0:T(8,128)(2,1)S(1)} %get-tuple-element.68), channel_id=1, source_target_pairs={{0,1},{1,0},{2,3},{3,2},{4,5},{5,4},{6,7},{7,6},{8,9},{9,8},{10,11... | collective-permute-start | bytes 1572872 | tf_op jit(solution)/shard_map/ppermute | solution.py:371
  108.9 14.9 %collective-permute-start.21 = (bf16[128,2048]{1,0:T(8,128)(2,1)S(1)}, bf16[128,2048]{1,0:T(8,128)(2,1)S(1)}, u32[]{:S(2)}, u32[]{:S(2)}) collective-permute-start(bf16[128,2048]{1,0:T(8,128)(2,1)S(1)} %add_convert_fusion.2), channel_id=1, source_target_pairs={{0,2},{1,3},{2,0},{3,1},{4,6},{5,7},{6,4},{7,5},{8,10},{9,11},{10,... | collective-permute-start | bytes 1572872 | tf_op jit(solution)/shard_map/ppermute | solution.py:375
  110.7 14.7 %collective-permute-start.16 = (bf16[128,2048]{1,0:T(8,128)(2,1)S(1)}, bf16[128,2048]{1,0:T(8,128)(2,1)S(1)}, u32[]{:S(2)}, u32[]{:S(2)}) collective-permute-start(bf16[128,2048]{1,0:T(8,128)(2,1)S(1)} %project.22), channel_id=1, source_target_pairs={{0,1},{1,0},{2,3},{3,2},{4,5},{5,4},{6,7},{7,6},{8,9},{9,8},{10,11... | collective-permute-start | bytes 1572872 | tf_op jit(solution)/shard_map/ppermute | solution.py:373
  111.1 23.9 %collective-permute-start.18 = (bf16[128,2048]{1,0:T(8,128)(2,1)S(1)}, bf16[128,2048]{1,0:T(8,128)(2,1)S(1)}, u32[]{:S(2)}, u32[]{:S(2)}) collective-permute-start(bf16[128,2048]{1,0:T(8,128)(2,1)S(1)} %add_convert_fusion.3), channel_id=1, source_target_pairs={{0,2},{1,3},{2,0},{3,1},{4,6},{5,7},{6,4},{7,5},{8,10},{9,11},{10,... | collective-permute-start | bytes 1572872 | tf_op jit(solution)/shard_map/ppermute | solution.py:375
  111.7 25.0 %collective-permute-start.11 = (bf16[128,2048]{1,0:T(8,128)(2,1)S(1)}, bf16[128,2048]{1,0:T(8,128)(2,1)S(1)}, u32[]{:S(2)}, u32[]{:S(2)}) collective-permute-start(bf16[128,2048]{1,0:T(8,128)(2,1)S(1)} %project.19), channel_id=1, source_target_pairs={{0,1},{1,0},{2,3},{3,2},{4,5},{5,4},{6,7},{7,6},{8,9},{9,8},{10,11... | collective-permute-start | bytes 1572872 | tf_op jit(solution)/shard_map/ppermute | solution.py:373
  111.7 34.1 %collective-permute-start.13 = (bf16[128,2048]{1,0:T(8,128)(2,1)S(1)}, bf16[128,2048]{1,0:T(8,128)(2,1)S(1)}, u32[]{:S(2)}, u32[]{:S(2)}) collective-permute-start(bf16[128,2048]{1,0:T(8,128)(2,1)S(1)} %add_convert_fusion.4), channel_id=1, source_target_pairs={{0,2},{1,3},{2,0},{3,1},{4,6},{5,7},{6,4},{7,5},{8,10},{9,11},{10,... | collective-permute-start | bytes 1572872 | tf_op jit(solution)/shard_map/ppermute | solution.py:375

commit v6 on v5

--- a/solution.py
+++ b/solution.py
@@ -313,24 +313,17 @@
     )(rows, weight)
 
 
-def finish_kernel(table_ref, kept_ref, core_ref, far_ref, *refs, first, qlength, tile):
+def finish_kernel(table_ref, kept_ref, core_ref, far_ref, *refs, first, qlength):
     o_ref, block_ref, sems = refs[-3:]
     number, _, columns = block_ref.shape
-    places = [jnp.maximum(table_ref[first + i], 0) for i in range(number)]
-    counts = [table_ref[table_ref.shape[0] // 2 + first + i] for i in range(number)]
-    t = lax.broadcasted_iota(jnp.int32, (qlength, tile), 0)
-
-    def one(j, carry):
-        out = pl.ds(pl.multiple_of(j * tile, tile), tile)
-        total = kept_ref[:, out] + core_ref[:, out].astype(F32) + far_ref[:, out].astype(F32)
-        for i in range(number):
-            block = total[i * qlength : (i + 1) * qlength, :]
-            block_ref[i, :, out] = jnp.where(t < counts[i], block, 0.0).astype(BF16)
-        return carry
-
-    lax.fori_loop(0, columns // tile, one, 0)
+    t = lax.broadcasted_iota(jnp.int32, (qlength, columns), 0)
     copies = []
-    for i, place in enumerate(places):
+    for i in range(number):
+        place = jnp.maximum(table_ref[first + i], 0)
+        count = table_ref[table_ref.shape[0] // 2 + first + i]
+        rows = slice(i * qlength, (i + 1) * qlength)
+        total = kept_ref[rows, :] + core_ref[rows, :].astype(F32) + far_ref[rows, :].astype(F32)
+        block_ref[i] = jnp.where(t < count, total, 0.0).astype(BF16)
         target = o_ref.at[pl.ds(pl.multiple_of(place * qlength, qlength), qlength), :]
         copies.append(pltpu.make_async_copy(block_ref.at[i], target, sems.at[i]))
         copies[-1].start()
@@ -338,12 +331,12 @@
         copy.wait()
 
 
-def finish(table, kept, from_core, from_far, first, previous, rows, qlength, tile):
+def finish(table, kept, from_core, from_far, first, previous, rows, qlength):
     number, columns = kept.shape[0] // qlength, kept.shape[1]
     extra = [] if previous is None else [pltpu.with_memory_space_constraint(previous, pltpu.HBM)]
     hbm = pl.BlockSpec(memory_space=pltpu.HBM)
     return pl.pallas_call(
-        functools.partial(finish_kernel, first=first, qlength=qlength, tile=tile),
+        functools.partial(finish_kernel, first=first, qlength=qlength),
         in_specs=[SMEM, VMEM, VMEM, VMEM] + [hbm] * len(extra),
         out_specs=hbm,
         out_shape=pltpu.HBM((rows, columns), BF16),
@@ -374,7 +367,7 @@
     chip_sum = (far_keep + far_core.astype(F32)).astype(BF16)
     far = lax.ppermute(chip_sum, "tensor", other_chip)
     (near_keep,) = project(results, weight, shares, tile, (0,), (F32,))
-    return finish(table, near_keep, near_core, far, first, out, rows, qlength, tile)
+    return finish(table, near_keep, near_core, far, first, out, rows, qlength)
 
 
 def answer_by_first_slots(queries, own, pairs, context, stored, ids, counts, heads, qlength):

time: 148 us -> 148 us (level)
  no operation moved by 1% of the time
where the time goes in v6:
time: 148 us; the launch traced here: 147 us
  Pallas kernels  103 us (70%)
  waiting for transfers between devices  27.8 us (19%)
  starting transfers between devices  14.6 us (10%)
    pallas_call x4, Pallas kernels, attend(): pl.pallas_call(functools.partial(attend_kernel, entry=entry, heads=heads,...  73.9 us
    ppermute x4, waiting for transfers between devices, project_out(): far = lax.ppermute(chip_sum, 'tensor', other_chip)  22.3 us
    pallas_call x12, Pallas kernels, project(): pl.pallas_call(functools.partial(project_kernel, flips=flips, tile=tile),...  17.7 us
    pallas_call x4, Pallas kernels, finish(): pl.pallas_call(functools.partial(finish_kernel, first=first, qlength=qlen...  5.86 us
    ppermute x2, waiting for transfers between devices, on_device(): lax.ppermute(returned[s], 'replica', by_shift(-shifts[s], replicas))  5.5 us
    ppermute x4, starting transfers between devices, project_out(): far = lax.ppermute(chip_sum, 'tensor', other_chip)  5.5 us
    ppermute x2, starting transfers between devices, on_device(): arrived[s] = lax.ppermute(packed[s], 'replica', by_shift(shift, replicas))  5.04 us
    pallas_call x1, Pallas kernels, pack(): pl.pallas_call(functools.partial(pack_kernel, route=route, heads=heads, q...  3.79 us
  transfers between devices with their start and end apart: 16, of which 4 were waited for; matrix products, arithmetic and copies ran while one was open for 0% of the time, Pallas kernels for 53%

profile of v6, /device:TPU:0, one launch (start us, length us, event | category | flops | bytes accessed | tf_op | source)
XLA Modules:
  0.0 147.4 jit_solution(17333206221726540576)
XLA Ops:
  0.0 3.8 %pack.3 = (s32[16]{0:T(128)S(1)}, s32[1]{0:T(128)}, f32[2,8,128]{2,1,0:T(8,128)S(1)}, bf16[2,640,128]{2,1,0:T(8,128)(2,1)S(1)}, bf16[2,640,128]{2,1,0:T(8,128)(2...) custom-call(s32[2,4]{1,0:T(2,128)} %bitcast.10, ...), custom_call_target="tpu_custom_call" | custom-call | bytes 4194304 | tf_op jit(solution)/shard_map/pack/pallas_call | solution.py:108
  3.8 18.4 %attend.6.after_ref.a_ref = bf16[128,1024]{1,0:T(8,128)(2,1)S(1)} custom-call(bf16[2,640,128]{2,1,0:T(8,128)(2,1)S(1)} %get-tuple-element.64.refs_0_, bf16[2,4096,128]{2,1,0:T(8,128)(2,1)S(1)} %get-tuple-element.62.refs_1_.keys_ref, bf16[2,144,4096]{2,1,0:T(8,128)(2,1)S(1)} %get-tuple-element.63.refs_2_.values_ref), custom_call_target="tpu_custom_call" | custom-call | flops 4294967296 | bytes 4194304 | tf_op jit(solution)/shard_map/attend/pallas_call | solution.py:268
  22.2 1.8 %project.29 = (bf16[128,2048]{1,0:T(8,128)(2,1)S(1)}, f32[128,2048]{1,0:T(8,128)S(1)}) custom-call(bf16[128,1024]{1,0:T(8,128)(2,1)S(1)} %attend.6.after_ref.a_ref, bf16[1024,8192]{1,0:T(8,128)(2,1)S(1)} %copy-done), custom_call_target="tpu_custom_call" | custom-call | flops 1073741824 | bytes 8388608 | tf_op jit(solution)/shard_map/project/pallas_call | solution.py:301
  26.0 3.0 %collective-permute-start.14 = (bf16[2,640,128]{2,1,0:T(8,128)(2,1)S(1)}, bf16[2,640,128]{2,1,0:T(8,128)(2,1)S(1)}, u32[]{:S(2)}, u32[]{:S(2)}) collective-permute-start(bf16[2,640,128]{2,1,0:T(8,128)(2,1)S(1)} %get-tuple-element.69), channel_id=1, source_target_pairs={{0,4},{4,8},{8,12},{12,0},{1,5},{5,9},{9,13},{13,1},{2,6},{6,10},{... | collective-permute-start | bytes 983048 | tf_op jit(solution)/shard_map/ppermute | solution.py:408
  29.0 2.1 %split.1 = (bf16[2,4096,128]{2,1,0:T(8,128)(2,1)S(1)}, bf16[2,144,4096]{2,1,0:T(8,128)(2,1)S(1)}) custom-call(bf16[16384,128]{1,0:T(8,128)(2,1)} %bitcast.6, bf16[2,4096,128]{2,1,0:T(8,128)(2,1)S(1)} %get-tuple-element.62.refs_1_.keys_ref, ...), custom_call_target="tpu_custom_call", output_to_operand_aliasing={{0}: (1, {}), {1}: (2, {})} | custom-call | bytes 4194304 | tf_op jit(solution)/shard_map/split/pallas_call | solution.py:179
  31.1 18.6 %attend.9.a_ref = bf16[128,1024]{1,0:T(8,128)(2,1)S(1)} custom-call(bf16[2,640,128]{2,1,0:T(8,128)(2,1)S(1)} %get-tuple-element.72.refs_0_, bf16[2,4096,128]{2,1,0:T(8,128)(2,1)S(1)} %get-tuple-element.65.refs_2_.refs_1_, bf16[2,144,4096]{2,1,0:T(8,128)(2,1)S(1)} %get-tuple-element.66.refs_3_.refs_2_), custom_call_target="tpu_custom_call" | custom-call | flops 4294967296 | bytes 4194304 | tf_op jit(solution)/shard_map/attend/pallas_call | solution.py:268
  49.7 1.8 %project.26 = (bf16[128,2048]{1,0:T(8,128)(2,1)S(1)}, f32[128,2048]{1,0:T(8,128)S(1)}) custom-call(bf16[128,1024]{1,0:T(8,128)(2,1)S(1)} %attend.9.a_ref, bf16[1024,8192]{1,0:T(8,128)(2,1)S(1)} %copy-done), custom_call_target="tpu_custom_call" | custom-call | flops 1073741824 | bytes 8388608 | tf_op jit(solution)/shard_map/project/pallas_call | solution.py:301
  53.5 2.0 %collective-permute-start.9 = (bf16[2,640,128]{2,1,0:T(8,128)(2,1)S(1)}, bf16[2,640,128]{2,1,0:T(8,128)(2,1)S(1)}, u32[]{:S(2)}, u32[]{:S(2)}) collective-permute-start(bf16[2,640,128]{2,1,0:T(8,128)(2,1)S(1)} %get-tuple-element.61), channel_id=1, source_target_pairs={{0,12},{4,0},{8,4},{12,8},{1,13},{5,1},{9,5},{13,9},{2,14},{6,2},{... | collective-permute-start | bytes 983048 | tf_op jit(solution)/shard_map/ppermute | solution.py:408
  55.5 18.5 %attend.8 = bf16[128,1024]{1,0:T(8,128)(2,1)S(1)} custom-call(f32[2,8,128]{2,1,0:T(8,128)S(1)} %get-tuple-element.60.refs_0_, bf16[2,640,128]{2,1,0:T(8,128)(2,1)S(1)} %collective-permute-done.14.refs_1_, bf16[2,4096,128]{2,1,0:T(8,128)(2,1)S(1)} %get-tuple-element.65.refs_2_.refs_1_, bf16[2,144,4096]{2,1,0:T(8,128)(2,1)S(1)} %get-tuple-element.66.refs_3_.refs_2_), custom_call_target="tpu_custom_call" | custom-call | flops 4294967296 | bytes 4194304 | tf_op jit(solution)/shard_map/attend/pallas_call | solution.py:268
  74.0 2.1 %collective-permute-start.15 = (bf16[128,1024]{1,0:T(8,128)(2,1)S(1)}, bf16[128,1024]{1,0:T(8,128)(2,1)S(1)}, u32[]{:S(2)}, u32[]{:S(2)}) collective-permute-start(bf16[128,1024]{1,0:T(8,128)(2,1)S(1)} %attend.8), channel_id=1, source_target_pairs={{0,12},{4,0},{8,4},{12,8},{1,13},{5,1},{9,5},{13,9},{2,14},{6,2},{... | collective-permute-start | bytes 786440 | tf_op jit(solution)/shard_map/ppermute | solution.py:414
  76.1 18.5 %attend.7 = bf16[128,1024]{1,0:T(8,128)(2,1)S(1)} custom-call(f32[2,8,128]{2,1,0:T(8,128)S(1)} %get-tuple-element.60.refs_0_, bf16[2,640,128]{2,1,0:T(8,128)(2,1)S(1)} %collective-permute-done.9.refs_1_, bf16[2,4096,128]{2,1,0:T(8,128)(2,1)S(1)} %get-tuple-element.65.refs_2_.refs_1_, bf16[2,144,4096]{2,1,0:T(8,128)(2,1)S(1)} %get-tuple-element.66.refs_3_.refs_2_), custom_call_target="tpu_custom_call" | custom-call | flops 4294967296 | bytes 4194304 | tf_op jit(solution)/shard_map/attend/pallas_call | solution.py:268
  95.0 1.8 %collective-permute-start.24 = (bf16[128,2048]{1,0:T(8,128)(2,1)S(1)}, bf16[128,2048]{1,0:T(8,128)(2,1)S(1)}, u32[]{:S(2)}, u32[]{:S(2)}) collective-permute-start(bf16[128,2048]{1,0:T(8,128)(2,1)S(1)} %add_convert_fusion.1), channel_id=1, source_target_pairs={{0,2},{1,3},{2,0},{3,1},{4,6},{5,7},{6,4},{7,5},{8,10},{9,11},{10,... | collective-permute-start | bytes 1572872 | tf_op jit(solution)/shard_map/ppermute | solution.py:368
  96.8 1.8 %project.23 = (bf16[128,2048]{1,0:T(8,128)(2,1)S(1)}, f32[128,2048]{1,0:T(8,128)S(1)}) custom-call(bf16[128,1024]{1,0:T(8,128)(2,1)S(1)} %collective-permute-done.15.a_ref, bf16[1024,8192]{1,0:T(8,128)(2,1)S(1)} %copy-done), custom_call_target="tpu_custom_call" | custom-call | flops 1073741824 | bytes 8388608 | tf_op jit(solution)/shard_map/project/pallas_call | solution.py:301
  98.9 5.5 %collective-permute-done.10.a_ref = bf16[128,1024]{1,0:T(8,128)(2,1)S(1)} collective-permute-done((bf16[128,1024]{1,0:T(8,128)(2,1)S(1)}, bf16[128,1024]{1,0:T(8,128)(2,1)S(1)}, u32[]{:S(2)}, u32[]{:S(2)}) %collective-permute-start.10) | collective-permute-done | bytes 262176 | tf_op jit(solution)/shard_map/ppermute | solution.py:414
  104.4 1.9 %project.20 = (bf16[128,2048]{1,0:T(8,128)(2,1)S(1)}, f32[128,2048]{1,0:T(8,128)S(1)}) custom-call(bf16[128,1024]{1,0:T(8,128)(2,1)S(1)} %collective-permute-done.10.a_ref, bf16[1024,8192]{1,0:T(8,128)(2,1)S(1)} %copy-done), custom_call_target="tpu_custom_call" | custom-call | flops 1073741824 | bytes 8388608 | tf_op jit(solution)/shard_map/project/pallas_call | solution.py:301
  108.9 1.6 %collective-permute-start.21 = (bf16[128,2048]{1,0:T(8,128)(2,1)S(1)}, bf16[128,2048]{1,0:T(8,128)(2,1)S(1)}, u32[]{:S(2)}, u32[]{:S(2)}) collective-permute-start(bf16[128,2048]{1,0:T(8,128)(2,1)S(1)} %add_convert_fusion.2), channel_id=1, source_target_pairs={{0,2},{1,3},{2,0},{3,1},{4,6},{5,7},{6,4},{7,5},{8,10},{9,11},{10,... | collective-permute-start | bytes 1572872 | tf_op jit(solution)/shard_map/ppermute | solution.py:368
  111.7 1.6 %collective-permute-start.13 = (bf16[128,2048]{1,0:T(8,128)(2,1)S(1)}, bf16[128,2048]{1,0:T(8,128)(2,1)S(1)}, u32[]{:S(2)}, u32[]{:S(2)}) collective-permute-start(bf16[128,2048]{1,0:T(8,128)(2,1)S(1)} %add_convert_fusion.4), channel_id=1, source_target_pairs={{0,2},{1,3},{2,0},{3,1},{4,6},{5,7},{6,4},{7,5},{8,10},{9,11},{10,... | collective-permute-start | bytes 1572872 | tf_op jit(solution)/shard_map/ppermute | solution.py:368
  119.1 1.5 %finish.6.refs_0_ = bf16[512,2048]{1,0:T(8,128)(2,1)} custom-call(s32[16]{0:T(128)S(1)} %get-tuple-element.59.table_ref, f32[128,2048]{1,0:T(8,128)S(1)} %project.27.kept_ref, bf16[128,2048]{1,0:T(8,128)(2,1)S(1)} %collective-permute-done.22.core_ref, bf16[128,2048]{1,0:T(8,128)(2,1)S(1)} %collective-permute-done.24.far_ref), custom_call_target="tpu_custom_call" | custom-call | bytes 2621440 | tf_op jit(solution)/shard_map/finish/pallas_call | solution.py:338
  120.6 3.2 %collective-permute-done.21.far_ref = bf16[128,2048]{1,0:T(8,128)(2,1)S(1)} collective-permute-done((bf16[128,2048]{1,0:T(8,128)(2,1)S(1)}, bf16[128,2048]{1,0:T(8,128)(2,1)S(1)}, u32[]{:S(2)}, u32[]{:S(2)}) %collective-permute-start.21) | collective-permute-done | bytes 524320 | tf_op jit(solution)/shard_map/ppermute | solution.py:368
  123.8 1.5 finish.7.refs_0_
  125.3 9.8 %collective-permute-done.18.far_ref = bf16[128,2048]{1,0:T(8,128)(2,1)S(1)} collective-permute-done((bf16[128,2048]{1,0:T(8,128)(2,1)S(1)}, bf16[128,2048]{1,0:T(8,128)(2,1)S(1)}, u32[]{:S(2)}, u32[]{:S(2)}) %collective-permute-start.18) | collective-permute-done | bytes 524320 | tf_op jit(solution)/shard_map/ppermute | solution.py:368
  135.0 1.5 finish.8.refs_0_
  136.5 9.3 %collective-permute-done.13.far_ref = bf16[128,2048]{1,0:T(8,128)(2,1)S(1)} collective-permute-done((bf16[128,2048]{1,0:T(8,128)(2,1)S(1)}, bf16[128,2048]{1,0:T(8,128)(2,1)S(1)}, u32[]{:S(2)}, u32[]{:S(2)}) %collective-permute-start.13) | collective-permute-done | bytes 524320 | tf_op jit(solution)/shard_map/ppermute | solution.py:368
  145.8 1.5 finish.9
  (37 shorter events, 13.4 us)
Async XLA Ops:
  0.0 22.2 %copy-start = (bf16[1024,8192]{1,0:T(8,128)(2,1)S(1)}, bf16[1024,8192]{1,0:T(8,128)(2,1)}, u32[]{:S(2)}) copy-start(bf16[1024,8192]{1,0:T(8,128)(2,1)} %w_ref.23) | copy-start | bytes 50331652
  24.1 70.5 %collective-permute-start.23 = (bf16[128,2048]{1,0:T(8,128)(2,1)S(1)}, bf16[128,2048]{1,0:T(8,128)(2,1)S(1)}, u32[]{:S(2)}, u32[]{:S(2)}) collective-permute-start(bf16[128,2048]{1,0:T(8,128)(2,1)S(1)} %get-tuple-element.76), channel_id=1, source_target_pairs={{0,1},{1,0},{2,3},{3,2},{4,5},{5,4},{6,7},{7,6},{8,9},{9,8},{10,11... | collective-permute-start | bytes 1572872 | tf_op jit(solution)/shard_map/ppermute | solution.py:364
  25.9 85.2 %collective-permute-start.22 = (bf16[128,2048]{1,0:T(8,128)(2,1)S(1)}, bf16[128,2048]{1,0:T(8,128)(2,1)S(1)}, u32[]{:S(2)}, u32[]{:S(2)}) collective-permute-start(bf16[128,2048]{1,0:T(8,128)(2,1)S(1)} %project.28), channel_id=1, source_target_pairs={{0,1},{1,0},{2,3},{3,2},{4,5},{5,4},{6,7},{7,6},{8,9},{9,8},{10,11... | collective-permute-start | bytes 1572872 | tf_op jit(solution)/shard_map/ppermute | solution.py:366
  26.0 27.5 %collective-permute-start.14 = (bf16[2,640,128]{2,1,0:T(8,128)(2,1)S(1)}, bf16[2,640,128]{2,1,0:T(8,128)(2,1)S(1)}, u32[]{:S(2)}, u32[]{:S(2)}) collective-permute-start(bf16[2,640,128]{2,1,0:T(8,128)(2,1)S(1)} %get-tuple-element.69), channel_id=1, source_target_pairs={{0,4},{4,8},{8,12},{12,0},{1,5},{5,9},{9,13},{13,1},{2,6},{6,10},{... | collective-permute-start | bytes 983048 | tf_op jit(solution)/shard_map/ppermute | solution.py:408
  51.6 47.1 %collective-permute-start.20 = (bf16[128,2048]{1,0:T(8,128)(2,1)S(1)}, bf16[128,2048]{1,0:T(8,128)(2,1)S(1)}, u32[]{:S(2)}, u32[]{:S(2)}) collective-permute-start(bf16[128,2048]{1,0:T(8,128)(2,1)S(1)} %get-tuple-element.74), channel_id=1, source_target_pairs={{0,1},{1,0},{2,3},{3,2},{4,5},{5,4},{6,7},{7,6},{8,9},{9,8},{10,11... | collective-permute-start | bytes 1572872 | tf_op jit(solution)/shard_map/ppermute | solution.py:364
  52.9 58.7 %collective-permute-start.19 = (bf16[128,2048]{1,0:T(8,128)(2,1)S(1)}, bf16[128,2048]{1,0:T(8,128)(2,1)S(1)}, u32[]{:S(2)}, u32[]{:S(2)}) collective-permute-start(bf16[128,2048]{1,0:T(8,128)(2,1)S(1)} %project.25), channel_id=1, source_target_pairs={{0,1},{1,0},{2,3},{3,2},{4,5},{5,4},{6,7},{7,6},{8,9},{9,8},{10,11... | collective-permute-start | bytes 1572872 | tf_op jit(solution)/shard_map/ppermute | solution.py:366
  53.5 20.5 %collective-permute-start.9 = (bf16[2,640,128]{2,1,0:T(8,128)(2,1)S(1)}, bf16[2,640,128]{2,1,0:T(8,128)(2,1)S(1)}, u32[]{:S(2)}, u32[]{:S(2)}) collective-permute-start(bf16[2,640,128]{2,1,0:T(8,128)(2,1)S(1)} %get-tuple-element.61), channel_id=1, source_target_pairs={{0,12},{4,0},{8,4},{12,8},{1,13},{5,1},{9,5},{13,9},{2,14},{6,2},{... | collective-permute-start | bytes 983048 | tf_op jit(solution)/shard_map/ppermute | solution.py:408
  74.0 21.0 %collective-permute-start.15 = (bf16[128,1024]{1,0:T(8,128)(2,1)S(1)}, bf16[128,1024]{1,0:T(8,128)(2,1)S(1)}, u32[]{:S(2)}, u32[]{:S(2)}) collective-permute-start(bf16[128,1024]{1,0:T(8,128)(2,1)S(1)} %attend.8), channel_id=1, source_target_pairs={{0,12},{4,0},{8,4},{12,8},{1,13},{5,1},{9,5},{13,9},{2,14},{6,2},{... | collective-permute-start | bytes 786440 | tf_op jit(solution)/shard_map/ppermute | solution.py:414
  94.6 9.8 %collective-permute-start.10 = (bf16[128,1024]{1,0:T(8,128)(2,1)S(1)}, bf16[128,1024]{1,0:T(8,128)(2,1)S(1)}, u32[]{:S(2)}, u32[]{:S(2)}) collective-permute-start(bf16[128,1024]{1,0:T(8,128)(2,1)S(1)} %attend.7), channel_id=1, source_target_pairs={{0,4},{4,8},{8,12},{12,0},{1,5},{5,9},{9,13},{13,1},{2,6},{6,10},{... | collective-permute-start | bytes 786440 | tf_op jit(solution)/shard_map/ppermute | solution.py:414
  95.0 16.7 %collective-permute-start.24 = (bf16[128,2048]{1,0:T(8,128)(2,1)S(1)}, bf16[128,2048]{1,0:T(8,128)(2,1)S(1)}, u32[]{:S(2)}, u32[]{:S(2)}) collective-permute-start(bf16[128,2048]{1,0:T(8,128)(2,1)S(1)} %add_convert_fusion.1), channel_id=1, source_target_pairs={{0,2},{1,3},{2,0},{3,1},{4,6},{5,7},{6,4},{7,5},{8,10},{9,11},{10,... | collective-permute-start | bytes 1572872 | tf_op jit(solution)/shard_map/ppermute | solution.py:368
  98.7 10.3 %collective-permute-start.17 = (bf16[128,2048]{1,0:T(8,128)(2,1)S(1)}, bf16[128,2048]{1,0:T(8,128)(2,1)S(1)}, u32[]{:S(2)}, u32[]{:S(2)}) collective-permute-start(bf16[128,2048]{1,0:T(8,128)(2,1)S(1)} %get-tuple-element.71), channel_id=1, source_target_pairs={{0,1},{1,0},{2,3},{3,2},{4,5},{5,4},{6,7},{7,6},{8,9},{9,8},{10,11... | collective-permute-start | bytes 1572872 | tf_op jit(solution)/shard_map/ppermute | solution.py:364
  106.2 4.4 %collective-permute-start.12 = (bf16[128,2048]{1,0:T(8,128)(2,1)S(1)}, bf16[128,2048]{1,0:T(8,128)(2,1)S(1)}, u32[]{:S(2)}, u32[]{:S(2)}) collective-permute-start(bf16[128,2048]{1,0:T(8,128)(2,1)S(1)} %get-tuple-element.68), channel_id=1, source_target_pairs={{0,1},{1,0},{2,3},{3,2},{4,5},{5,4},{6,7},{7,6},{8,9},{9,8},{10,11... | collective-permute-start | bytes 1572872 | tf_op jit(solution)/shard_map/ppermute | solution.py:364
  108.9 14.9 %collective-permute-start.21 = (bf16[128,2048]{1,0:T(8,128)(2,1)S(1)}, bf16[128,2048]{1,0:T(8,128)(2,1)S(1)}, u32[]{:S(2)}, u32[]{:S(2)}) collective-permute-start(bf16[128,2048]{1,0:T(8,128)(2,1)S(1)} %add_convert_fusion.2), channel_id=1, source_target_pairs={{0,2},{1,3},{2,0},{3,1},{4,6},{5,7},{6,4},{7,5},{8,10},{9,11},{10,... | collective-permute-start | bytes 1572872 | tf_op jit(solution)/shard_map/ppermute | solution.py:368
  110.7 14.6 %collective-permute-start.16 = (bf16[128,2048]{1,0:T(8,128)(2,1)S(1)}, bf16[128,2048]{1,0:T(8,128)(2,1)S(1)}, u32[]{:S(2)}, u32[]{:S(2)}) collective-permute-start(bf16[128,2048]{1,0:T(8,128)(2,1)S(1)} %project.22), channel_id=1, source_target_pairs={{0,1},{1,0},{2,3},{3,2},{4,5},{5,4},{6,7},{7,6},{8,9},{9,8},{10,11... | collective-permute-start | bytes 1572872 | tf_op jit(solution)/shard_map/ppermute | solution.py:366
  111.1 23.9 %collective-permute-start.18 = (bf16[128,2048]{1,0:T(8,128)(2,1)S(1)}, bf16[128,2048]{1,0:T(8,128)(2,1)S(1)}, u32[]{:S(2)}, u32[]{:S(2)}) collective-permute-start(bf16[128,2048]{1,0:T(8,128)(2,1)S(1)} %add_convert_fusion.3), channel_id=1, source_target_pairs={{0,2},{1,3},{2,0},{3,1},{4,6},{5,7},{6,4},{7,5},{8,10},{9,11},{10,... | collective-permute-start | bytes 1572872 | tf_op jit(solution)/shard_map/ppermute | solution.py:368
  111.7 24.9 %collective-permute-start.11 = (bf16[128,2048]{1,0:T(8,128)(2,1)S(1)}, bf16[128,2048]{1,0:T(8,128)(2,1)S(1)}, u32[]{:S(2)}, u32[]{:S(2)}) collective-permute-start(bf16[128,2048]{1,0:T(8,128)(2,1)S(1)} %project.19), channel_id=1, source_target_pairs={{0,1},{1,0},{2,3},{3,2},{4,5},{5,4},{6,7},{7,6},{8,9},{9,8},{10,11... | collective-permute-start | bytes 1572872 | tf_op jit(solution)/shard_map/ppermute | solution.py:366
  111.7 34.1 %collective-permute-start.13 = (bf16[128,2048]{1,0:T(8,128)(2,1)S(1)}, bf16[128,2048]{1,0:T(8,128)(2,1)S(1)}, u32[]{:S(2)}, u32[]{:S(2)}) collective-permute-start(bf16[128,2048]{1,0:T(8,128)(2,1)S(1)} %add_convert_fusion.4), channel_id=1, source_target_pairs={{0,2},{1,3},{2,0},{3,1},{4,6},{5,7},{6,4},{7,5},{8,10},{9,11},{10,... | collective-permute-start | bytes 1572872 | tf_op jit(solution)/shard_map/ppermute | solution.py:368

commit v7 on v6

--- a/solution.py
+++ b/solution.py
@@ -356,11 +356,15 @@
     return groups <= 2 and replicas == 4 and shares == 4
 
 
-def project_out(table, results, weight, shares, first, out, rows, qlength):
+def project_out(label, table, results, weight, shares, first, out, rows, qlength):
     other_core = [(i, i ^ 1) for i in range(shares)]
     other_chip = [(i, i ^ 2) for i in range(shares)]
     tile = 512
-    far_give, far_keep = project(results, weight, shares, tile, (3, 2), (BF16, F32))
+    if label in (2, 3):
+        (far_give,) = project(results, weight, shares, tile, (3,), (BF16,))
+        (far_keep,) = project(results, weight, shares, tile, (2,), (F32,))
+    else:
+        far_give, far_keep = project(results, weight, shares, tile, (3, 2), (BF16, F32))
     far_core = lax.ppermute(far_give, "tensor", other_core)
     (near_give,) = project(results, weight, shares, tile, (1,), (BF16,))
     near_core = lax.ppermute(near_give, "tensor", other_core)
@@ -414,11 +418,15 @@
                 returned[s] = lax.ppermute(returned[s], "replica", by_shift(-shifts[s], replicas))
         out = None
         for s in range(4):
-            out = project_out(table, returned[s], out_weight, shares, s * CAP, out, rows, qlength)
+            out = project_out(
+                s, table, returned[s], out_weight, shares, s * CAP, out, rows, qlength
+            )
 
         def again():
             table, results = answer_by_first_slots(queries, own, pairs, context, stored, ids, token_counts, heads, qlength)
-            return project_out(table, results, out_weight, shares, 0, None, rows, qlength)
+            return project_out(
+                "again", table, results, out_weight, shares, 0, None, rows, qlength
+            )
 
         return lax.cond(failed[0] > 0, again, lambda: out)
 

time: 148 us -> 150 us (1.014)
  Pallas kernels: 103 us -> 105 us
    pallas_call x12 -> x14, Pallas kernels: 17.7 us -> 19.1 us  [project(): pl.pallas_call(functools.partial(project_kernel, flips=flips, tile=tile),...]
where the time goes in v7:
time: 150 us; the launch traced here: 149 us
  Pallas kernels  105 us (70%)
  waiting for transfers between devices  28.4 us (19%)
  starting transfers between devices  14.7 us (10%)
    pallas_call x4, Pallas kernels, attend(): pl.pallas_call(functools.partial(attend_kernel, entry=entry, heads=heads,...  73.9 us
    ppermute x4, waiting for transfers between devices, project_out(): far = lax.ppermute(chip_sum, 'tensor', other_chip)  22.3 us
    pallas_call x14, Pallas kernels, project(): pl.pallas_call(functools.partial(project_kernel, flips=flips, tile=tile),...  19.1 us
    ppermute x2, waiting for transfers between devices, on_device(): lax.ppermute(returned[s], 'replica', by_shift(-shifts[s], replicas))  6.09 us
    pallas_call x4, Pallas kernels, finish(): pl.pallas_call(functools.partial(finish_kernel, first=first, qlength=qlen...  5.85 us
    ppermute x4, starting transfers between devices, project_out(): far = lax.ppermute(chip_sum, 'tensor', other_chip)  5.5 us
    ppermute x2, starting transfers between devices, on_device(): arrived[s] = lax.ppermute(packed[s], 'replica', by_shift(shift, replicas))  5.09 us
    pallas_call x1, Pallas kernels, pack(): pl.pallas_call(functools.partial(pack_kernel, route=route, heads=heads, q...  3.79 us
  transfers between devices with their start and end apart: 16, of which 4 were waited for; matrix products, arithmetic and copies ran while one was open for 0% of the time, Pallas kernels for 53%

profile of v7, /device:TPU:0, one launch (start us, length us, event | category | flops | bytes accessed | tf_op | source)
XLA Modules:
  0.0 149.4 jit_solution(18350665970040566342)
XLA Ops:
  0.0 3.8 %pack.3 = (s32[16]{0:T(128)S(1)}, s32[1]{0:T(128)}, f32[2,8,128]{2,1,0:T(8,128)S(1)}, bf16[2,640,128]{2,1,0:T(8,128)(2,1)S(1)}, bf16[2,640,128]{2,1,0:T(8,128)(2...) custom-call(s32[2,4]{1,0:T(2,128)} %bitcast.10, ...), custom_call_target="tpu_custom_call" | custom-call | bytes 4194304 | tf_op jit(solution)/shard_map/pack/pallas_call | solution.py:108
  3.8 18.4 %attend.6.after_ref.a_ref = bf16[128,1024]{1,0:T(8,128)(2,1)S(1)} custom-call(bf16[2,640,128]{2,1,0:T(8,128)(2,1)S(1)} %get-tuple-element.60.refs_0_, bf16[2,4096,128]{2,1,0:T(8,128)(2,1)S(1)} %get-tuple-element.58.refs_1_.keys_ref, bf16[2,144,4096]{2,1,0:T(8,128)(2,1)S(1)} %get-tuple-element.59.refs_2_.values_ref), custom_call_target="tpu_custom_call" | custom-call | flops 4294967296 | bytes 4194304 | tf_op jit(solution)/shard_map/attend/pallas_call | solution.py:268
  22.2 1.8 %project.33 = (bf16[128,2048]{1,0:T(8,128)(2,1)S(1)}, f32[128,2048]{1,0:T(8,128)S(1)}) custom-call(bf16[128,1024]{1,0:T(8,128)(2,1)S(1)} %attend.6.after_ref.a_ref, bf16[1024,8192]{1,0:T(8,128)(2,1)S(1)} %copy-done), custom_call_target="tpu_custom_call" | custom-call | flops 1073741824 | bytes 8388608 | tf_op jit(solution)/shard_map/project/pallas_call | solution.py:301
  26.0 3.0 %collective-permute-start.14 = (bf16[2,640,128]{2,1,0:T(8,128)(2,1)S(1)}, bf16[2,640,128]{2,1,0:T(8,128)(2,1)S(1)}, u32[]{:S(2)}, u32[]{:S(2)}) collective-permute-start(bf16[2,640,128]{2,1,0:T(8,128)(2,1)S(1)} %get-tuple-element.63), channel_id=1, source_target_pairs={{0,4},{4,8},{8,12},{12,0},{1,5},{5,9},{9,13},{13,1},{2,6},{6,10},{... | collective-permute-start | bytes 983048 | tf_op jit(solution)/shard_map/ppermute | solution.py:412
  29.0 2.1 %split.1 = (bf16[2,4096,128]{2,1,0:T(8,128)(2,1)S(1)}, bf16[2,144,4096]{2,1,0:T(8,128)(2,1)S(1)}) custom-call(bf16[16384,128]{1,0:T(8,128)(2,1)} %bitcast.6, bf16[2,4096,128]{2,1,0:T(8,128)(2,1)S(1)} %get-tuple-element.58.refs_1_.keys_ref, ...), custom_call_target="tpu_custom_call", output_to_operand_aliasing={{0}: (1, {}), {1}: (2, {})} | custom-call | bytes 4194304 | tf_op jit(solution)/shard_map/split/pallas_call | solution.py:179
  31.1 18.5 %attend.9.a_ref = bf16[128,1024]{1,0:T(8,128)(2,1)S(1)} custom-call(bf16[2,640,128]{2,1,0:T(8,128)(2,1)S(1)} %get-tuple-element.64.refs_0_, bf16[2,4096,128]{2,1,0:T(8,128)(2,1)S(1)} %get-tuple-element.61.refs_2_.refs_1_, bf16[2,144,4096]{2,1,0:T(8,128)(2,1)S(1)} %get-tuple-element.62.refs_3_.refs_2_), custom_call_target="tpu_custom_call" | custom-call | flops 4294967296 | bytes 4194304 | tf_op jit(solution)/shard_map/attend/pallas_call | solution.py:268
  49.7 1.8 %project.30 = (bf16[128,2048]{1,0:T(8,128)(2,1)S(1)}, f32[128,2048]{1,0:T(8,128)S(1)}) custom-call(bf16[128,1024]{1,0:T(8,128)(2,1)S(1)} %attend.9.a_ref, bf16[1024,8192]{1,0:T(8,128)(2,1)S(1)} %copy-done), custom_call_target="tpu_custom_call" | custom-call | flops 1073741824 | bytes 8388608 | tf_op jit(solution)/shard_map/project/pallas_call | solution.py:301
  51.6 1.3 project.29
  53.5 2.1 %collective-permute-start.9 = (bf16[2,640,128]{2,1,0:T(8,128)(2,1)S(1)}, bf16[2,640,128]{2,1,0:T(8,128)(2,1)S(1)}, u32[]{:S(2)}, u32[]{:S(2)}) collective-permute-start(bf16[2,640,128]{2,1,0:T(8,128)(2,1)S(1)} %get-tuple-element.57), channel_id=1, source_target_pairs={{0,12},{4,0},{8,4},{12,8},{1,13},{5,1},{9,5},{13,9},{2,14},{6,2},{... | collective-permute-start | bytes 983048 | tf_op jit(solution)/shard_map/ppermute | solution.py:412
  55.5 18.5 %attend.8 = bf16[128,1024]{1,0:T(8,128)(2,1)S(1)} custom-call(f32[2,8,128]{2,1,0:T(8,128)S(1)} %get-tuple-element.56.refs_0_, bf16[2,640,128]{2,1,0:T(8,128)(2,1)S(1)} %collective-permute-done.14.refs_1_, bf16[2,4096,128]{2,1,0:T(8,128)(2,1)S(1)} %get-tuple-element.61.refs_2_.refs_1_, bf16[2,144,4096]{2,1,0:T(8,128)(2,1)S(1)} %get-tuple-element.62.refs_3_.refs_2_), custom_call_target="tpu_custom_call" | custom-call | flops 4294967296 | bytes 4194304 | tf_op jit(solution)/shard_map/attend/pallas_call | solution.py:268
  74.0 2.1 %collective-permute-start.15 = (bf16[128,1024]{1,0:T(8,128)(2,1)S(1)}, bf16[128,1024]{1,0:T(8,128)(2,1)S(1)}, u32[]{:S(2)}, u32[]{:S(2)}) collective-permute-start(bf16[128,1024]{1,0:T(8,128)(2,1)S(1)} %attend.8), channel_id=1, source_target_pairs={{0,12},{4,0},{8,4},{12,8},{1,13},{5,1},{9,5},{13,9},{2,14},{6,2},{... | collective-permute-start | bytes 786440 | tf_op jit(solution)/shard_map/ppermute | solution.py:418
  76.1 18.5 %attend.7 = bf16[128,1024]{1,0:T(8,128)(2,1)S(1)} custom-call(f32[2,8,128]{2,1,0:T(8,128)S(1)} %get-tuple-element.56.refs_0_, bf16[2,640,128]{2,1,0:T(8,128)(2,1)S(1)} %collective-permute-done.9.refs_1_, bf16[2,4096,128]{2,1,0:T(8,128)(2,1)S(1)} %get-tuple-element.61.refs_2_.refs_1_, bf16[2,144,4096]{2,1,0:T(8,128)(2,1)S(1)} %get-tuple-element.62.refs_3_.refs_2_), custom_call_target="tpu_custom_call" | custom-call | flops 4294967296 | bytes 4194304 | tf_op jit(solution)/shard_map/attend/pallas_call | solution.py:268
  95.0 1.8 %collective-permute-start.24 = (bf16[128,2048]{1,0:T(8,128)(2,1)S(1)}, bf16[128,2048]{1,0:T(8,128)(2,1)S(1)}, u32[]{:S(2)}, u32[]{:S(2)}) collective-permute-start(bf16[128,2048]{1,0:T(8,128)(2,1)S(1)} %add_convert_fusion.1), channel_id=1, source_target_pairs={{0,2},{1,3},{2,0},{3,1},{4,6},{5,7},{6,4},{7,5},{8,10},{9,11},{10,... | collective-permute-start | bytes 1572872 | tf_op jit(solution)/shard_map/ppermute | solution.py:372
  98.3 6.1 %collective-permute-done.10.a_ref = bf16[128,1024]{1,0:T(8,128)(2,1)S(1)} collective-permute-done((bf16[128,1024]{1,0:T(8,128)(2,1)S(1)}, bf16[128,1024]{1,0:T(8,128)(2,1)S(1)}, u32[]{:S(2)}, u32[]{:S(2)}) %collective-permute-start.10) | collective-permute-done | bytes 262176 | tf_op jit(solution)/shard_map/ppermute | solution.py:418
  107.0 1.3 project.25
  110.9 1.6 %collective-permute-start.21 = (bf16[128,2048]{1,0:T(8,128)(2,1)S(1)}, bf16[128,2048]{1,0:T(8,128)(2,1)S(1)}, u32[]{:S(2)}, u32[]{:S(2)}) collective-permute-start(bf16[128,2048]{1,0:T(8,128)(2,1)S(1)} %add_convert_fusion.2), channel_id=1, source_target_pairs={{0,2},{1,3},{2,0},{3,1},{4,6},{5,7},{6,4},{7,5},{8,10},{9,11},{10,... | collective-permute-start | bytes 1572872 | tf_op jit(solution)/shard_map/ppermute | solution.py:372
  113.6 1.6 %collective-permute-start.13 = (bf16[128,2048]{1,0:T(8,128)(2,1)S(1)}, bf16[128,2048]{1,0:T(8,128)(2,1)S(1)}, u32[]{:S(2)}, u32[]{:S(2)}) collective-permute-start(bf16[128,2048]{1,0:T(8,128)(2,1)S(1)} %add_convert_fusion.4), channel_id=1, source_target_pairs={{0,2},{1,3},{2,0},{3,1},{4,6},{5,7},{6,4},{7,5},{8,10},{9,11},{10,... | collective-permute-start | bytes 1572872 | tf_op jit(solution)/shard_map/ppermute | solution.py:372
  121.0 1.5 finish.6.refs_0_
  122.5 3.3 %collective-permute-done.21.far_ref = bf16[128,2048]{1,0:T(8,128)(2,1)S(1)} collective-permute-done((bf16[128,2048]{1,0:T(8,128)(2,1)S(1)}, bf16[128,2048]{1,0:T(8,128)(2,1)S(1)}, u32[]{:S(2)}, u32[]{:S(2)}) %collective-permute-start.21) | collective-permute-done | bytes 524320 | tf_op jit(solution)/shard_map/ppermute | solution.py:372
  125.8 1.5 finish.7.refs_0_
  127.2 9.8 %collective-permute-done.18.far_ref = bf16[128,2048]{1,0:T(8,128)(2,1)S(1)} collective-permute-done((bf16[128,2048]{1,0:T(8,128)(2,1)S(1)}, bf16[128,2048]{1,0:T(8,128)(2,1)S(1)}, u32[]{:S(2)}, u32[]{:S(2)}) %collective-permute-start.18) | collective-permute-done | bytes 524320 | tf_op jit(solution)/shard_map/ppermute | solution.py:372
  137.0 1.5 finish.8.refs_0_
  138.5 9.3 %collective-permute-done.13.far_ref = bf16[128,2048]{1,0:T(8,128)(2,1)S(1)} collective-permute-done((bf16[128,2048]{1,0:T(8,128)(2,1)S(1)}, bf16[128,2048]{1,0:T(8,128)(2,1)S(1)}, u32[]{:S(2)}, u32[]{:S(2)}) %collective-permute-start.13) | collective-permute-done | bytes 524320 | tf_op jit(solution)/shard_map/ppermute | solution.py:372
  147.8 1.5 finish.9
  (39 shorter events, 15.9 us)
Async XLA Ops:
  0.0 22.2 %copy-start = (bf16[1024,8192]{1,0:T(8,128)(2,1)S(1)}, bf16[1024,8192]{1,0:T(8,128)(2,1)}, u32[]{:S(2)}) copy-start(bf16[1024,8192]{1,0:T(8,128)(2,1)} %w_ref.27) | copy-start | bytes 50331652
  24.1 70.5 %collective-permute-start.23 = (bf16[128,2048]{1,0:T(8,128)(2,1)S(1)}, bf16[128,2048]{1,0:T(8,128)(2,1)S(1)}, u32[]{:S(2)}, u32[]{:S(2)}) collective-permute-start(bf16[128,2048]{1,0:T(8,128)(2,1)S(1)} %get-tuple-element.68), channel_id=1, source_target_pairs={{0,1},{1,0},{2,3},{3,2},{4,5},{5,4},{6,7},{7,6},{8,9},{9,8},{10,11... | collective-permute-start | bytes 1572872 | tf_op jit(solution)/shard_map/ppermute | solution.py:368
  25.9 87.1 %collective-permute-start.22 = (bf16[128,2048]{1,0:T(8,128)(2,1)S(1)}, bf16[128,2048]{1,0:T(8,128)(2,1)S(1)}, u32[]{:S(2)}, u32[]{:S(2)}) collective-permute-start(bf16[128,2048]{1,0:T(8,128)(2,1)S(1)} %project.32), channel_id=1, source_target_pairs={{0,1},{1,0},{2,3},{3,2},{4,5},{5,4},{6,7},{7,6},{8,9},{9,8},{10,11... | collective-permute-start | bytes 1572872 | tf_op jit(solution)/shard_map/ppermute | solution.py:370
  26.0 27.5 %collective-permute-start.14 = (bf16[2,640,128]{2,1,0:T(8,128)(2,1)S(1)}, bf16[2,640,128]{2,1,0:T(8,128)(2,1)S(1)}, u32[]{:S(2)}, u32[]{:S(2)}) collective-permute-start(bf16[2,640,128]{2,1,0:T(8,128)(2,1)S(1)} %get-tuple-element.63), channel_id=1, source_target_pairs={{0,4},{4,8},{8,12},{12,0},{1,5},{5,9},{9,13},{13,1},{2,6},{6,10},{... | collective-permute-start | bytes 983048 | tf_op jit(solution)/shard_map/ppermute | solution.py:412
  51.5 46.5 %collective-permute-start.20 = (bf16[128,2048]{1,0:T(8,128)(2,1)S(1)}, bf16[128,2048]{1,0:T(8,128)(2,1)S(1)}, u32[]{:S(2)}, u32[]{:S(2)}) collective-permute-start(bf16[128,2048]{1,0:T(8,128)(2,1)S(1)} %get-tuple-element.66), channel_id=1, source_target_pairs={{0,1},{1,0},{2,3},{3,2},{4,5},{5,4},{6,7},{7,6},{8,9},{9,8},{10,11... | collective-permute-start | bytes 1572872 | tf_op jit(solution)/shard_map/ppermute | solution.py:368
  52.9 60.7 %collective-permute-start.19 = (bf16[128,2048]{1,0:T(8,128)(2,1)S(1)}, bf16[128,2048]{1,0:T(8,128)(2,1)S(1)}, u32[]{:S(2)}, u32[]{:S(2)}) collective-permute-start(bf16[128,2048]{1,0:T(8,128)(2,1)S(1)} %project.29), channel_id=1, source_target_pairs={{0,1},{1,0},{2,3},{3,2},{4,5},{5,4},{6,7},{7,6},{8,9},{9,8},{10,11... | collective-permute-start | bytes 1572872 | tf_op jit(solution)/shard_map/ppermute | solution.py:370
  53.5 20.5 %collective-permute-start.9 = (bf16[2,640,128]{2,1,0:T(8,128)(2,1)S(1)}, bf16[2,640,128]{2,1,0:T(8,128)(2,1)S(1)}, u32[]{:S(2)}, u32[]{:S(2)}) collective-permute-start(bf16[2,640,128]{2,1,0:T(8,128)(2,1)S(1)} %get-tuple-element.57), channel_id=1, source_target_pairs={{0,12},{4,0},{8,4},{12,8},{1,13},{5,1},{9,5},{13,9},{2,14},{6,2},{... | collective-permute-start | bytes 983048 | tf_op jit(solution)/shard_map/ppermute | solution.py:412
  74.0 21.0 %collective-permute-start.15 = (bf16[128,1024]{1,0:T(8,128)(2,1)S(1)}, bf16[128,1024]{1,0:T(8,128)(2,1)S(1)}, u32[]{:S(2)}, u32[]{:S(2)}) collective-permute-start(bf16[128,1024]{1,0:T(8,128)(2,1)S(1)} %attend.8), channel_id=1, source_target_pairs={{0,12},{4,0},{8,4},{12,8},{1,13},{5,1},{9,5},{13,9},{2,14},{6,2},{... | collective-permute-start | bytes 786440 | tf_op jit(solution)/shard_map/ppermute | solution.py:418
  94.6 9.8 %collective-permute-start.10 = (bf16[128,1024]{1,0:T(8,128)(2,1)S(1)}, bf16[128,1024]{1,0:T(8,128)(2,1)S(1)}, u32[]{:S(2)}, u32[]{:S(2)}) collective-permute-start(bf16[128,1024]{1,0:T(8,128)(2,1)S(1)} %attend.7), channel_id=1, source_target_pairs={{0,4},{4,8},{8,12},{12,0},{1,5},{5,9},{9,13},{13,1},{2,6},{6,10},{... | collective-permute-start | bytes 786440 | tf_op jit(solution)/shard_map/ppermute | solution.py:418
  95.0 18.6 %collective-permute-start.24 = (bf16[128,2048]{1,0:T(8,128)(2,1)S(1)}, bf16[128,2048]{1,0:T(8,128)(2,1)S(1)}, u32[]{:S(2)}, u32[]{:S(2)}) collective-permute-start(bf16[128,2048]{1,0:T(8,128)(2,1)S(1)} %add_convert_fusion.1), channel_id=1, source_target_pairs={{0,2},{1,3},{2,0},{3,1},{4,6},{5,7},{6,4},{7,5},{8,10},{9,11},{10,... | collective-permute-start | bytes 1572872 | tf_op jit(solution)/shard_map/ppermute | solution.py:372
  98.1 12.8 %collective-permute-start.17 = (bf16[128,2048]{1,0:T(8,128)(2,1)S(1)}, bf16[128,2048]{1,0:T(8,128)(2,1)S(1)}, u32[]{:S(2)}, u32[]{:S(2)}) collective-permute-start(bf16[128,2048]{1,0:T(8,128)(2,1)S(1)} %project.27), channel_id=1, source_target_pairs={{0,1},{1,0},{2,3},{3,2},{4,5},{5,4},{6,7},{7,6},{8,9},{9,8},{10,11... | collective-permute-start | bytes 1572872 | tf_op jit(solution)/shard_map/ppermute | solution.py:368
  105.7 6.9 %collective-permute-start.12 = (bf16[128,2048]{1,0:T(8,128)(2,1)S(1)}, bf16[128,2048]{1,0:T(8,128)(2,1)S(1)}, u32[]{:S(2)}, u32[]{:S(2)}) collective-permute-start(bf16[128,2048]{1,0:T(8,128)(2,1)S(1)} %project.23), channel_id=1, source_target_pairs={{0,1},{1,0},{2,3},{3,2},{4,5},{5,4},{6,7},{7,6},{8,9},{9,8},{10,11... | collective-permute-start | bytes 1572872 | tf_op jit(solution)/shard_map/ppermute | solution.py:368
  110.9 14.9 %collective-permute-start.21 = (bf16[128,2048]{1,0:T(8,128)(2,1)S(1)}, bf16[128,2048]{1,0:T(8,128)(2,1)S(1)}, u32[]{:S(2)}, u32[]{:S(2)}) collective-permute-start(bf16[128,2048]{1,0:T(8,128)(2,1)S(1)} %add_convert_fusion.2), channel_id=1, source_target_pairs={{0,2},{1,3},{2,0},{3,1},{4,6},{5,7},{6,4},{7,5},{8,10},{9,11},{10,... | collective-permute-start | bytes 1572872 | tf_op jit(solution)/shard_map/ppermute | solution.py:372
  112.6 14.6 %collective-permute-start.16 = (bf16[128,2048]{1,0:T(8,128)(2,1)S(1)}, bf16[128,2048]{1,0:T(8,128)(2,1)S(1)}, u32[]{:S(2)}, u32[]{:S(2)}) collective-permute-start(bf16[128,2048]{1,0:T(8,128)(2,1)S(1)} %project.25), channel_id=1, source_target_pairs={{0,1},{1,0},{2,3},{3,2},{4,5},{5,4},{6,7},{7,6},{8,9},{9,8},{10,11... | collective-permute-start | bytes 1572872 | tf_op jit(solution)/shard_map/ppermute | solution.py:370
  113.0 24.0 %collective-permute-start.18 = (bf16[128,2048]{1,0:T(8,128)(2,1)S(1)}, bf16[128,2048]{1,0:T(8,128)(2,1)S(1)}, u32[]{:S(2)}, u32[]{:S(2)}) collective-permute-start(bf16[128,2048]{1,0:T(8,128)(2,1)S(1)} %add_convert_fusion.3), channel_id=1, source_target_pairs={{0,2},{1,3},{2,0},{3,1},{4,6},{5,7},{6,4},{7,5},{8,10},{9,11},{10,... | collective-permute-start | bytes 1572872 | tf_op jit(solution)/shard_map/ppermute | solution.py:372
  113.6 24.9 %collective-permute-start.11 = (bf16[128,2048]{1,0:T(8,128)(2,1)S(1)}, bf16[128,2048]{1,0:T(8,128)(2,1)S(1)}, u32[]{:S(2)}, u32[]{:S(2)}) collective-permute-start(bf16[128,2048]{1,0:T(8,128)(2,1)S(1)} %project.21), channel_id=1, source_target_pairs={{0,1},{1,0},{2,3},{3,2},{4,5},{5,4},{6,7},{7,6},{8,9},{9,8},{10,11... | collective-permute-start | bytes 1572872 | tf_op jit(solution)/shard_map/ppermute | solution.py:370
  113.6 34.1 %collective-permute-start.13 = (bf16[128,2048]{1,0:T(8,128)(2,1)S(1)}, bf16[128,2048]{1,0:T(8,128)(2,1)S(1)}, u32[]{:S(2)}, u32[]{:S(2)}) collective-permute-start(bf16[128,2048]{1,0:T(8,128)(2,1)S(1)} %add_convert_fusion.4), channel_id=1, source_target_pairs={{0,2},{1,3},{2,0},{3,1},{4,6},{5,7},{6,4},{7,5},{8,10},{9,11},{10,... | collective-permute-start | bytes 1572872 | tf_op jit(solution)/shard_map/ppermute | solution.py:372
